TPU v7x, 128 devices: a whole 4x4x4 slice. The times are simulated.
128 devices in a mesh: leaf: 16 (over x, y), near: 8 (over z, core).
Axes of the slice: x: 4, y: 4, z: 4, core: 2. Of those that a mesh axis runs over, the one named last changes fastest.
Arguments:
- near_blocks: bfloat16 [512, 8, 256, 256], P(('leaf', 'near')), may hold values from -0.125 to 0.125
- near_index: int32 [512, 8], P(('leaf', 'near')), may hold values from 0 to 511, as said below
- test_vectors: bfloat16 [512, 64, 256], P(('leaf', 'near')), may hold values from -6 to 6
- samples: bfloat16 [512, 64, 256], P(('leaf', 'near')), may hold values from -6 to 6
- leaf_basis: bfloat16 [512, 64, 256], P(('leaf', 'near')), may hold values from -0.375 to 0.375
- col_weights: bfloat16 [512, 64, 64], P(('leaf', 'near')), may hold values from -0.75 to 0.75
- coupling: bfloat16 [512, 64, 2048], P(('leaf', 'near')), may hold values from -6 to 6
- adm_index: int32 [512, 32], P(('leaf', 'near')), may hold values from 0 to 511, as said below
- adm_count: int32 [512], P(('leaf', 'near')), may hold values from 2 to 32, as said below
- leaf_transfer: bfloat16 [512, 64, 64], P(('leaf', 'near')), may hold values from -0.75 to 0.75
- inner_transfer: bfloat16 [128, 3, 64, 64], P(('leaf', 'near')), may hold values from -0.75 to 0.75
- upper_transfer: bfloat16 [126, 64, 64], replicated, may hold values from -0.75 to 0.75
Outputs:
- leaf_factors: float32 [512, 64, 64], P(('leaf', 'near'))
- inner_factors: float32 [128, 3, 64, 64], P(('leaf', 'near'))
- upper_factors: float32 [128, 7, 64, 64], P(('leaf', 'near'))
Inputs may be any that keep to these rules, and one draw needn't show every extreme that they name: `near_index`: leaves are the cells of a 3-D grid in Morton order: bit b of a leaf's number is bit b // 3 of its coordinate along dimension b mod 3. Entry 0 of each row is the row's own leaf; every entry is the leaf of a cell at most one step from the row's cell along each dimension. `adm_index`: with the leaves in the grid of near_index: slot 0 is the cell three steps back along every dimension and slot 1 three steps ahead, each coordinate clipped to the grid; slot 2 is the leaf whose number is the row's own with its highest bit flipped (the cell half the grid away along that bit's dimension); every other entry is the leaf of a cell at most three steps from the row's cell along each dimension. `adm_count`: in every aligned block of 4 leaves some leaf has 32 live slots.
All inputs are finite; a program needn't handle non-finite values.
Results may differ from a plain program's by a relative error of at most 0.0019.
Values may be sent and summed in bfloat16 or wider, within the bound.
No kernel may reach another device: no remote copies, remote signals or barrier semaphores. Data moves between devices by JAX's collectives and lax.ppermute only.
A program may use at most 128 MiB of HBM per device.

v0:
```python
import jax
import jax.numpy as jnp
from jax import lax
from jax.sharding import PartitionSpec as P

PRECISE = lax.Precision.HIGHEST


def upper_factor(gram):
    return jnp.swapaxes(jnp.linalg.cholesky(gram), -1, -2)


def weigh(factors, transfer):
    return jnp.einsum("nab,nbc->nac", factors, transfer.astype(jnp.float32), precision=PRECISE)


def self_gram(weighted):
    return jnp.einsum("nab,nac->nbc", weighted, weighted, precision=PRECISE)


def merge_pairs(weighted, identity):
    gram = self_gram(weighted)
    return upper_factor(0.5 * (gram[0::2] + gram[1::2]) + identity)


def replicated_levels(
    weighted_all, first_level, total_levels, device, upper_transfer, devices, identity
):
    ancestors = []
    for level in range(first_level, total_levels + 1):
        factors = merge_pairs(weighted_all, identity)
        ancestors.append(lax.dynamic_index_in_dim(factors, device >> level, 0, keepdims=False))
        if level < total_levels:
            start = devices - (devices >> level - 1)
            weighted_all = weigh(factors, upper_transfer[start : start + (devices >> level)])
    return ancestors


def body(
    near_blocks,
    near_index,
    test_vectors,
    samples,
    leaf_basis,
    col_weights,
    coupling,
    adm_index,
    adm_count,
    leaf_transfer,
    inner_transfer,
    upper_transfer,
):
    count_local, rank_size, leaf_size = test_vectors.shape
    slot_total = adm_index.shape[1]
    weight_lines = rank_size * rank_size // leaf_size
    identity = jnp.eye(rank_size, dtype=jnp.float32)
    near_size = lax.axis_size("near")
    devices = lax.axis_size("leaf") * near_size
    total_levels = devices.bit_length() - 1
    device = lax.axis_index("leaf") * near_size + lax.axis_index("near")
    packed = jnp.concatenate(
        [test_vectors, col_weights.reshape(count_local, weight_lines, leaf_size)], axis=1
    )
    everything = lax.all_gather(packed, ("leaf", "near"), axis=0, tiled=True)
    neighbours = jnp.take(everything[:, :rank_size], near_index, axis=0)
    partner_lines = jnp.take(everything[:, rank_size:], adm_index, axis=0)
    near_part = jnp.einsum(
        "ikrq,ikpq->irp", neighbours, near_blocks, preferred_element_type=jnp.float32
    )
    far_sample = (samples.astype(jnp.float32) - near_part).astype(jnp.bfloat16)
    projected = jnp.einsum(
        "irp,isp->irs", leaf_basis, far_sample, preferred_element_type=jnp.float32
    ) * rank_size ** (-0.5)
    partner_weights = partner_lines.reshape(count_local, slot_total, rank_size, rank_size)
    slot_live = (jnp.arange(slot_total)[None, :] < adm_count[:, None])[:, :, None, None]
    partner_weights = jnp.where(slot_live, partner_weights, jnp.zeros((), jnp.bfloat16))
    blocks = coupling.reshape(count_local, rank_size, slot_total, rank_size)
    coupled = jnp.einsum(
        "irsc,isce->irse", blocks, partner_weights, preferred_element_type=jnp.float32
    )
    gram = jnp.einsum("iab,iac->ibc", projected, projected, precision=PRECISE)
    gram = (
        gram
        + jnp.einsum("irse,irsf->ief", coupled, coupled, precision=PRECISE)
        / (rank_size * slot_total)
        + identity
    )
    leaf_factors = upper_factor(gram)
    current = leaf_factors
    transfer = leaf_transfer
    inner = []
    for level in range(1, count_local.bit_length()):
        current = merge_pairs(weigh(current, transfer), identity)
        count_now = count_local >> level
        inner.append(current.reshape(1, count_now, rank_size, rank_size))
        start = count_local - (count_local >> level - 1)
        transfer = inner_transfer[0, start : start + count_now]
    inner_factors = jnp.concatenate(inner, axis=1)
    weighted = weigh(current, transfer)
    weighted_all = lax.all_gather(weighted, ("leaf", "near"), axis=0, tiled=True)
    ancestors = replicated_levels(
        weighted_all, 1, total_levels, device, upper_transfer, devices, identity
    )
    upper_factors = jnp.stack(ancestors, axis=0)[None]
    return (leaf_factors, inner_factors, upper_factors)


def solution(mesh):
    return jax.shard_map(
        body,
        mesh=mesh,
        in_specs=(
            P(("leaf", "near"), None, None, None),
            P(("leaf", "near"), None),
            P(("leaf", "near"), None, None),
            P(("leaf", "near"), None, None),
            P(("leaf", "near"), None, None),
            P(("leaf", "near"), None, None),
            P(("leaf", "near"), None, None),
            P(("leaf", "near"), None),
            P(("leaf", "near")),
            P(("leaf", "near"), None, None),
            P(("leaf", "near"), None, None, None),
            P(),
        ),
        out_specs=(
            P(("leaf", "near"), None, None),
            P(("leaf", "near"), None, None, None),
            P(("leaf", "near"), None, None, None),
        ),
        check_vma=False,
    )
```

profile of v0, /device:TPU:0, one launch (start us, length us, event | category | flops | bytes accessed | tf_op | source)
XLA Modules:
  0.0 1056.1 jit_solution(8612201137694237279)
XLA Ops:
  7.3 1.0 reshape.140
  8.2 1.6 pad_maximum_fusion
  9.9 3.3 reshape.141
  13.7 87.1 %all-gather.4.cloned.1.call-done = bf16[512,80,256]{2,1,0:T(8,128)(2,1)} async-done(((bf16[4,80,256]{2,1,0:T(8,128)(2,1)}), bf16[512,80,256]{2,1,0:T(8,128)(2,1)}) %all-gather.4.cloned.1.call-update) | async-done | bytes 20971536 | tf_op jit(solution)/shard_map/all_gather | solution.py:64
  100.8 4.5 slice.157
  105.2 2.8 gather_fusion.1
  108.0 1.9 gather.12
  109.9 4.1 copy.89
  114.0 2.7 fusion.3
  116.7 4.3 fusion.17
  121.0 14.2 %slice.156 = bf16[512,64,256]{2,1,0:T(8,128)(2,1)} slice(bf16[512,80,256]{2,1,0:T(8,128)(2,1)} %all-gather.4.cloned.1.call-done), slice={[0:512], [0:64], [0:256]} | slice | bytes 33554432 | tf_op jit(solution)/shard_map/slice | solution.py:65
  135.3 6.4 gather_fusion
  141.7 3.7 fusion.12
  145.9 23.5 %custom-call.32 = f32[4,64,64]{2,1,0:T(8,128)S(1)} custom-call(f32[4,64,64]{2,1,0:T(8,128)S(1)} %fusion.33), custom_call_target="Cholesky" | custom-call | tf_op jit(solution)/shard_map/jit(cholesky)/cholesky | solution.py:10
  169.6 0.4 fusion.34
  169.9 0.4 fusion.73
  170.5 11.9 %custom-call.33 = f32[2,64,64]{2,1,0:T(8,128)S(1)} custom-call(f32[2,64,64]{2,1,0:T(8,128)S(1)} %fusion.37), custom_call_target="Cholesky" | custom-call | tf_op jit(solution)/shard_map/jit(cholesky)/cholesky | solution.py:10
  183.3 5.8 custom-call.34
  189.2 0.6 compare_reduce_fusion.7
  189.8 1.4 fusion.47
  191.3 1.4 slice.137
  192.7 0.4 slice.140
  193.1 1.4 slice.143
  194.4 1.4 slice.146
  195.9 1.4 slice.149
  197.3 1.6 copy.169
  198.9 2.9 copy.170
  201.8 1.2 copy.171
  203.1 1.7 copy.172
  204.8 1.2 copy.173
  206.0 1.1 copy.174
  207.1 2.0 fusion.56
  209.0 48.4 %all-gather.6.cloned.1.call-done = f32[8192,64]{1,0:T(8,128)} async-done(((f32[64,64]{1,0:T(8,128)}), f32[8192,64]{1,0:T(8,128)}) %all-gather.6.cloned.1.call-update) | async-done | bytes 2097168 | tf_op jit(solution)/shard_map/all_gather | solution.py:100
  257.4 10.3 fusion.75
  267.7 1.9 copy-done.2
  269.7 0.4 multiply_add_fusion
  270.1 1.9 copy.108
  272.0 5.1 fusion.2
  277.1 376.1 %custom-call.25 = f32[64,64,64]{2,1,0:T(8,128)S(1)} custom-call(f32[64,64,64]{2,1,0:T(8,128)} %fusion.2), custom_call_target="Cholesky" | custom-call | tf_op jit(solution)/shard_map/jit(cholesky)/cholesky | solution.py:10
  653.2 0.3 select_reduce_fusion
  653.9 1.9 fusion.76
  655.8 3.6 fusion.77
  659.7 1.3 copy.112
  661.0 2.5 fusion.20
  663.5 188.4 %custom-call.26 = f32[32,64,64]{2,1,0:T(8,128)S(1)} custom-call(f32[32,64,64]{2,1,0:T(8,128)} %fusion.20), custom_call_target="Cholesky" | custom-call | tf_op jit(solution)/shard_map/jit(cholesky)/cholesky | solution.py:10
  852.4 1.0 fusion.78
  853.4 1.8 fusion.79
  855.5 0.9 fusion.27
  856.4 94.5 %custom-call.27 = f32[16,64,64]{2,1,0:T(8,128)S(1)} custom-call(f32[16,64,64]{2,1,0:T(8,128)} %fusion.27), custom_call_target="Cholesky" | custom-call | tf_op jit(solution)/shard_map/jit(cholesky)/cholesky | solution.py:10
  951.2 0.6 fusion.80
  951.8 1.0 fusion.81
  953.1 46.9 %custom-call.28 = f32[8,64,64]{2,1,0:T(8,128)S(1)} custom-call(f32[8,64,64]{2,1,0:T(8,128)S(1)} %fusion.30), custom_call_target="Cholesky" | custom-call | tf_op jit(solution)/shard_map/jit(cholesky)/cholesky | solution.py:10
  1000.3 0.4 fusion.82
  1000.7 0.6 fusion.83
  1001.5 23.5 %custom-call.35 = f32[4,64,64]{2,1,0:T(8,128)S(1)} custom-call(f32[4,64,64]{2,1,0:T(8,128)S(1)} %fusion.32), custom_call_target="Cholesky" | custom-call | tf_op jit(solution)/shard_map/jit(cholesky)/cholesky | solution.py:10
  1025.2 0.8 copy.139
  1026.3 0.4 fusion.85
  1026.8 11.7 %custom-call.36 = f32[2,64,64]{2,1,0:T(8,128)S(1)} custom-call(f32[2,64,64]{2,1,0:T(8,128)S(1)} %fusion.36), custom_call_target="Cholesky" | custom-call | tf_op jit(solution)/shard_map/jit(cholesky)/cholesky | solution.py:10
  1038.8 0.7 copy.140
  1039.5 0.8 bitcast_dynamic-update-slice_fusion.6
  1041.0 5.8 custom-call.37
  1046.8 0.6 compare_reduce_fusion.4
  1047.5 0.7 bitcast_dynamic-update-slice_fusion
  1048.2 0.8 copy.141
  (118 shorter events, 6.0 us)
Async XLA Ops:
  7.2 134.5 %copy-start = (bf16[4,64,256]{2,1,0:T(8,128)(2,1)S(1)}, bf16[4,64,256]{2,1,0:T(8,128)(2,1)}, u32[]{:S(2)}) copy-start(bf16[4,64,256]{2,1,0:T(8,128)(2,1)} %param.19) | copy-start | bytes 393220
  7.2 6.1 copy-start.17
  7.2 6.2 copy-start.16
  7.2 6.4 copy-start.22
  7.2 93.5 %all-gather.4.cloned.1.call-start = ((), (), s32[]{:S(2)}) async-start(), calls=%async_computation | async-start | bytes 21135360 | tf_op jit(solution)/shard_map/all_gather | solution.py:64
  9.9 247.6 %all-gather.6.cloned.1.call-start = ((), (), s32[]{:S(2)}) async-start(), calls=%async_computation.1 | async-start | bytes 4227072 | tf_op jit(solution)/shard_map/all_gather | solution.py:100
  135.3 6.4 copy-start.11
  141.7 27.9 %copy-start.14 = (bf16[4,64,64]{2,1,0:T(8,128)(2,1)S(1)}, bf16[4,64,64]{2,1,0:T(8,128)(2,1)}, u32[]{:S(2)}) copy-start(bf16[4,64,64]{2,1,0:T(8,128)(2,1)} %param.24) | copy-start | bytes 98308
  145.4 37.1 %copy-start.15 = (bf16[1,3,64,64]{3,2,1,0:T(8,128)(2,1)S(1)}, bf16[1,3,64,64]{3,2,1,0:T(8,128)(2,1)}, u32[]{:S(2)}) copy-start(bf16[1,3,64,64]{3,2,1,0:T(8,128)(2,1)} %param.25) | copy-start | bytes 73732
  145.4 45.8 %copy-start.3 = (bf16[126,64,64]{0,2,1:T(8,128)(2,1)S(1)}, bf16[126,64,64]{0,2,1:T(8,128)(2,1)}, u32[]{:S(2)}) copy-start(bf16[126,64,64]{0,2,1:T(8,128)(2,1)} %param.26) | copy-start | bytes 3096580
  169.6 21.7 %copy-start.18 = (pred[4]{0:T(512)(128)(4,1)}, pred[4]{0:T(512)(128)(4,1)S(1)}, u32[]{:S(2)}) copy-start(pred[4]{0:T(512)(128)(4,1)S(1)} %compare_reduce_fusion.9) | copy-start | bytes 16
  182.5 8.7 copy-start.20
  189.1 3.9 copy-start.9
  198.9 5.9 copy-start.5
  203.1 2.9 copy-start.6
  267.7 1.9 copy-start.2
  653.9 1.9 copy-start.4
  663.5 188.9 %copy-start.7 = (bf16[32,64,64]{2,1,0:T(8,128)(2,1)S(1)}, bf16[32,64,64]{2,1,0:T(8,128)(2,1)}, u32[]{:S(2)}) copy-start(bf16[32,64,64]{2,1,0:T(8,128)(2,1)} %copy.170) | copy-start | bytes 786436
  855.5 95.7 %copy-start.8 = (bf16[16,64,64]{2,1,0:T(8,128)(2,1)S(1)}, bf16[16,64,64]{2,1,0:T(8,128)(2,1)}, u32[]{:S(2)}) copy-start(bf16[16,64,64]{2,1,0:T(8,128)(2,1)} %copy.171) | copy-start | bytes 393220
  953.1 72.0 %copy-start.19 = (pred[4]{0:T(512)(128)(4,1)S(1)}, pred[4]{0:T(512)(128)(4,1)}, u32[]{:S(2)}) copy-start(pred[4]{0:T(512)(128)(4,1)} %copy-done.18) | copy-start | bytes 16
  1000.1 25.9 %copy-start.10 = (bf16[4,64,64]{2,1,0:T(8,128)(2,1)S(1)}, bf16[4,64,64]{2,1,0:T(8,128)(2,1)}, u32[]{:S(2)}) copy-start(bf16[4,64,64]{2,1,0:T(8,128)(2,1)} %copy.173) | copy-start | bytes 98308
  1000.7 38.0 %copy-start.21 = (pred[2]{0:T(512)(128)(4,1)S(1)}, pred[2]{0:T(512)(128)(4,1)}, u32[]{:S(2)}) copy-start(pred[2]{0:T(512)(128)(4,1)} %copy-done.20) | copy-start | bytes 10
  1001.3 37.5 %copy-start.13 = (f32[1,1,64,64]{2,3,1,0:T(8,128)S(1)}, f32[1,1,64,64]{2,3,1,0:T(8,128)}, u32[]{:S(2)}) copy-start(f32[1,1,64,64]{2,3,1,0:T(8,128)} %fusion.56) | copy-start | bytes 49156
  1001.3 39.0 %copy-start.12 = (bf16[2,64,64]{2,1,0:T(8,128)(2,1)S(1)}, bf16[2,64,64]{2,1,0:T(8,128)(2,1)}, u32[]{:S(2)}) copy-start(bf16[2,64,64]{2,1,0:T(8,128)(2,1)} %copy.174) | copy-start | bytes 49156
  1025.1 23.9 %copy-start.1 = (bf16[4,64,256]{2,1,0:T(8,128)(2,1)S(1)}, bf16[4,64,256]{2,1,0:T(8,128)(2,1)}, u32[]{:S(2)}) copy-start(bf16[4,64,256]{2,1,0:T(8,128)(2,1)} %param.19) | copy-start | bytes 393220
Sparse Core Ops, SparseCore 0:
  11.6 89.1 all-gather.3
  191.4 66.0 all-gather.5
where the time goes:
time: 1070 us; the launch traced here: 1060 us
  other arithmetic  806 us (75%)
  waiting for transfers between devices  136 us (13%)
  local copies, waits for them, and re-layouts  63.3 us (6%)
  matrix products  36.2 us (3%)
  between operations  15.1 us (1%)
    another operation x31, other arithmetic, upper_factor(): return jnp.swapaxes(jnp.linalg.cholesky(gram), -1, -2)  791 us
    all_gather x1, waiting for transfers between devices, body(): everything = lax.all_gather(packed, ('leaf', 'near'), axis=0, tiled=True)  87.1 us
    all_gather x1, waiting for transfers between devices, body(): lax.all_gather(weighted, ('leaf', 'near'), axis=0, tiled=True)  48.4 us
  transfers between devices with their start and end apart: 2, of which 2 were waited for; matrix products, arithmetic and copies ran while one was open for 2% of the time, Pallas kernels for 0%

commit v1 on v0

v1 whole, which is shorter than its diff:
```python
import jax
import jax.numpy as jnp
from jax import lax
from jax.experimental import pallas as pl
from jax.experimental.pallas import tpu as pltpu
from jax.sharding import PartitionSpec as P

PRECISE = lax.Precision.HIGHEST
AXES = ("leaf", "near")
HOPS = (1, 2, 6, 8, 24, 32, 96)
RANK = 64


def split_three(x):
    hi = x.astype(jnp.bfloat16)
    rest = x - hi.astype(jnp.float32)
    mid = rest.astype(jnp.bfloat16)
    return hi, mid, (rest - mid.astype(jnp.float32)).astype(jnp.bfloat16)


def dot32(a, b):
    return jnp.dot(a, b, preferred_element_type=jnp.float32)


def congruence(gram, transfer):
    across = jnp.transpose(transfer.astype(jnp.float32)).astype(jnp.bfloat16)
    hi, mid, low = split_three(gram)
    half = dot32(hi, transfer) + (dot32(mid, transfer) + dot32(low, transfer))
    hi, mid, low = split_three(half)
    return dot32(across, hi) + (dot32(across, mid) + dot32(across, low))


def unit_matrix():
    rows = lax.broadcasted_iota(jnp.int32, (RANK, RANK), 0)
    cols = lax.broadcasted_iota(jnp.int32, (RANK, RANK), 1)
    return (rows == cols).astype(jnp.float32)


def factor_panels(matrices):
    shape = (8, RANK)
    work = [list(panels) for panels in matrices]
    rows = lax.broadcasted_iota(jnp.int32, shape, 0)
    cols = lax.broadcasted_iota(jnp.int32, shape, 1)
    factors = [[None] * 8 for _ in work]
    for step in range(8):
        base = 8 * step
        for panels, factor in zip(work, factors):
            panel = panels[step]
            column = [
                jnp.broadcast_to(panel[:, base + k : base + k + 1], shape) for k in range(8)
            ]
            weights = [
                [jnp.broadcast_to(lower[:, base + k : base + k + 1], shape) for k in range(8)]
                for lower in panels[step + 1 :]
            ]
            rows_out = jnp.zeros(shape, jnp.float32)
            for j in range(8):
                here = rows == j
                pivot = jnp.broadcast_to(column[j][j : j + 1, :], shape)
                panel_row = jnp.broadcast_to(panel[j : j + 1, :], shape)
                rows_out = jnp.where(here, panel_row * lax.rsqrt(pivot), rows_out)
                inverse = 1.0 / pivot
                scale = column[j] * inverse
                for k in range(j + 1, 8):
                    entry = jnp.broadcast_to(column[k][j : j + 1, :], shape)
                    column[k] = jnp.where(here, entry * inverse, column[k] - scale * entry)
                panel = jnp.where(here, panel_row * inverse, panel - scale * panel_row)
            factor[step] = jnp.where(cols >= rows + base, rows_out, 0.0)
            for at, weight in enumerate(weights):
                lower = panels[step + 1 + at]
                for k in range(8):
                    lower = lower - weight[k] * jnp.broadcast_to(panel[k : k + 1, :], shape)
                panels[step + 1 + at] = lower
    return factors


def factor_kernel(grams, factors):
    count = grams.shape[0]
    out = factor_panels([[grams[b, 8 * p : 8 * p + 8, :] for p in range(8)] for b in range(count)])
    for b in range(count):
        for p in range(8):
            factors[b, 8 * p : 8 * p + 8, :] = out[b][p]


def factor(grams):
    return pl.pallas_call(
        factor_kernel, out_shape=jax.ShapeDtypeStruct(grams.shape, jnp.float32), name="factor"
    )(grams)


def local_kernel(leaf_grams, leaf_transfer, inner_transfer, inner_grams, sent):
    unit = unit_matrix()
    moved = [congruence(leaf_grams[i], leaf_transfer[i]) for i in range(4)]
    first = 0.5 * (moved[0] + moved[1]) + unit
    second = 0.5 * (moved[2] + moved[3]) + unit
    inner_grams[0] = first
    inner_grams[1] = second
    top = 0.5 * (congruence(first, inner_transfer[0, 0]) + congruence(second, inner_transfer[0, 1]))
    top = top + unit
    inner_grams[2] = top
    sent[...] = congruence(top, inner_transfer[0, 2])


def local_levels(leaf_grams, leaf_transfer, inner_transfer):
    return pl.pallas_call(
        local_kernel,
        out_shape=(
            jax.ShapeDtypeStruct((3, RANK, RANK), jnp.float32),
            jax.ShapeDtypeStruct((RANK, RANK), jnp.float32),
        ),
        name="local_levels",
    )(leaf_grams, leaf_transfer, inner_transfer)


def merge_kernel(at, own, other, transfer, gram, sent):
    merged = 0.5 * (own[...] + other[...]) + unit_matrix()
    gram[...] = merged
    sent[...] = congruence(merged, transfer[0])


def merge(at, own, other, upper_transfer):
    whole = pl.BlockSpec((RANK, RANK), lambda i, at: (0, 0))
    return pl.pallas_call(
        merge_kernel,
        grid_spec=pltpu.PrefetchScalarGridSpec(
            num_scalar_prefetch=1,
            grid=(1,),
            in_specs=[
                whole,
                whole,
                pl.BlockSpec((1, RANK, RANK), lambda i, at: (at[0], 0, 0)),
            ],
            out_specs=[whole, whole],
        ),
        out_shape=[jax.ShapeDtypeStruct((RANK, RANK), jnp.float32)] * 2,
        name="merge",
    )(at.reshape(1), own, other, upper_transfer)


def last_kernel(own, other, factor_out):
    merged = 0.5 * (own[...] + other[...]) + unit_matrix()
    out = factor_panels([[merged[8 * p : 8 * p + 8, :] for p in range(8)]])
    for p in range(8):
        factor_out[0, 8 * p : 8 * p + 8, :] = out[0][p]


def body(
    near_blocks,
    near_index,
    test_vectors,
    samples,
    leaf_basis,
    col_weights,
    coupling,
    adm_index,
    adm_count,
    leaf_transfer,
    inner_transfer,
    upper_transfer,
):
    count_local, rank_size, leaf_size = test_vectors.shape
    slot_total = adm_index.shape[1]
    weight_lines = rank_size * rank_size // leaf_size
    identity = jnp.eye(rank_size, dtype=jnp.float32)
    near_size = lax.axis_size("near")
    devices = lax.axis_size("leaf") * near_size
    total_levels = devices.bit_length() - 1
    device = lax.axis_index("leaf") * near_size + lax.axis_index("near")
    packed = jnp.concatenate(
        [test_vectors, col_weights.reshape(count_local, weight_lines, leaf_size)], axis=1
    )
    everything = lax.all_gather(packed, AXES, axis=0, tiled=True)
    neighbours = jnp.take(everything[:, :rank_size], near_index, axis=0)
    partner_lines = jnp.take(everything[:, rank_size:], adm_index, axis=0)
    near_part = jnp.einsum(
        "ikrq,ikpq->irp", neighbours, near_blocks, preferred_element_type=jnp.float32
    )
    far_sample = (samples.astype(jnp.float32) - near_part).astype(jnp.bfloat16)
    projected = jnp.einsum(
        "irp,isp->irs", leaf_basis, far_sample, preferred_element_type=jnp.float32
    ) * rank_size ** (-0.5)
    partner_weights = partner_lines.reshape(count_local, slot_total, rank_size, rank_size)
    slot_live = (jnp.arange(slot_total)[None, :] < adm_count[:, None])[:, :, None, None]
    partner_weights = jnp.where(slot_live, partner_weights, jnp.zeros((), jnp.bfloat16))
    blocks = coupling.reshape(count_local, rank_size, slot_total, rank_size)
    coupled = jnp.einsum(
        "irsc,isce->irse", blocks, partner_weights, preferred_element_type=jnp.float32
    )
    gram = jnp.einsum("iab,iac->ibc", projected, projected, precision=PRECISE)
    gram = (
        gram
        + jnp.einsum("irse,irsf->ief", coupled, coupled, precision=PRECISE)
        / (rank_size * slot_total)
        + identity
    )
    inner_grams, sent = local_levels(gram, leaf_transfer, inner_transfer)
    grams = []
    for level in range(1, total_levels + 1):
        hop = HOPS[level - 1]
        other = lax.ppermute(sent, AXES, [(d, d ^ hop) for d in range(devices)])
        if level < total_levels:
            start = devices - (devices >> level - 1)
            gram_here, sent = merge(start + (device >> level), sent, other, upper_transfer)
            grams.append(gram_here)
    root = pl.pallas_call(
        last_kernel, out_shape=jax.ShapeDtypeStruct((1, RANK, RANK), jnp.float32), name="last"
    )(sent, other)
    leaf_factors = factor(gram)
    inner_factors = factor(inner_grams)
    low = factor(jnp.stack(grams[:3]))
    high = factor(jnp.stack(grams[3:]))
    upper_factors = jnp.concatenate([low, high, root])
    return (leaf_factors, inner_factors[None], upper_factors[None])


def solution(mesh):
    split = P(AXES)
    return jax.shard_map(
        body,
        mesh=mesh,
        in_specs=(split,) * 11 + (P(),),
        out_specs=(split,) * 3,
        check_vma=False,
    )
```

time: 1070 us -> 215 us (0.20); the launches traced: 1060 us -> 214 us
  other arithmetic: 806 us -> 8.17 us
  waiting for transfers between devices: 136 us -> 95.6 us
  Pallas kernels: 0 us -> 33 us
  matrix products: 36.2 us -> 11.3 us
  local copies, waits for them, and re-layouts: 63.3 us -> 41.5 us
    another operation x32 -> x2, other arithmetic: 792 us -> 2.07 us  [the longest x1 1.42 us: body(): high = factor(jnp.stack(grams[3:]))]
    all_gather x2 -> x1, waiting for transfers between devices: 135 us -> 85.8 us  [body(): everything = lax.all_gather(packed, AXES, axis=0, tiled=True)]
    pallas_call x0 -> x12, Pallas kernels: none -> 33 us  [the longest x4 17 us: factor(): pl.pallas_call(factor_kernel, out_shape=jax.ShapeDtypeStruct(grams.shape,...]
    dot_general x18 -> x0, matrix products: 25.1 us -> none  [the longest x9 18.7 us: self_gram(): return jnp.einsum('nab,nac->nbc', weighted, weighted, precision=PRECISE)]
  transfers between devices with their start and end apart: 2 -> 8, of which waited for: 2 -> 4; matrix products, arithmetic and copies ran while one was open for 2% -> 5% of each run, Pallas kernels for 0% -> 8%
where the time goes in v1:
time: 215 us; the launch traced here: 214 us
  waiting for transfers between devices  95.6 us (44%)
  local copies, waits for them, and re-layouts  41.5 us (19%)
  Pallas kernels  33 us (15%)
  between operations  14.1 us (7%)
  matrix products  11.3 us (5%)
  starting transfers between devices  10.4 us (5%)
  other arithmetic  8.17 us (4%)
    all_gather x1, waiting for transfers between devices, body(): everything = lax.all_gather(packed, AXES, axis=0, tiled=True)  85.8 us
    pallas_call x4, Pallas kernels, factor(): pl.pallas_call(factor_kernel, out_shape=jax.ShapeDtypeStruct(grams.shape,...  17 us
    slice x1, local copies, waits for them, and re-layouts, body(): neighbours = jnp.take(everything[:, :rank_size], near_index, axis=0)  14.3 us
    ppermute x7, starting transfers between devices, body(): other = lax.ppermute(sent, AXES, [(d, d ^ hop) for d in range(devices)])  10.4 us
    pallas_call x6, Pallas kernels, merge(): pl.pallas_call(merge_kernel, grid_spec=pltpu.PrefetchScalarGridSpec(num_s...  10.1 us
    ppermute x7, waiting for transfers between devices, body(): other = lax.ppermute(sent, AXES, [(d, d ^ hop) for d in range(devices)])  9.74 us
    unnamed x29, local copies, waits for them, and re-layouts  8.41 us
    gather x1, local copies, waits for them, and re-layouts, body(): neighbours = jnp.take(everything[:, :rank_size], near_index, axis=0)  6.47 us
  transfers between devices with their start and end apart: 8, of which 4 were waited for; matrix products, arithmetic and copies ran while one was open for 5% of the time, Pallas kernels for 8%

profile of v1, /device:TPU:0, one launch (start us, length us, event | category | flops | bytes accessed | tf_op | source)
XLA Modules:
  0.0 214.2 jit_solution(9787571576720976830)
XLA Ops:
  7.2 0.0 copy-start
  7.2 0.0 all-gather.2.cloned.1.call-start
  7.2 1.0 reshape.71
  8.2 1.6 pad_maximum_fusion
  9.8 0.0 all-gather.2.cloned.1.call-update
  9.8 0.7 compare_select_fusion
  10.5 0.1 reshape.89
  10.6 2.0 copy.33
  12.6 0.7 compare_select_fusion.1
  13.3 0.1 reshape.81
  13.4 0.7 compare_and_fusion.1
  14.1 0.8 iota_compare_fusion.1
  14.9 85.8 %all-gather.2.cloned.1.call-done = bf16[512,80,256]{2,1,0:T(8,128)(2,1)} async-done(((bf16[4,80,256]{2,1,0:T(8,128)(2,1)}), bf16[512,80,256]{2,1,0:T(8,128)(2,1)}) %all-gather.2.cloned.1.call-update) | async-done | bytes 20971536 | tf_op jit(solution)/shard_map/all_gather | solution.py:172
  100.7 4.5 %slice.13 = bf16[512,16,256]{2,1,0:T(8,128)(2,1)} slice(bf16[512,80,256]{2,1,0:T(8,128)(2,1)} %all-gather.2.cloned.1.call-done), slice={[0:512], [64:80], [0:256]} | slice | bytes 8388608 | tf_op jit(solution)/shard_map/slice | solution.py:174
  105.2 2.8 %gather_fusion.1 = bf16[128,16,256]{2,1,0:T(8,128)(2,1)S(1)} fusion(bf16[512,16,256]{2,1,0:T(8,128)(2,1)} %slice.13, s32[1024]{0:T(1024)S(1)} %pad_clamp_fusion), kind=kCustom, calls=%fused_computation.1 | custom fusion | bytes 2097664 | tf_op jit(solution)/shard_map/jit(_take)/gather | solution.py:174
  108.1 1.8 gather.12
  109.9 2.6 %fusion.2 = f32[4,32,64,64]{3,2,1,0:T(8,128)S(1)} fusion(bf16[4,64,32,64]{1,3,2,0:T(8,128)(2,1)S(1)} %bitcast.45, bf16[4,32,64,64]{3,2,1,0:T(8,128)(2,1)} %gather.12, pred[4,32]{1,0:T(4,128)(4,1)S(1)} %get-tuple-element.32, pred[4,32]{1,0:T(4,128)(4,1)S(1)} %get-tuple-element.31), kind=kOutput, calls=%fused_computation.4 | convolution fusion | flops 68157440 | bytes 4194560 | tf_op jit(solution)/shard_map/irsc,isce->irse/dot_general | solution.py:186
  112.5 4.0 %fusion.15 = f32[4,64,64]{2,1,0:T(8,128)S(1)} fusion(f32[4,32,64,64]{3,2,1,0:T(8,128)S(1)} %fusion.2), kind=kOutput, calls=%fused_computation.17 | convolution fusion | flops 402669568 | bytes 2162688 | tf_op jit(solution)/shard_map/irse,irsf->ief/dot_general | solution.py:192
  116.5 0.0 copy-start.2
  116.6 14.3 %slice.12 = bf16[512,64,256]{2,1,0:T(8,128)(2,1)} slice(bf16[512,80,256]{2,1,0:T(8,128)(2,1)} %all-gather.2.cloned.1.call-done), slice={[0:512], [0:64], [0:256]} | slice | bytes 33554432 | tf_op jit(solution)/shard_map/slice | solution.py:173
  130.9 6.5 %gather_fusion = bf16[32,64,256]{2,1,0:T(8,128)(2,1)S(1)} fusion(bf16[512,64,256]{2,1,0:T(8,128)(2,1)} %slice.12, s32[1024]{0:T(1024)S(1)} %pad_clamp_fusion.1), kind=kCustom, calls=%fused_computation | custom fusion | bytes 2097280 | tf_op jit(solution)/shard_map/jit(_take)/gather | solution.py:173
  137.3 0.0 copy-done
  137.4 0.0 copy-done.2
  137.4 3.7 %fusion.10 = f32[4,64,64]{2,1,0:T(8,128)S(1)} fusion(bf16[4,64,256]{2,1,0:T(8,128)(2,1)S(1)} %copy-done, bf16[4,8,256,256]{3,2,1,0:T(8,128)(2,1)} %param.12, bf16[4,8,64,256]{3,2,1,0:T(8,128)(2,1)S(1)} %bitcast.46, pred[4,8]{1,0:T(4,128)(4,1)S(1)} %compare_and_fusion.1, bf16[4,64,256]{2,1,0:T(8,128)(2,1)S(1)} %copy-done.2), kind=kOutput, calls=%fused_computation.13 | convolution fusion | flops 277561344 | bytes 5570592 | tf_op jit(solution)/shard_map/irp,isp->irs/dot_general | solution.py:179
  141.1 1.0 fusion.14.grams.leaf_grams
  142.1 2.5 %local_levels.1 = (f32[3,64,64]{2,1,0:T(8,128)}, f32[64,64]{1,0:T(8,128)}) custom-call(f32[4,64,64]{2,1,0:T(8,128)} %fusion.14.grams.leaf_grams, bf16[4,64,64]{2,1,0:T(8,128)(2,1)} %leaf_transfer.1, bf16[1,3,64,64]{3,2,1,0:T(8,128)(2,1)} %inner_transfer.1), custom_call_target="tpu_custom_call" | custom-call | tf_op jit(solution)/shard_map/local_levels/pallas_call | solution.py:105
  144.6 0.3 collective-permute-start
  144.8 0.0 copy-done.1
  144.8 4.1 %copy.23.transfer = bf16[126,64,64]{2,1,0:T(8,128)(2,1)} copy(bf16[126,64,64]{0,2,1:T(8,128)(2,1)S(1)} %copy-done.1) | data formatting | bytes 2064384 | tf_op args[11]
  148.9 0.0 collective-permute-done.other
  148.9 0.6 copy-done.3
  149.5 1.7 merge.6
  151.2 0.5 collective-permute-start.1
  151.7 3.6 %collective-permute-done.1.other = f32[64,64]{1,0:T(8,128)S(1)} collective-permute-done((f32[64,64]{1,0:T(8,128)}, f32[64,64]{1,0:T(8,128)S(1)}, u32[]{:S(2)}, u32[]{:S(2)}) %collective-permute-start.1) | collective-permute-done | bytes 16416 | tf_op jit(solution)/shard_map/ppermute | solution.py:200
  155.4 0.6 copy-done.6
  156.0 1.7 merge.7
  157.7 1.9 collective-permute-start.2
  159.6 3.4 %collective-permute-done.2.other = f32[64,64]{1,0:T(8,128)S(1)} collective-permute-done((f32[64,64]{1,0:T(8,128)}, f32[64,64]{1,0:T(8,128)S(1)}, u32[]{:S(2)}, u32[]{:S(2)}) %collective-permute-start.2) | collective-permute-done | bytes 16416 | tf_op jit(solution)/shard_map/ppermute | solution.py:200
  163.0 0.6 copy-done.7
  163.6 1.7 merge.8
  165.3 1.5 collective-permute-start.3
  166.8 2.6 %collective-permute-done.3.other = f32[64,64]{1,0:T(8,128)S(1)} collective-permute-done((f32[64,64]{1,0:T(8,128)}, f32[64,64]{1,0:T(8,128)S(1)}, u32[]{:S(2)}, u32[]{:S(2)}) %collective-permute-start.3) | collective-permute-done | bytes 16416 | tf_op jit(solution)/shard_map/ppermute | solution.py:200
  169.4 0.6 copy-done.8
  170.1 1.7 merge.9
  171.7 2.7 %collective-permute-start.4 = (f32[64,64]{1,0:T(8,128)}, f32[64,64]{1,0:T(8,128)S(1)}, u32[]{:S(2)}, u32[]{:S(2)}) collective-permute-start(f32[64,64]{1,0:T(8,128)} %get-tuple-element.26.own), channel_id=1, source_target_pairs={{0,24},{1,25},{2,26},{3,27},{4,28},{5,29},{6,30},{7,31},{8,16},{9,... | collective-permute-start | bytes 49160 | tf_op jit(solution)/shard_map/ppermute | solution.py:200
  174.5 4.6 %factor.4 = f32[4,64,64]{2,1,0:T(8,128)} custom-call(f32[4,64,64]{2,1,0:T(8,128)} %fusion.14.grams.leaf_grams), custom_call_target="tpu_custom_call" | custom-call | tf_op jit(solution)/shard_map/factor/pallas_call | solution.py:86
  179.1 4.1 %factor.5 = f32[3,64,64]{2,1,0:T(8,128)} custom-call(f32[3,64,64]{2,1,0:T(8,128)} %get-tuple-element.17.grams), custom_call_target="tpu_custom_call" | custom-call | tf_op jit(solution)/shard_map/factor/pallas_call | solution.py:86
  183.2 0.0 collective-permute-done.4.other
  183.2 0.6 copy-done.4
  183.8 1.7 merge.10
  185.5 1.5 collective-permute-start.5
  187.0 0.0 copy-done.11
  187.0 0.7 pad_maximum_fusion.1.grams
  187.7 4.1 %factor.6 = f32[3,64,64]{2,1,0:T(8,128)} custom-call(f32[3,64,64]{2,1,0:T(8,128)} %pad_maximum_fusion.1.grams), custom_call_target="tpu_custom_call" | custom-call | tf_op jit(solution)/shard_map/factor/pallas_call | solution.py:86
  191.8 0.0 collective-permute-done.5.other
  191.8 0.6 copy-done.5
  192.4 1.7 merge.11
  194.1 2.1 collective-permute-start.6
  196.1 1.4 pad_maximum_fusion.2.grams
  197.6 4.1 %factor.7 = f32[3,64,64]{2,1,0:T(8,128)} custom-call(f32[3,64,64]{2,1,0:T(8,128)} %pad_maximum_fusion.2.grams), custom_call_target="tpu_custom_call" | custom-call | tf_op jit(solution)/shard_map/factor/pallas_call | solution.py:86
  201.7 0.0 collective-permute-done.6.other
  201.7 0.6 copy-done.9
  202.3 3.4 %last.1 = f32[1,64,64]{2,1,0:T(8,128)} custom-call(f32[64,64]{1,0:T(8,128)} %get-tuple-element.30.own, f32[64,64]{1,0:T(8,128)} %copy-done.9), custom_call_target="tpu_custom_call" | custom-call | tf_op jit(solution)/shard_map/last/pallas_call | solution.py:205
  205.7 1.7 maximum_bitcast_fusion
  (18 shorter events, 0.0 us)
Async XLA Ops:
  7.2 130.2 %copy-start = (bf16[4,64,256]{2,1,0:T(8,128)(2,1)S(1)}, bf16[4,64,256]{2,1,0:T(8,128)(2,1)}, u32[]{:S(2)}) copy-start(bf16[4,64,256]{2,1,0:T(8,128)(2,1)} %param.16) | copy-start | bytes 393220
  7.2 93.5 %all-gather.2.cloned.1.call-start = ((), (), s32[]{:S(2)}) async-start(), calls=%async_computation | async-start | bytes 21135360 | tf_op jit(solution)/shard_map/all_gather | solution.py:172
  116.5 20.8 %copy-start.2 = (bf16[4,64,256]{2,1,0:T(8,128)(2,1)S(1)}, bf16[4,64,256]{2,1,0:T(8,128)(2,1)}, u32[]{:S(2)}) copy-start(bf16[4,64,256]{2,1,0:T(8,128)(2,1)} %param.15) | copy-start | bytes 393220
  130.9 14.0 %copy-start.1 = (bf16[126,64,64]{0,2,1:T(8,128)(2,1)S(1)}, bf16[126,64,64]{0,2,1:T(8,128)(2,1)}, u32[]{:S(2)}) copy-start(bf16[126,64,64]{0,2,1:T(8,128)(2,1)} %param.23) | copy-start | bytes 3096580
  144.6 4.3 %collective-permute-start = (f32[64,64]{1,0:T(8,128)}, f32[64,64]{1,0:T(8,128)S(1)}, u32[]{:S(2)}, u32[]{:S(2)}) collective-permute-start(f32[64,64]{1,0:T(8,128)} %get-tuple-element.18.own), channel_id=1, source_target_pairs={{0,1},{1,0},{2,3},{3,2},{4,5},{5,4},{6,7},{7,6},{8,9},{9,8},{10,11... | collective-permute-start | bytes 49160 | tf_op jit(solution)/shard_map/ppermute | solution.py:200
  148.9 0.6 copy-start.3
  151.2 4.1 %collective-permute-start.1 = (f32[64,64]{1,0:T(8,128)}, f32[64,64]{1,0:T(8,128)S(1)}, u32[]{:S(2)}, u32[]{:S(2)}) collective-permute-start(f32[64,64]{1,0:T(8,128)} %get-tuple-element.20.own), channel_id=1, source_target_pairs={{0,2},{1,3},{2,0},{3,1},{4,6},{5,7},{6,4},{7,5},{8,10},{9,11},{10,... | collective-permute-start | bytes 49160 | tf_op jit(solution)/shard_map/ppermute | solution.py:200
  155.4 0.6 copy-start.6
  156.0 31.0 %copy-start.10 = (f32[64,64]{1,0:T(8,128)S(1)}, f32[64,64]{1,0:T(8,128)}, u32[]{:S(2)}) copy-start(f32[64,64]{1,0:T(8,128)} %get-tuple-element.19) | copy-start | bytes 49156
  157.7 29.3 %copy-start.11 = (f32[64,64]{1,0:T(8,128)S(1)}, f32[64,64]{1,0:T(8,128)}, u32[]{:S(2)}) copy-start(f32[64,64]{1,0:T(8,128)} %get-tuple-element.21) | copy-start | bytes 49156
  157.7 5.3 %collective-permute-start.2 = (f32[64,64]{1,0:T(8,128)}, f32[64,64]{1,0:T(8,128)S(1)}, u32[]{:S(2)}, u32[]{:S(2)}) collective-permute-start(f32[64,64]{1,0:T(8,128)} %get-tuple-element.22.own), channel_id=1, source_target_pairs={{0,6},{1,7},{2,4},{3,5},{4,2},{5,3},{6,0},{7,1},{8,14},{9,15},{10,... | collective-permute-start | bytes 49160 | tf_op jit(solution)/shard_map/ppermute | solution.py:200
  163.0 0.6 copy-start.7
  165.3 21.7 %copy-start.13 = (f32[64,64]{1,0:T(8,128)S(1)}, f32[64,64]{1,0:T(8,128)}, u32[]{:S(2)}) copy-start(f32[64,64]{1,0:T(8,128)} %get-tuple-element.23) | copy-start | bytes 49156
  165.3 4.1 %collective-permute-start.3 = (f32[64,64]{1,0:T(8,128)}, f32[64,64]{1,0:T(8,128)S(1)}, u32[]{:S(2)}, u32[]{:S(2)}) collective-permute-start(f32[64,64]{1,0:T(8,128)} %get-tuple-element.24.own), channel_id=1, source_target_pairs={{0,8},{1,9},{2,10},{3,11},{4,12},{5,13},{6,14},{7,15},{8,0},{9,1},... | collective-permute-start | bytes 49160 | tf_op jit(solution)/shard_map/ppermute | solution.py:200
  169.4 0.6 copy-start.8
  171.7 24.4 %copy-start.12 = (f32[64,64]{1,0:T(8,128)S(1)}, f32[64,64]{1,0:T(8,128)}, u32[]{:S(2)}) copy-start(f32[64,64]{1,0:T(8,128)} %get-tuple-element.25) | copy-start | bytes 49156
  171.7 11.5 %collective-permute-start.4 = (f32[64,64]{1,0:T(8,128)}, f32[64,64]{1,0:T(8,128)S(1)}, u32[]{:S(2)}, u32[]{:S(2)}) collective-permute-start(f32[64,64]{1,0:T(8,128)} %get-tuple-element.26.own), channel_id=1, source_target_pairs={{0,24},{1,25},{2,26},{3,27},{4,28},{5,29},{6,30},{7,31},{8,16},{9,... | collective-permute-start | bytes 49160 | tf_op jit(solution)/shard_map/ppermute | solution.py:200
  183.2 0.6 copy-start.4
  185.5 6.2 %collective-permute-start.5 = (f32[64,64]{1,0:T(8,128)}, f32[64,64]{1,0:T(8,128)S(1)}, u32[]{:S(2)}, u32[]{:S(2)}) collective-permute-start(f32[64,64]{1,0:T(8,128)} %get-tuple-element.28.own), channel_id=1, source_target_pairs={{0,32},{1,33},{2,34},{3,35},{4,36},{5,37},{6,38},{7,39},{8,40},{9,... | collective-permute-start | bytes 49160 | tf_op jit(solution)/shard_map/ppermute | solution.py:200
  191.8 0.6 copy-start.5
  194.1 7.6 %collective-permute-start.6 = (f32[64,64]{1,0:T(8,128)}, f32[64,64]{1,0:T(8,128)S(1)}, u32[]{:S(2)}, u32[]{:S(2)}) collective-permute-start(f32[64,64]{1,0:T(8,128)} %get-tuple-element.30.own), channel_id=1, source_target_pairs={{0,96},{1,97},{2,98},{3,99},{4,100},{5,101},{6,102},{7,103},{8,104... | collective-permute-start | bytes 49160 | tf_op jit(solution)/shard_map/ppermute | solution.py:200
  201.7 0.6 copy-start.9
Sparse Core Ops, SparseCore 0:
  11.5 89.1 all-gather.1

commit v2 on v1

--- a/solution.py
+++ b/solution.py
@@ -5,7 +5,6 @@
 from jax.experimental.pallas import tpu as pltpu
 from jax.sharding import PartitionSpec as P
 
-PRECISE = lax.Precision.HIGHEST
 AXES = ("leaf", "near")
 HOPS = (1, 2, 6, 8, 24, 32, 96)
 RANK = 64
@@ -20,6 +19,10 @@
 
 def dot32(a, b):
     return jnp.dot(a, b, preferred_element_type=jnp.float32)
+
+
+def dot_last(a, b):
+    return lax.dot_general(a, b, (((1,), (1,)), ((), ())), preferred_element_type=jnp.float32)
 
 
 def congruence(gram, transfer):
@@ -88,28 +91,263 @@
     )(grams)
 
 
-def local_kernel(leaf_grams, leaf_transfer, inner_transfer, inner_grams, sent):
+RING = ((0, 1, 2), (1, 2, 0))
+
+
+def chip_shift(device, stage, amount):
+    core = device & 1
+    axis = RING[core][stage]
+    at = 1 + 2 * axis
+    place = device >> at & 3
+    return device - (place << at) + ((place + amount & 3) << at)
+
+
+def ring_send(x, stage, amount, devices):
+    return lax.ppermute(x, AXES, [(d, chip_shift(d, stage, amount)) for d in range(devices)])
+
+
+def grid_places(device):
+    first = (device >> 1 & 1) + 2 * (device >> 4 & 1)
+    second = (device >> 2 & 1) + 2 * (device >> 5 & 1)
+    third = (device & 1) + 2 * (device >> 3 & 1) + 4 * (device >> 6 & 1)
+    return first, second, third
+
+
+def grid_device(first, second, third):
+    low = (third & 1) + 2 * (first & 1) + 4 * (second & 1) + 8 * (third >> 1 & 1)
+    return low + 16 * (first >> 1) + 32 * (second >> 1) + 64 * (third >> 2)
+
+
+def grid_send(x, dim, amount, devices):
+    pairs = []
+    for d in range(devices):
+        place = list(grid_places(d))
+        place[dim] += amount
+        if 0 <= place[dim] < (4, 4, 8)[dim]:
+            pairs.append((d, grid_device(*place)))
+    return lax.ppermute(x, AXES, pairs)
+
+
+def across_chips(x, devices):
+    pairs = []
+    for d in range(devices):
+        first, second, third = grid_places(d)
+        third += 1 if third & 1 else -1
+        if 0 <= third < 8:
+            pairs.append((d, grid_device(first, second, third)))
+    return lax.ppermute(x, AXES, pairs)
+
+
+def swap_cores(x, devices):
+    return lax.ppermute(x, AXES, [(d, d ^ 1) for d in range(devices)])
+
+
+def exchange_vectors(own, devices):
+    inside = swap_cores(own, devices)
+    outside = across_chips(own, devices)
+    layers = jnp.stack([inside, own, outside])
+    before = grid_send(layers[:, 2:4], 1, 1, devices)
+    after = grid_send(layers[:, 0:2], 1, -1, devices)
+    rows = jnp.concatenate([before, layers, after], axis=1)
+    left = grid_send(rows[:, 1::2], 0, 1, devices)
+    right = grid_send(rows[:, 0::2], 0, -1, devices)
+    return [own, inside, outside, before, after, left, right]
+
+
+def vector_slots(near_index, device):
+    first, second, third = grid_places(device)
+    cell = near_index
+    x = (cell & 1) + 2 * (cell >> 3 & 1) + 4 * (cell >> 6 & 1) - 2 * first
+    y = (cell >> 1 & 1) + 2 * (cell >> 4 & 1) + 4 * (cell >> 7 & 1) - 2 * second
+    z = (cell >> 2 & 1) + 2 * (cell >> 5 & 1) + 4 * (cell >> 8 & 1)
+    layer = jnp.where(z == third, 1, jnp.where(z >> 1 == third >> 1, 0, 2))
+    start = jnp.where(layer == 1, 0, jnp.where(layer == 0, 4, 8))
+    slot = start + x + 2 * y
+    slot = jnp.where(y == -1, 12 + 2 * layer + x, slot)
+    slot = jnp.where(y == 2, 18 + 2 * layer + x, slot)
+    slot = jnp.where(x == -1, 24 + 4 * layer + y + 1, slot)
+    return jnp.where(x == 2, 36 + 4 * layer + y + 1, slot)
+
+
+def exchange_weights(own, devices):
+    held = own
+    for stage in range(2):
+        parts = [ring_send(held, stage, k, devices) for k in (1, 3, 2)]
+        held = jnp.concatenate([held] + parts)
+    half = held.shape[0] // 2
+    back = ring_send(held, 2, 1, devices)
+    front = ring_send(held, 2, 3, devices)
+    far_low = ring_send(back[:half], 2, 1, devices)
+    far_high = ring_send(front[half:], 2, 3, devices)
+    mine = [held, back, front, far_low, far_high]
+    return mine + [swap_cores(x, devices) for x in mine]
+
+
+def weight_tiles(adm_index, device):
+    owner = adm_index >> 2
+    label = []
+    for axis in range(3):
+        ahead = (owner >> 1 + 2 * axis) - (device >> 1 + 2 * axis) & 3
+        label.append(jnp.where(ahead == 3, 1, jnp.where(ahead == 1, 2, jnp.where(ahead == 2, 3, 0))))
+    order = [
+        label[RING[0][2]] * 16 + label[RING[0][1]] * 4 + label[RING[0][0]],
+        label[RING[1][2]] * 16 + label[RING[1][1]] * 4 + label[RING[1][0]],
+    ]
+    core = owner & 1
+    other = core ^ (device & 1)
+    return other * 128 + 2 * jnp.where(core == 1, order[1], order[0]) + (adm_index >> 1 & 1)
+
+
+def load_pieces(pieces, buffer, semaphores):
+    at = 0
+    copies = []
+    for n, piece in enumerate(pieces):
+        copies.append(
+            pltpu.make_async_copy(piece, buffer.at[pl.ds(at, piece.shape[0])], semaphores.at[n])
+        )
+        at += piece.shape[0]
+    return copies
+
+
+def near_kernel(slots, blocks, samples, basis, *rest):
+    pieces, (gram, vectors, semaphores) = rest[:7], rest[7:]
+    leaf = pl.program_id(0)
+
+    @pl.when(leaf == 0)
+    def _():
+        copies = load_pieces(pieces, vectors, semaphores)
+        for copy in copies:
+            copy.start()
+        for copy in copies:
+            copy.wait()
+
+    total = None
+    for k in range(8):
+        part = dot_last(vectors[slots[8 * leaf + k]], blocks[0, k])
+        total = part if total is None else total + part
+    far = (samples[0].astype(jnp.float32) - total).astype(jnp.bfloat16)
+    scale = RANK**-0.5
+    wide = dot_last(basis[0], far) * scale
+    tall = dot_last(far, basis[0]) * scale
+    wide_hi = wide.astype(jnp.bfloat16)
+    wide_low = (wide - wide_hi.astype(jnp.float32)).astype(jnp.bfloat16)
+    tall_hi = tall.astype(jnp.bfloat16)
+    tall_low = (tall - tall_hi.astype(jnp.float32)).astype(jnp.bfloat16)
+    gram[0] = dot32(tall_hi, wide_hi) + (dot32(tall_hi, wide_low) + dot32(tall_low, wide_hi))
+
+
+def near_grams(slots, near_blocks, samples, leaf_basis, pieces):
+    count, per_leaf, size, _ = near_blocks.shape
+    rank = samples.shape[1]
+    row = pl.BlockSpec((1, rank, size), lambda i, slots: (i, 0, 0))
+    pieces = [piece.reshape(-1, rank, size) for piece in pieces]
+    return pl.pallas_call(
+        near_kernel,
+        grid_spec=pltpu.PrefetchScalarGridSpec(
+            num_scalar_prefetch=1,
+            grid=(count,),
+            in_specs=[
+                pl.BlockSpec((1, per_leaf, size, size), lambda i, slots: (i, 0, 0, 0)),
+                row,
+                row,
+            ]
+            + [pl.BlockSpec(memory_space=pl.ANY)] * len(pieces),
+            out_specs=pl.BlockSpec((1, rank, rank), lambda i, slots: (i, 0, 0)),
+            scratch_shapes=[
+                pltpu.VMEM((48, rank, size), jnp.bfloat16),
+                pltpu.SemaphoreType.DMA((len(pieces),)),
+            ],
+        ),
+        out_shape=jax.ShapeDtypeStruct((count, rank, rank), jnp.float32),
+        name="near_grams",
+    )(slots, near_blocks, samples, leaf_basis, *pieces)
+
+
+def leaf_kernel(tiles, halves, coupling, near_gram, leaf_transfer, inner_transfer, *rest):
+    pieces = rest[:10]
+    leaf_grams, inner_grams, sent, weights, coupled, moved, semaphores = rest[10:]
+    leaf = pl.program_id(0)
+
+    @pl.when(leaf == 0)
+    def _():
+        copies = load_pieces(pieces, weights, semaphores)
+        for copy in copies:
+            copy.start()
+        for copy in copies:
+            copy.wait()
+
+    side = lax.broadcasted_iota(jnp.int32, (RANK, 2 * RANK), 1) >> 6
+    nothing = jnp.zeros((RANK, 2 * RANK), jnp.bfloat16)
+    for pair in range(16):
+        chosen = []
+        for s in (2 * pair, 2 * pair + 1):
+            tile = weights[tiles[32 * leaf + s]]
+            chosen.append(jnp.where(side == halves[32 * leaf + s], tile, nothing))
+        both = jnp.concatenate(
+            [
+                jnp.concatenate([chosen[0], nothing], axis=1),
+                jnp.concatenate([nothing, chosen[1]], axis=1),
+            ],
+            axis=0,
+        )
+        product = dot32(coupling[0, :, 128 * pair : 128 * pair + 128], both).astype(jnp.bfloat16)
+        coupled[128 * pair : 128 * pair + 64, :] = product[:, :128]
+        coupled[128 * pair + 64 : 128 * pair + 128, :] = product[:, 128:]
+    square = lax.dot_general(
+        coupled[...], coupled[...], (((0,), (0,)), ((), ())), preferred_element_type=jnp.float32
+    )
+    sums = square[:RANK, :RANK] + square[RANK:, RANK:]
     unit = unit_matrix()
-    moved = [congruence(leaf_grams[i], leaf_transfer[i]) for i in range(4)]
-    first = 0.5 * (moved[0] + moved[1]) + unit
-    second = 0.5 * (moved[2] + moved[3]) + unit
-    inner_grams[0] = first
-    inner_grams[1] = second
-    top = 0.5 * (congruence(first, inner_transfer[0, 0]) + congruence(second, inner_transfer[0, 1]))
-    top = top + unit
-    inner_grams[2] = top
-    sent[...] = congruence(top, inner_transfer[0, 2])
-
-
-def local_levels(leaf_grams, leaf_transfer, inner_transfer):
+    gram = near_gram[0] + sums * (1.0 / 2048) + unit
+    leaf_grams[leaf] = gram
+    moved[leaf] = congruence(gram, leaf_transfer[leaf])
+
+    @pl.when(leaf == 3)
+    def _():
+        first = 0.5 * (moved[0] + moved[1]) + unit
+        second = 0.5 * (moved[2] + moved[3]) + unit
+        inner_grams[0] = first
+        inner_grams[1] = second
+        top = congruence(first, inner_transfer[0, 0]) + congruence(second, inner_transfer[0, 1])
+        top = 0.5 * top + unit
+        inner_grams[2] = top
+        sent[...] = congruence(top, inner_transfer[0, 2])
+
+
+def leaf_levels(tiles, halves, coupling, near_gram, leaf_transfer, inner_transfer, pieces):
+    count, rank, width = coupling.shape
+    f32 = jnp.float32
     return pl.pallas_call(
-        local_kernel,
-        out_shape=(
-            jax.ShapeDtypeStruct((3, RANK, RANK), jnp.float32),
-            jax.ShapeDtypeStruct((RANK, RANK), jnp.float32),
+        leaf_kernel,
+        grid_spec=pltpu.PrefetchScalarGridSpec(
+            num_scalar_prefetch=2,
+            grid=(count,),
+            in_specs=[
+                pl.BlockSpec((1, rank, width), lambda i, *_: (i, 0, 0)),
+                pl.BlockSpec((1, rank, rank), lambda i, *_: (i, 0, 0)),
+                pl.BlockSpec((count, rank, rank), lambda i, *_: (0, 0, 0)),
+                pl.BlockSpec((1, count - 1, rank, rank), lambda i, *_: (0, 0, 0, 0)),
+            ]
+            + [pl.BlockSpec(memory_space=pl.ANY)] * len(pieces),
+            out_specs=[
+                pl.BlockSpec((count, rank, rank), lambda i, *_: (0, 0, 0)),
+                pl.BlockSpec((count - 1, rank, rank), lambda i, *_: (0, 0, 0)),
+                pl.BlockSpec((rank, rank), lambda i, *_: (0, 0)),
+            ],
+            scratch_shapes=[
+                pltpu.VMEM((256, rank, 2 * rank), jnp.bfloat16),
+                pltpu.VMEM((width, 2 * rank), jnp.bfloat16),
+                pltpu.VMEM((count, rank, rank), f32),
+                pltpu.SemaphoreType.DMA((len(pieces),)),
+            ],
         ),
-        name="local_levels",
-    )(leaf_grams, leaf_transfer, inner_transfer)
+        out_shape=[
+            jax.ShapeDtypeStruct((count, rank, rank), f32),
+            jax.ShapeDtypeStruct((count - 1, rank, rank), f32),
+            jax.ShapeDtypeStruct((rank, rank), f32),
+        ],
+        name="leaf_levels",
+    )(tiles, halves, coupling, near_gram, leaf_transfer, inner_transfer, *pieces)
 
 
 def merge_kernel(at, own, other, transfer, gram, sent):
@@ -158,42 +396,28 @@
     inner_transfer,
     upper_transfer,
 ):
-    count_local, rank_size, leaf_size = test_vectors.shape
-    slot_total = adm_index.shape[1]
-    weight_lines = rank_size * rank_size // leaf_size
-    identity = jnp.eye(rank_size, dtype=jnp.float32)
-    near_size = lax.axis_size("near")
-    devices = lax.axis_size("leaf") * near_size
+    count, rank, size = test_vectors.shape
+    slots = adm_index.shape[1]
+    devices = lax.axis_size("leaf") * lax.axis_size("near")
     total_levels = devices.bit_length() - 1
-    device = lax.axis_index("leaf") * near_size + lax.axis_index("near")
-    packed = jnp.concatenate(
-        [test_vectors, col_weights.reshape(count_local, weight_lines, leaf_size)], axis=1
+    device = lax.axis_index("leaf") * lax.axis_size("near") + lax.axis_index("near")
+    paired = jnp.concatenate([col_weights[0::2], col_weights[1::2]], axis=2)
+    weights = exchange_weights(paired, devices)
+    vectors = exchange_vectors(test_vectors, devices)
+    near_gram = near_grams(
+        vector_slots(near_index, device).reshape(-1), near_blocks, samples, leaf_basis, vectors
     )
-    everything = lax.all_gather(packed, AXES, axis=0, tiled=True)
-    neighbours = jnp.take(everything[:, :rank_size], near_index, axis=0)
-    partner_lines = jnp.take(everything[:, rank_size:], adm_index, axis=0)
-    near_part = jnp.einsum(
-        "ikrq,ikpq->irp", neighbours, near_blocks, preferred_element_type=jnp.float32
+    live = jnp.arange(slots)[None, :] < adm_count[:, None]
+    halves = jnp.where(live, adm_index & 1, 2)
+    gram, inner_grams, sent = leaf_levels(
+        weight_tiles(adm_index, device).reshape(-1),
+        halves.reshape(-1),
+        coupling,
+        near_gram,
+        leaf_transfer,
+        inner_transfer,
+        weights,
     )
-    far_sample = (samples.astype(jnp.float32) - near_part).astype(jnp.bfloat16)
-    projected = jnp.einsum(
-        "irp,isp->irs", leaf_basis, far_sample, preferred_element_type=jnp.float32
-    ) * rank_size ** (-0.5)
-    partner_weights = partner_lines.reshape(count_local, slot_total, rank_size, rank_size)
-    slot_live = (jnp.arange(slot_total)[None, :] < adm_count[:, None])[:, :, None, None]
-    partner_weights = jnp.where(slot_live, partner_weights, jnp.zeros((), jnp.bfloat16))
-    blocks = coupling.reshape(count_local, rank_size, slot_total, rank_size)
-    coupled = jnp.einsum(
-        "irsc,isce->irse", blocks, partner_weights, preferred_element_type=jnp.float32
-    )
-    gram = jnp.einsum("iab,iac->ibc", projected, projected, precision=PRECISE)
-    gram = (
-        gram
-        + jnp.einsum("irse,irsf->ief", coupled, coupled, precision=PRECISE)
-        / (rank_size * slot_total)
-        + identity
-    )
-    inner_grams, sent = local_levels(gram, leaf_transfer, inner_transfer)
     grams = []
     for level in range(1, total_levels + 1):
         hop = HOPS[level - 1]

time: 215 us -> 142 us (0.66)
  waiting for transfers between devices: 95.6 us -> 25 us
  starting transfers between devices: 10.4 us -> 47.8 us
  local copies, waits for them, and re-layouts: 41.5 us -> 13.6 us
  Pallas kernels: 33 us -> 47 us
  between operations: 14.1 us -> 1.02 us
  matrix products: 11.3 us -> 0 us
    all_gather x1 -> x0, waiting for transfers between devices: 85.8 us -> none  [body(): everything = lax.all_gather(packed, AXES, axis=0, tiled=True)]
    ppermute x0 -> x21, starting transfers between devices: none -> 32.2 us  [the longest x10 21.3 us: ring_send(): lax.ppermute(x, AXES, [(d, chip_shift(d, stage, amount)) for d in range(d...]
    ppermute x0 -> x21, waiting for transfers between devices: none -> 17.3 us  [the longest x4 14.3 us: grid_send(): return lax.ppermute(x, AXES, pairs)]
    slice x2 -> x5, local copies, waits for them, and re-layouts: 18.8 us -> 2.49 us  [the longest x1 0.81 us: exchange_weights(): far_high = ring_send(front[half:], 2, 3, devices)]
    pallas_call x1 -> x2, Pallas kernels: 2.53 us -> 16.4 us  [the longest x1 8.88 us: leaf_levels(): pl.pallas_call(leaf_kernel, grid_spec=pltpu.PrefetchScalarGridSpec(num_sc...]
    dot_general x4 -> x0, matrix products: 11.3 us -> none  [the longest x1 4.03 us: body(): jnp.einsum('irse,irsf->ief', coupled, coupled, precision=PRECISE)]
    gather x3 -> x0, local copies, waits for them, and re-layouts: 11.1 us -> none  [the longest x1 6.47 us: body(): neighbours = jnp.take(everything[:, :rank_size], near_index, axis=0)]
    ppermute x7, starting transfers between devices: 10.4 us -> 15.6 us  [body(): other = lax.ppermute(sent, AXES, [(d, d ^ hop) for d in range(devices)])]
  transfers between devices with their start and end apart: 8 -> 28, of which waited for: 4 -> 7; matrix products, arithmetic and copies ran while one was open for 5% -> 9% of each run, Pallas kernels for 8% -> 17%
where the time goes in v2:
time: 142 us; the launch traced here: 140 us
  starting transfers between devices  47.8 us (34%)
  Pallas kernels  47 us (33%)
  waiting for transfers between devices  25 us (18%)
  local copies, waits for them, and re-layouts  13.6 us (10%)
  other arithmetic  6.11 us (4%)
    ppermute x10, starting transfers between devices, ring_send(): lax.ppermute(x, AXES, [(d, chip_shift(d, stage, amount)) for d in range(d...  21.3 us
    pallas_call x4, Pallas kernels, factor(): pl.pallas_call(factor_kernel, out_shape=jax.ShapeDtypeStruct(grams.shape,...  17 us
    ppermute x7, starting transfers between devices, body(): other = lax.ppermute(sent, AXES, [(d, d ^ hop) for d in range(devices)])  15.6 us
    ppermute x4, waiting for transfers between devices, grid_send(): return lax.ppermute(x, AXES, pairs)  14.3 us
    pallas_call x6, Pallas kernels, merge(): pl.pallas_call(merge_kernel, grid_spec=pltpu.PrefetchScalarGridSpec(num_s...  10.2 us
    unnamed x56, local copies, waits for them, and re-layouts  9.23 us
    ppermute x4, starting transfers between devices, grid_send(): return lax.ppermute(x, AXES, pairs)  9.22 us
    pallas_call x1, Pallas kernels, leaf_levels(): pl.pallas_call(leaf_kernel, grid_spec=pltpu.PrefetchScalarGridSpec(num_sc...  8.88 us
  transfers between devices with their start and end apart: 28, of which 7 were waited for; matrix products, arithmetic and copies ran while one was open for 9% of the time, Pallas kernels for 17%

profile of v2, /device:TPU:0, one launch (start us, length us, event | category | flops | bytes accessed | tf_op | source)
XLA Modules:
  0.0 140.5 jit_solution(12903652090935139315)
XLA Ops:
  0.7 0.8 fusion.7
  1.6 2.1 %collective-permute-start.6 = (bf16[2,64,128]{2,1,0:T(8,128)(2,1)S(1)}, bf16[2,64,128]{2,1,0:T(8,128)(2,1)S(1)}, u32[]{:S(2)}, u32[]{:S(2)}) collective-permute-start(bf16[2,64,128]{2,1,0:T(8,128)(2,1)S(1)} %get-tuple-element.34), channel_id=1, source_target_pairs={{0,2},{1,9},{2,4},{3,11},{4,6},{5,13},{6,0},{7,15},{8,10},{9,17},{... | collective-permute-start | bytes 98312 | tf_op jit(solution)/shard_map/ppermute | solution.py:106
  3.6 2.2 %collective-permute-start.7 = (bf16[2,64,128]{2,1,0:T(8,128)(2,1)S(1)}, bf16[2,64,128]{2,1,0:T(8,128)(2,1)S(1)}, u32[]{:S(2)}, u32[]{:S(2)}) collective-permute-start(bf16[2,64,128]{2,1,0:T(8,128)(2,1)S(1)} %get-tuple-element.34), channel_id=1, source_target_pairs={{0,6},{1,25},{2,0},{3,27},{4,2},{5,29},{6,4},{7,31},{8,14},{9,1},{... | collective-permute-start | bytes 98312 | tf_op jit(solution)/shard_map/ppermute | solution.py:106
  5.9 1.8 %collective-permute-start.8 = (bf16[2,64,128]{2,1,0:T(8,128)(2,1)S(1)}, bf16[2,64,128]{2,1,0:T(8,128)(2,1)S(1)}, u32[]{:S(2)}, u32[]{:S(2)}) collective-permute-start(bf16[2,64,128]{2,1,0:T(8,128)(2,1)S(1)} %get-tuple-element.34), channel_id=1, source_target_pairs={{0,4},{1,17},{2,6},{3,19},{4,0},{5,21},{6,2},{7,23},{8,12},{9,25},... | collective-permute-start | bytes 98312 | tf_op jit(solution)/shard_map/ppermute | solution.py:106
  7.6 0.7 collective-permute-start.1
  8.3 2.9 %collective-permute-done.8 = bf16[2,64,128]{2,1,0:T(8,128)(2,1)S(1)} collective-permute-done((bf16[2,64,128]{2,1,0:T(8,128)(2,1)S(1)}, bf16[2,64,128]{2,1,0:T(8,128)(2,1)S(1)}, u32[]{:S(2)}, u32[]{:S(2)}) %collective-permute-start.8) | collective-permute-done | bytes 32800 | tf_op jit(solution)/shard_map/ppermute | solution.py:106
  11.4 1.6 %collective-permute-start.9 = (bf16[8,64,128]{2,1,0:T(8,128)(2,1)S(1)}, bf16[8,64,128]{2,1,0:T(8,128)(2,1)S(1)}, u32[]{:S(2)}, u32[]{:S(2)}) collective-permute-start(bf16[8,64,128]{2,1,0:T(8,128)(2,1)S(1)} %pad_maximum_fusion.2), channel_id=1, source_target_pairs={{0,8},{1,33},{2,10},{3,35},{4,12},{5,37},{6,14},{7,39},{8,16},{9,4... | collective-permute-start | bytes 393224 | tf_op jit(solution)/shard_map/ppermute | solution.py:106
  13.0 1.7 %collective-permute-start.10 = (bf16[8,64,128]{2,1,0:T(8,128)(2,1)S(1)}, bf16[8,64,128]{2,1,0:T(8,128)(2,1)S(1)}, u32[]{:S(2)}, u32[]{:S(2)}) collective-permute-start(bf16[8,64,128]{2,1,0:T(8,128)(2,1)S(1)} %pad_maximum_fusion.2), channel_id=1, source_target_pairs={{0,24},{1,97},{2,26},{3,99},{4,28},{5,101},{6,30},{7,103},{8,0},{9... | collective-permute-start | bytes 393224 | tf_op jit(solution)/shard_map/ppermute | solution.py:106
  14.7 2.0 %collective-permute-start.11 = (bf16[8,64,128]{2,1,0:T(8,128)(2,1)S(1)}, bf16[8,64,128]{2,1,0:T(8,128)(2,1)S(1)}, u32[]{:S(2)}, u32[]{:S(2)}) collective-permute-start(bf16[8,64,128]{2,1,0:T(8,128)(2,1)S(1)} %pad_maximum_fusion.2), channel_id=1, source_target_pairs={{0,16},{1,65},{2,18},{3,67},{4,20},{5,69},{6,22},{7,71},{8,24},{9,... | collective-permute-start | bytes 393224 | tf_op jit(solution)/shard_map/ppermute | solution.py:106
  16.7 1.0 pad_maximum_fusion.1
  17.8 3.7 %collective-permute-start.2 = (bf16[3,2,64,256]{3,2,1,0:T(8,128)(2,1)S(1)}, bf16[3,2,64,256]{3,2,1,0:T(8,128)(2,1)S(1)}, u32[]{:S(2)}, u32[]{:S(2)}) collective-permute-start(bf16[3,2,64,256]{3,2,1,0:T(8,128)(2,1)S(1)} %get-tuple-element.38), channel_id=1, source_target_pairs={{0,4},{1,5},{2,6},{3,7},{4,32},{5,33},{6,34},{7,35},{8,12},{9,13},... | collective-permute-start | bytes 589832 | tf_op jit(solution)/shard_map/ppermute | solution.py:128
  21.5 1.3 collective-permute-start.3
  22.9 4.8 %collective-permute-start.12 = (bf16[32,64,128]{2,1,0:T(8,128)(2,1)S(1)}, bf16[32,64,128]{2,1,0:T(8,128)(2,1)S(1)}, u32[]{:S(2)}, u32[]{:S(2)}) collective-permute-start(bf16[32,64,128]{2,1,0:T(8,128)(2,1)S(1)} %constant_dynamic-update-slice_fusion.rest_0_), channel_id=1, source_target_pairs={{0,32},{1,3},{2,34},{3,5},{4,36},{5,7},{6,38},{7,1},{8,40},{9,11},... | collective-permute-start | bytes 1572872 | tf_op jit(solution)/shard_map/ppermute | solution.py:106
  27.7 1.9 %collective-permute-start.13 = (bf16[32,64,128]{2,1,0:T(8,128)(2,1)S(1)}, bf16[32,64,128]{2,1,0:T(8,128)(2,1)S(1)}, u32[]{:S(2)}, u32[]{:S(2)}) collective-permute-start(bf16[32,64,128]{2,1,0:T(8,128)(2,1)S(1)} %constant_dynamic-update-slice_fusion.rest_0_), channel_id=1, source_target_pairs={{0,96},{1,7},{2,98},{3,1},{4,100},{5,3},{6,102},{7,5},{8,104},{9,1... | collective-permute-start | bytes 1572872 | tf_op jit(solution)/shard_map/ppermute | solution.py:106
  29.6 1.2 collective-permute-done.2
  30.8 1.8 %collective-permute-done.3 = bf16[3,2,64,256]{3,2,1,0:T(8,128)(2,1)S(1)} collective-permute-done((bf16[3,2,64,256]{3,2,1,0:T(8,128)(2,1)S(1)}, bf16[3,2,64,256]{3,2,1,0:T(8,128)(2,1)S(1)}, u32[]{:S(2)}, u32[]{:S(2)}) %collective-permute-start.3) | collective-permute-done | bytes 196640 | tf_op jit(solution)/shard_map/ppermute | solution.py:128
  32.7 1.1 pad_maximum_fusion
  33.8 2.9 %collective-permute-start.4 = (bf16[3,4,64,256]{3,2,1,0:T(8,128)(2,1)S(1)}, bf16[3,4,64,256]{3,2,1,0:T(8,128)(2,1)S(1)}, u32[]{:S(2)}, u32[]{:S(2)}) collective-permute-start(bf16[3,4,64,256]{3,2,1,0:T(8,128)(2,1)S(1)} %get-tuple-element.36), channel_id=1, source_target_pairs={{0,2},{1,3},{2,16},{3,17},{4,6},{5,7},{6,20},{7,21},{8,10},{9,11},... | collective-permute-start | bytes 1179656 | tf_op jit(solution)/shard_map/ppermute | solution.py:128
  36.8 1.3 collective-permute-start.5
  38.1 0.8 slice.34
  38.9 1.5 %collective-permute-start.14 = (bf16[16,64,128]{2,1,0:T(8,128)(2,1)}, bf16[16,64,128]{2,1,0:T(8,128)(2,1)}, u32[]{:S(2)}, u32[]{:S(2)}) collective-permute-start(bf16[16,64,128]{2,1,0:T(8,128)(2,1)} %slice.34), channel_id=1, source_target_pairs={{0,32},{1,3},{2,34},{3,5},{4,36},{5,7},{6,38},{7,1},{8,40},{9,11},... | collective-permute-start | bytes 786440 | tf_op jit(solution)/shard_map/ppermute | solution.py:106
  40.4 0.8 slice.35
  41.2 1.8 %collective-permute-start.15 = (bf16[16,64,128]{2,1,0:T(8,128)(2,1)}, bf16[16,64,128]{2,1,0:T(8,128)(2,1)}, u32[]{:S(2)}, u32[]{:S(2)}) collective-permute-start(bf16[16,64,128]{2,1,0:T(8,128)(2,1)} %slice.35), channel_id=1, source_target_pairs={{0,96},{1,7},{2,98},{3,1},{4,100},{5,3},{6,102},{7,5},{8,104},{9,1... | collective-permute-start | bytes 786440 | tf_op jit(solution)/shard_map/ppermute | solution.py:106
  43.0 11.3 %collective-permute-done.4 = bf16[3,4,64,256]{3,2,1,0:T(8,128)(2,1)S(1)} collective-permute-done((bf16[3,4,64,256]{3,2,1,0:T(8,128)(2,1)S(1)}, bf16[3,4,64,256]{3,2,1,0:T(8,128)(2,1)S(1)}, u32[]{:S(2)}, u32[]{:S(2)}) %collective-permute-start.4) | collective-permute-done | bytes 393248 | tf_op jit(solution)/shard_map/ppermute | solution.py:128
  54.3 0.5 collective-permute-start.18
  54.8 0.1 collective-permute-start.19
  54.9 0.4 collective-permute-start.20
  55.3 0.6 reshape.48.slots
  56.0 0.6 reshape.46.tiles
  56.6 0.6 reshape.47.halves
  57.2 7.6 %near_grams.1.near_gram = f32[4,64,64]{2,1,0:T(8,128)} custom-call(s32[32]{0:T(128)} %reshape.48.slots, bf16[4,8,256,256]{3,2,1,0:T(8,128)(2,1)} %blocks.1, bf16[4,64,256]{2,1,0:T(8,128)(2,1)} %samples.1, bf16[4,64,256]{2,1,0:T(8,128)(2,1)} %basis.1, bf16[4,64,256]{2,1,0:T(8,128)(2,1)} %rest_0_.1, bf16[4,64,256]{2,1,0:T(8,128)(2,1)} %copy-done.2, ...), custom_call_target="tpu_custom_call" | custom-call | tf_op jit(solution)/shard_map/near_grams/pallas_call | solution.py:244
  64.9 0.7 copy-done.8
  65.6 8.9 %leaf_levels.1 = (f32[4,64,64]{2,1,0:T(8,128)}, f32[3,64,64]{2,1,0:T(8,128)}, f32[64,64]{1,0:T(8,128)}) custom-call(s32[128]{0:T(128)} %reshape.46.tiles, s32[128]{0:T(128)} %reshape.47.halves, bf16[4,64,2048]{2,1,0:T(8,128)(2,1)} %coupling.1, f32[4,64,64]{2,1,0:T(8,128)} %near_grams.1.near_gram, bf16[4,64,64]{2,1,0:T(8,128)(2,1)} %leaf_transfer.1, ...), custom_call_target="tpu_custom_call" | custom-call | tf_op jit(solution)/shard_map/leaf_levels/pallas_call | solution.py:320
  74.5 0.2 collective-permute-start.21
  74.7 4.0 %copy.15.transfer = bf16[126,64,64]{2,1,0:T(8,128)(2,1)} copy(bf16[126,64,64]{0,2,1:T(8,128)(2,1)S(1)} %copy-done.4) | data formatting | bytes 2064384 | tf_op args[11]
  78.8 0.6 copy-done.16
  79.4 1.7 %merge.6 = (f32[64,64]{1,0:T(8,128)}, f32[64,64]{1,0:T(8,128)}) custom-call(s32[1]{0:T(128)} %bitcast.8.at, f32[64,64]{1,0:T(8,128)} %get-tuple-element.20.own, f32[64,64]{1,0:T(8,128)} %copy-done.16, bf16[126,64,64]{2,1,0:T(8,128)(2,1)} %copy.15.transfer), custom_call_target="tpu_custom_call" | custom-call | tf_op jit(solution)/shard_map/merge/pallas_call | solution.py:361
  81.1 2.5 %collective-permute-start.22 = (f32[64,64]{1,0:T(8,128)}, f32[64,64]{1,0:T(8,128)S(1)}, u32[]{:S(2)}, u32[]{:S(2)}) collective-permute-start(f32[64,64]{1,0:T(8,128)} %get-tuple-element.22.own), channel_id=1, source_target_pairs={{0,2},{1,3},{2,0},{3,1},{4,6},{5,7},{6,4},{7,5},{8,10},{9,11},{10,... | collective-permute-start | bytes 49160 | tf_op jit(solution)/shard_map/ppermute | solution.py:424
  83.6 2.2 %collective-permute-done.22.other = f32[64,64]{1,0:T(8,128)S(1)} collective-permute-done((f32[64,64]{1,0:T(8,128)}, f32[64,64]{1,0:T(8,128)S(1)}, u32[]{:S(2)}, u32[]{:S(2)}) %collective-permute-start.22) | collective-permute-done | bytes 16416 | tf_op jit(solution)/shard_map/ppermute | solution.py:424
  85.7 0.6 copy-done.13
  86.4 1.7 %merge.7 = (f32[64,64]{1,0:T(8,128)}, f32[64,64]{1,0:T(8,128)}) custom-call(s32[1]{0:T(128)} %bitcast.10.at, f32[64,64]{1,0:T(8,128)} %get-tuple-element.22.own, f32[64,64]{1,0:T(8,128)} %copy-done.13, bf16[126,64,64]{2,1,0:T(8,128)(2,1)} %copy.15.transfer), custom_call_target="tpu_custom_call" | custom-call | tf_op jit(solution)/shard_map/merge/pallas_call | solution.py:361
  88.1 1.9 %collective-permute-start.23 = (f32[64,64]{1,0:T(8,128)}, f32[64,64]{1,0:T(8,128)S(1)}, u32[]{:S(2)}, u32[]{:S(2)}) collective-permute-start(f32[64,64]{1,0:T(8,128)} %get-tuple-element.24.own), channel_id=1, source_target_pairs={{0,6},{1,7},{2,4},{3,5},{4,2},{5,3},{6,0},{7,1},{8,14},{9,15},{10,... | collective-permute-start | bytes 49160 | tf_op jit(solution)/shard_map/ppermute | solution.py:424
  89.9 3.5 %collective-permute-done.23.other = f32[64,64]{1,0:T(8,128)S(1)} collective-permute-done((f32[64,64]{1,0:T(8,128)}, f32[64,64]{1,0:T(8,128)S(1)}, u32[]{:S(2)}, u32[]{:S(2)}) %collective-permute-start.23) | collective-permute-done | bytes 16416 | tf_op jit(solution)/shard_map/ppermute | solution.py:424
  93.4 0.6 copy-done.14
  94.0 1.7 %merge.8 = (f32[64,64]{1,0:T(8,128)}, f32[64,64]{1,0:T(8,128)}) custom-call(s32[1]{0:T(128)} %bitcast.12.at, f32[64,64]{1,0:T(8,128)} %get-tuple-element.24.own, f32[64,64]{1,0:T(8,128)} %copy-done.14, bf16[126,64,64]{2,1,0:T(8,128)(2,1)} %copy.15.transfer), custom_call_target="tpu_custom_call" | custom-call | tf_op jit(solution)/shard_map/merge/pallas_call | solution.py:361
  95.7 2.3 %collective-permute-start.24 = (f32[64,64]{1,0:T(8,128)}, f32[64,64]{1,0:T(8,128)S(1)}, u32[]{:S(2)}, u32[]{:S(2)}) collective-permute-start(f32[64,64]{1,0:T(8,128)} %get-tuple-element.26.own), channel_id=1, source_target_pairs={{0,8},{1,9},{2,10},{3,11},{4,12},{5,13},{6,14},{7,15},{8,0},{9,1},... | collective-permute-start | bytes 49160 | tf_op jit(solution)/shard_map/ppermute | solution.py:424
  98.0 2.1 %collective-permute-done.24.other = f32[64,64]{1,0:T(8,128)S(1)} collective-permute-done((f32[64,64]{1,0:T(8,128)}, f32[64,64]{1,0:T(8,128)S(1)}, u32[]{:S(2)}, u32[]{:S(2)}) %collective-permute-start.24) | collective-permute-done | bytes 16416 | tf_op jit(solution)/shard_map/ppermute | solution.py:424
  100.1 0.6 copy-done.15
  100.7 1.7 %merge.9 = (f32[64,64]{1,0:T(8,128)}, f32[64,64]{1,0:T(8,128)}) custom-call(s32[1]{0:T(128)} %bitcast.14.at, f32[64,64]{1,0:T(8,128)} %get-tuple-element.26.own, f32[64,64]{1,0:T(8,128)} %copy-done.15, bf16[126,64,64]{2,1,0:T(8,128)(2,1)} %copy.15.transfer), custom_call_target="tpu_custom_call" | custom-call | tf_op jit(solution)/shard_map/merge/pallas_call | solution.py:361
  102.4 4.0 %collective-permute-start.25 = (f32[64,64]{1,0:T(8,128)}, f32[64,64]{1,0:T(8,128)S(1)}, u32[]{:S(2)}, u32[]{:S(2)}) collective-permute-start(f32[64,64]{1,0:T(8,128)} %get-tuple-element.28.own), channel_id=1, source_target_pairs={{0,24},{1,25},{2,26},{3,27},{4,28},{5,29},{6,30},{7,31},{8,16},{9,... | collective-permute-start | bytes 49160 | tf_op jit(solution)/shard_map/ppermute | solution.py:424
  106.5 4.6 %factor.4 = f32[4,64,64]{2,1,0:T(8,128)} custom-call(f32[4,64,64]{2,1,0:T(8,128)} %get-tuple-element.18.grams), custom_call_target="tpu_custom_call" | custom-call | tf_op jit(solution)/shard_map/factor/pallas_call | solution.py:89
  111.1 4.1 %factor.5 = f32[3,64,64]{2,1,0:T(8,128)} custom-call(f32[3,64,64]{2,1,0:T(8,128)} %get-tuple-element.19.grams), custom_call_target="tpu_custom_call" | custom-call | tf_op jit(solution)/shard_map/factor/pallas_call | solution.py:89
  115.2 0.6 copy-done.11
  115.8 1.7 %merge.10 = (f32[64,64]{1,0:T(8,128)}, f32[64,64]{1,0:T(8,128)}) custom-call(s32[1]{0:T(128)} %bitcast.16.at, f32[64,64]{1,0:T(8,128)} %get-tuple-element.28.own, f32[64,64]{1,0:T(8,128)} %copy-done.11, bf16[126,64,64]{2,1,0:T(8,128)(2,1)} %copy.15.transfer), custom_call_target="tpu_custom_call" | custom-call | tf_op jit(solution)/shard_map/merge/pallas_call | solution.py:361
  117.5 4.6 %collective-permute-start.26 = (f32[64,64]{1,0:T(8,128)}, f32[64,64]{1,0:T(8,128)S(1)}, u32[]{:S(2)}, u32[]{:S(2)}) collective-permute-start(f32[64,64]{1,0:T(8,128)} %get-tuple-element.30.own), channel_id=1, source_target_pairs={{0,32},{1,33},{2,34},{3,35},{4,36},{5,37},{6,38},{7,39},{8,40},{9,... | collective-permute-start | bytes 49160 | tf_op jit(solution)/shard_map/ppermute | solution.py:424
  122.2 0.7 pad_maximum_fusion.3.grams
  122.8 4.1 %factor.6 = f32[3,64,64]{2,1,0:T(8,128)} custom-call(f32[3,64,64]{2,1,0:T(8,128)} %pad_maximum_fusion.3.grams), custom_call_target="tpu_custom_call" | custom-call | tf_op jit(solution)/shard_map/factor/pallas_call | solution.py:89
  127.0 0.6 copy-done.12
  127.6 1.7 %merge.11 = (f32[64,64]{1,0:T(8,128)}, f32[64,64]{1,0:T(8,128)}) custom-call(s32[1]{0:T(128)} %bitcast.18.at, f32[64,64]{1,0:T(8,128)} %get-tuple-element.30.own, f32[64,64]{1,0:T(8,128)} %copy-done.12, bf16[126,64,64]{2,1,0:T(8,128)(2,1)} %copy.15.transfer), custom_call_target="tpu_custom_call" | custom-call | tf_op jit(solution)/shard_map/merge/pallas_call | solution.py:361
  129.3 1.4 %pad_maximum_fusion.4.grams = f32[3,64,64]{2,1,0:T(8,128)} fusion(f32[1,64,64]{2,1,0:T(8,128)} %bitcast.38, f32[1,64,64]{2,1,0:T(8,128)} %bitcast.37, f32[1,64,64]{2,1,0:T(8,128)S(1)} %bitcast.35), kind=kLoop, calls=%fused_computation.5 | loop fusion | flops 24576 | bytes 98304 | tf_op jit(solution)/shard_map/stack | solution.py:435
  130.7 4.1 %factor.7 = f32[3,64,64]{2,1,0:T(8,128)} custom-call(f32[3,64,64]{2,1,0:T(8,128)} %pad_maximum_fusion.4.grams), custom_call_target="tpu_custom_call" | custom-call | tf_op jit(solution)/shard_map/factor/pallas_call | solution.py:89
  134.8 0.6 copy-done.17
  135.5 3.4 %last.1 = f32[1,64,64]{2,1,0:T(8,128)} custom-call(f32[64,64]{1,0:T(8,128)} %get-tuple-element.32.own, f32[64,64]{1,0:T(8,128)} %copy-done.17), custom_call_target="tpu_custom_call" | custom-call | tf_op jit(solution)/shard_map/last/pallas_call | solution.py:429
  138.8 1.7 %maximum_bitcast_fusion = f32[1,7,64,64]{3,2,1,0:T(8,128)} fusion(f32[1,64,64]{2,1,0:T(8,128)} %last.1, f32[3,64,64]{2,1,0:T(8,128)} %factor.7, f32[3,64,64]{2,1,0:T(8,128)} %factor.6), kind=kLoop, calls=%fused_computation.2 | loop fusion | flops 57344 | bytes 229376 | tf_op jit(solution)/shard_map/broadcast_in_dim | solution.py:437
  (79 shorter events, 0.6 us)
Async XLA Ops:
  0.6 54.7 %copy-start.22 = (s32[4,8]{1,0:T(4,128)S(1)}, s32[4,8]{1,0:T(4,128)}, u32[]{:S(2)}) copy-start(s32[4,8]{1,0:T(4,128)} %param.13) | copy-start | bytes 388
  0.6 55.3 %copy-start.23 = (s32[4,32]{1,0:T(4,128)S(1)}, s32[4,32]{1,0:T(4,128)}, u32[]{:S(2)}) copy-start(s32[4,32]{1,0:T(4,128)} %param.19) | copy-start | bytes 1540
  0.7 55.3 %copy-start.24 = (s32[4]{0:T(128)S(1)}, s32[4]{0:T(128)}, u32[]{:S(2)}) copy-start(s32[4]{0:T(128)} %param.20) | copy-start | bytes 52
  1.6 6.8 %collective-permute-start.6 = (bf16[2,64,128]{2,1,0:T(8,128)(2,1)S(1)}, bf16[2,64,128]{2,1,0:T(8,128)(2,1)S(1)}, u32[]{:S(2)}, u32[]{:S(2)}) collective-permute-start(bf16[2,64,128]{2,1,0:T(8,128)(2,1)S(1)} %get-tuple-element.34), channel_id=1, source_target_pairs={{0,2},{1,9},{2,4},{3,11},{4,6},{5,13},{6,0},{7,15},{8,10},{9,17},{... | collective-permute-start | bytes 98312 | tf_op jit(solution)/shard_map/ppermute | solution.py:106
  3.6 4.7 %collective-permute-start.7 = (bf16[2,64,128]{2,1,0:T(8,128)(2,1)S(1)}, bf16[2,64,128]{2,1,0:T(8,128)(2,1)S(1)}, u32[]{:S(2)}, u32[]{:S(2)}) collective-permute-start(bf16[2,64,128]{2,1,0:T(8,128)(2,1)S(1)} %get-tuple-element.34), channel_id=1, source_target_pairs={{0,6},{1,25},{2,0},{3,27},{4,2},{5,29},{6,4},{7,31},{8,14},{9,1},{... | collective-permute-start | bytes 98312 | tf_op jit(solution)/shard_map/ppermute | solution.py:106
  5.9 5.4 %collective-permute-start.8 = (bf16[2,64,128]{2,1,0:T(8,128)(2,1)S(1)}, bf16[2,64,128]{2,1,0:T(8,128)(2,1)S(1)}, u32[]{:S(2)}, u32[]{:S(2)}) collective-permute-start(bf16[2,64,128]{2,1,0:T(8,128)(2,1)S(1)} %get-tuple-element.34), channel_id=1, source_target_pairs={{0,4},{1,17},{2,6},{3,19},{4,0},{5,21},{6,2},{7,23},{8,12},{9,25},... | collective-permute-start | bytes 98312 | tf_op jit(solution)/shard_map/ppermute | solution.py:106
  7.6 9.1 %collective-permute-start = (bf16[4,64,256]{2,1,0:T(8,128)(2,1)}, bf16[4,64,256]{2,1,0:T(8,128)(2,1)S(1)}, u32[]{:S(2)}, u32[]{:S(2)}) collective-permute-start(bf16[4,64,256]{2,1,0:T(8,128)(2,1)} %rest_0_.1), channel_id=1, source_target_pairs={{0,1},{1,0},{2,3},{3,2},{4,5},{5,4},{6,7},{7,6},{8,9},{9,8},{10,11... | collective-permute-start | bytes 393224 | tf_op jit(solution)/shard_map/ppermute | solution.py:142
  7.6 9.1 %collective-permute-start.1 = (bf16[4,64,256]{2,1,0:T(8,128)(2,1)}, bf16[4,64,256]{2,1,0:T(8,128)(2,1)S(1)}, u32[]{:S(2)}, u32[]{:S(2)}) collective-permute-start(bf16[4,64,256]{2,1,0:T(8,128)(2,1)} %rest_0_.1), channel_id=1, source_target_pairs={{1,8},{3,10},{5,12},{7,14},{8,1},{9,64},{10,3},{11,66},{12,5},{13,... | collective-permute-start | bytes 393224 | tf_op jit(solution)/shard_map/ppermute | solution.py:138
  11.4 11.5 %collective-permute-start.9 = (bf16[8,64,128]{2,1,0:T(8,128)(2,1)S(1)}, bf16[8,64,128]{2,1,0:T(8,128)(2,1)S(1)}, u32[]{:S(2)}, u32[]{:S(2)}) collective-permute-start(bf16[8,64,128]{2,1,0:T(8,128)(2,1)S(1)} %pad_maximum_fusion.2), channel_id=1, source_target_pairs={{0,8},{1,33},{2,10},{3,35},{4,12},{5,37},{6,14},{7,39},{8,16},{9,4... | collective-permute-start | bytes 393224 | tf_op jit(solution)/shard_map/ppermute | solution.py:106
  13.0 9.8 %collective-permute-start.10 = (bf16[8,64,128]{2,1,0:T(8,128)(2,1)S(1)}, bf16[8,64,128]{2,1,0:T(8,128)(2,1)S(1)}, u32[]{:S(2)}, u32[]{:S(2)}) collective-permute-start(bf16[8,64,128]{2,1,0:T(8,128)(2,1)S(1)} %pad_maximum_fusion.2), channel_id=1, source_target_pairs={{0,24},{1,97},{2,26},{3,99},{4,28},{5,101},{6,30},{7,103},{8,0},{9... | collective-permute-start | bytes 393224 | tf_op jit(solution)/shard_map/ppermute | solution.py:106
  14.7 8.2 %collective-permute-start.11 = (bf16[8,64,128]{2,1,0:T(8,128)(2,1)S(1)}, bf16[8,64,128]{2,1,0:T(8,128)(2,1)S(1)}, u32[]{:S(2)}, u32[]{:S(2)}) collective-permute-start(bf16[8,64,128]{2,1,0:T(8,128)(2,1)S(1)} %pad_maximum_fusion.2), channel_id=1, source_target_pairs={{0,16},{1,65},{2,18},{3,67},{4,20},{5,69},{6,22},{7,71},{8,24},{9,... | collective-permute-start | bytes 393224 | tf_op jit(solution)/shard_map/ppermute | solution.py:106
  16.7 40.5 %copy-start.2 = (bf16[4,64,256]{2,1,0:T(8,128)(2,1)}, bf16[4,64,256]{2,1,0:T(8,128)(2,1)S(1)}, u32[]{:S(2)}) copy-start(bf16[4,64,256]{2,1,0:T(8,128)(2,1)S(1)} %collective-permute-done.rest_1_) | copy-start | bytes 393220
  16.7 40.5 %copy-start.3 = (bf16[4,64,256]{2,1,0:T(8,128)(2,1)}, bf16[4,64,256]{2,1,0:T(8,128)(2,1)S(1)}, u32[]{:S(2)}) copy-start(bf16[4,64,256]{2,1,0:T(8,128)(2,1)S(1)} %collective-permute-done.1.rest_2_) | copy-start | bytes 393220
  17.8 13.0 %collective-permute-start.2 = (bf16[3,2,64,256]{3,2,1,0:T(8,128)(2,1)S(1)}, bf16[3,2,64,256]{3,2,1,0:T(8,128)(2,1)S(1)}, u32[]{:S(2)}, u32[]{:S(2)}) collective-permute-start(bf16[3,2,64,256]{3,2,1,0:T(8,128)(2,1)S(1)} %get-tuple-element.38), channel_id=1, source_target_pairs={{0,4},{1,5},{2,6},{3,7},{4,32},{5,33},{6,34},{7,35},{8,12},{9,13},... | collective-permute-start | bytes 589832 | tf_op jit(solution)/shard_map/ppermute | solution.py:128
  21.5 11.2 %collective-permute-start.3 = (bf16[3,2,64,256]{3,2,1,0:T(8,128)(2,1)S(1)}, bf16[3,2,64,256]{3,2,1,0:T(8,128)(2,1)S(1)}, u32[]{:S(2)}, u32[]{:S(2)}) collective-permute-start(bf16[3,2,64,256]{3,2,1,0:T(8,128)(2,1)S(1)} %get-tuple-element.37), channel_id=1, source_target_pairs={{4,0},{5,1},{6,2},{7,3},{12,8},{13,9},{14,10},{15,11},{20,16},{21,... | collective-permute-start | bytes 589832 | tf_op jit(solution)/shard_map/ppermute | solution.py:128
  22.9 41.9 %copy-start.7 = (bf16[32,64,128]{2,1,0:T(8,128)(2,1)}, bf16[32,64,128]{2,1,0:T(8,128)(2,1)S(1)}, u32[]{:S(2)}) copy-start(bf16[32,64,128]{2,1,0:T(8,128)(2,1)S(1)} %constant_dynamic-update-slice_fusion.rest_0_) | copy-start | bytes 1572868
  22.9 15.2 %collective-permute-start.12 = (bf16[32,64,128]{2,1,0:T(8,128)(2,1)S(1)}, bf16[32,64,128]{2,1,0:T(8,128)(2,1)S(1)}, u32[]{:S(2)}, u32[]{:S(2)}) collective-permute-start(bf16[32,64,128]{2,1,0:T(8,128)(2,1)S(1)} %constant_dynamic-update-slice_fusion.rest_0_), channel_id=1, source_target_pairs={{0,32},{1,3},{2,34},{3,5},{4,36},{5,7},{6,38},{7,1},{8,40},{9,11},... | collective-permute-start | bytes 1572872 | tf_op jit(solution)/shard_map/ppermute | solution.py:106
  27.7 12.6 %collective-permute-start.13 = (bf16[32,64,128]{2,1,0:T(8,128)(2,1)S(1)}, bf16[32,64,128]{2,1,0:T(8,128)(2,1)S(1)}, u32[]{:S(2)}, u32[]{:S(2)}) collective-permute-start(bf16[32,64,128]{2,1,0:T(8,128)(2,1)S(1)} %constant_dynamic-update-slice_fusion.rest_0_), channel_id=1, source_target_pairs={{0,96},{1,7},{2,98},{3,1},{4,100},{5,3},{6,102},{7,5},{8,104},{9,1... | collective-permute-start | bytes 1572872 | tf_op jit(solution)/shard_map/ppermute | solution.py:106
  30.8 26.4 %copy-start.5 = (bf16[3,2,64,256]{3,2,1,0:T(8,128)(2,1)}, bf16[3,2,64,256]{3,2,1,0:T(8,128)(2,1)S(1)}, u32[]{:S(2)}) copy-start(bf16[3,2,64,256]{3,2,1,0:T(8,128)(2,1)S(1)} %collective-permute-done.2) | copy-start | bytes 589828
  32.7 24.5 %copy-start.6 = (bf16[3,2,64,256]{3,2,1,0:T(8,128)(2,1)}, bf16[3,2,64,256]{3,2,1,0:T(8,128)(2,1)S(1)}, u32[]{:S(2)}) copy-start(bf16[3,2,64,256]{3,2,1,0:T(8,128)(2,1)S(1)} %collective-permute-done.3) | copy-start | bytes 589828
  33.8 20.4 %collective-permute-start.4 = (bf16[3,4,64,256]{3,2,1,0:T(8,128)(2,1)S(1)}, bf16[3,4,64,256]{3,2,1,0:T(8,128)(2,1)S(1)}, u32[]{:S(2)}, u32[]{:S(2)}) collective-permute-start(bf16[3,4,64,256]{3,2,1,0:T(8,128)(2,1)S(1)} %get-tuple-element.36), channel_id=1, source_target_pairs={{0,2},{1,3},{2,16},{3,17},{4,6},{5,7},{6,20},{7,21},{8,10},{9,11},... | collective-permute-start | bytes 1179656 | tf_op jit(solution)/shard_map/ppermute | solution.py:128
  36.8 17.5 %collective-permute-start.5 = (bf16[3,4,64,256]{3,2,1,0:T(8,128)(2,1)S(1)}, bf16[3,4,64,256]{3,2,1,0:T(8,128)(2,1)S(1)}, u32[]{:S(2)}, u32[]{:S(2)}) collective-permute-start(bf16[3,4,64,256]{3,2,1,0:T(8,128)(2,1)S(1)} %get-tuple-element.35), channel_id=1, source_target_pairs={{2,0},{3,1},{6,4},{7,5},{10,8},{11,9},{14,12},{15,13},{16,2},{17,3... | collective-permute-start | bytes 1179656 | tf_op jit(solution)/shard_map/ppermute | solution.py:128
  38.1 26.8 %copy-start = (bf16[32,64,128]{2,1,0:T(8,128)(2,1)}, bf16[32,64,128]{2,1,0:T(8,128)(2,1)S(1)}, u32[]{:S(2)}) copy-start(bf16[32,64,128]{2,1,0:T(8,128)(2,1)S(1)} %collective-permute-done.12.rest_1_) | copy-start | bytes 1572868
  38.9 15.9 %collective-permute-start.14 = (bf16[16,64,128]{2,1,0:T(8,128)(2,1)}, bf16[16,64,128]{2,1,0:T(8,128)(2,1)}, u32[]{:S(2)}, u32[]{:S(2)}) collective-permute-start(bf16[16,64,128]{2,1,0:T(8,128)(2,1)} %slice.34), channel_id=1, source_target_pairs={{0,32},{1,3},{2,34},{3,5},{4,36},{5,7},{6,38},{7,1},{8,40},{9,11},... | collective-permute-start | bytes 786440 | tf_op jit(solution)/shard_map/ppermute | solution.py:106
  40.4 24.5 %copy-start.1 = (bf16[32,64,128]{2,1,0:T(8,128)(2,1)}, bf16[32,64,128]{2,1,0:T(8,128)(2,1)S(1)}, u32[]{:S(2)}) copy-start(bf16[32,64,128]{2,1,0:T(8,128)(2,1)S(1)} %collective-permute-done.13.rest_2_) | copy-start | bytes 1572868
  41.2 13.7 %collective-permute-start.15 = (bf16[16,64,128]{2,1,0:T(8,128)(2,1)}, bf16[16,64,128]{2,1,0:T(8,128)(2,1)}, u32[]{:S(2)}, u32[]{:S(2)}) collective-permute-start(bf16[16,64,128]{2,1,0:T(8,128)(2,1)} %slice.35), channel_id=1, source_target_pairs={{0,96},{1,7},{2,98},{3,1},{4,100},{5,3},{6,102},{7,5},{8,104},{9,1... | collective-permute-start | bytes 786440 | tf_op jit(solution)/shard_map/ppermute | solution.py:106
  43.0 21.9 %collective-permute-start.16 = (bf16[32,64,128]{2,1,0:T(8,128)(2,1)S(1)}, bf16[32,64,128]{2,1,0:T(8,128)(2,1)S(1)}, u32[]{:S(2)}, u32[]{:S(2)}) collective-permute-start(bf16[32,64,128]{2,1,0:T(8,128)(2,1)S(1)} %constant_dynamic-update-slice_fusion.rest_0_), channel_id=1, source_target_pairs={{0,1},{1,0},{2,3},{3,2},{4,5},{5,4},{6,7},{7,6},{8,9},{9,8},{10,11... | collective-permute-start | bytes 1572872 | tf_op jit(solution)/shard_map/ppermute | solution.py:142
  54.2 3.0 %copy-start.9 = (bf16[3,4,64,256]{3,2,1,0:T(8,128)(2,1)}, bf16[3,4,64,256]{3,2,1,0:T(8,128)(2,1)S(1)}, u32[]{:S(2)}) copy-start(bf16[3,4,64,256]{3,2,1,0:T(8,128)(2,1)S(1)} %collective-permute-done.4) | copy-start | bytes 1179652
  54.2 10.6 %collective-permute-start.17 = (bf16[32,64,128]{2,1,0:T(8,128)(2,1)S(1)}, bf16[32,64,128]{2,1,0:T(8,128)(2,1)}, u32[]{:S(2)}, u32[]{:S(2)}) collective-permute-start(bf16[32,64,128]{2,1,0:T(8,128)(2,1)S(1)} %collective-permute-done.12.rest_1_), channel_id=1, source_target_pairs={{0,1},{1,0},{2,3},{3,2},{4,5},{5,4},{6,7},{7,6},{8,9},{9,8},{10,11... | collective-permute-start | bytes 1572872 | tf_op jit(solution)/shard_map/ppermute | solution.py:142
  54.3 3.0 %copy-start.10 = (bf16[3,4,64,256]{3,2,1,0:T(8,128)(2,1)}, bf16[3,4,64,256]{3,2,1,0:T(8,128)(2,1)S(1)}, u32[]{:S(2)}) copy-start(bf16[3,4,64,256]{3,2,1,0:T(8,128)(2,1)S(1)} %collective-permute-done.5) | copy-start | bytes 1179652
  54.3 10.6 %collective-permute-start.18 = (bf16[32,64,128]{2,1,0:T(8,128)(2,1)S(1)}, bf16[32,64,128]{2,1,0:T(8,128)(2,1)}, u32[]{:S(2)}, u32[]{:S(2)}) collective-permute-start(bf16[32,64,128]{2,1,0:T(8,128)(2,1)S(1)} %collective-permute-done.13.rest_2_), channel_id=1, source_target_pairs={{0,1},{1,0},{2,3},{3,2},{4,5},{5,4},{6,7},{7,6},{8,9},{9,8},{10,11... | collective-permute-start | bytes 1572872 | tf_op jit(solution)/shard_map/ppermute | solution.py:142
  54.8 10.1 %collective-permute-start.19 = (bf16[16,64,128]{2,1,0:T(8,128)(2,1)}, bf16[16,64,128]{2,1,0:T(8,128)(2,1)}, u32[]{:S(2)}, u32[]{:S(2)}) collective-permute-start(bf16[16,64,128]{2,1,0:T(8,128)(2,1)} %collective-permute-done.14.rest_3_), channel_id=1, source_target_pairs={{0,1},{1,0},{2,3},{3,2},{4,5},{5,4},{6,7},{7,6},{8,9},{9,8},{10,11... | collective-permute-start | bytes 786440 | tf_op jit(solution)/shard_map/ppermute | solution.py:142
  54.9 10.0 %collective-permute-start.20 = (bf16[16,64,128]{2,1,0:T(8,128)(2,1)}, bf16[16,64,128]{2,1,0:T(8,128)(2,1)}, u32[]{:S(2)}, u32[]{:S(2)}) collective-permute-start(bf16[16,64,128]{2,1,0:T(8,128)(2,1)} %collective-permute-done.15.rest_4_), channel_id=1, source_target_pairs={{0,1},{1,0},{2,3},{3,2},{4,5},{5,4},{6,7},{7,6},{8,9},{9,8},{10,11... | collective-permute-start | bytes 786440 | tf_op jit(solution)/shard_map/ppermute | solution.py:142
  64.8 9.9 %copy-start.4 = (bf16[126,64,64]{0,2,1:T(8,128)(2,1)S(1)}, bf16[126,64,64]{0,2,1:T(8,128)(2,1)}, u32[]{:S(2)}) copy-start(bf16[126,64,64]{0,2,1:T(8,128)(2,1)} %param.23) | copy-start | bytes 3096580
  64.8 0.8 copy-start.8
  74.5 4.2 %collective-permute-start.21 = (f32[64,64]{1,0:T(8,128)}, f32[64,64]{1,0:T(8,128)S(1)}, u32[]{:S(2)}, u32[]{:S(2)}) collective-permute-start(f32[64,64]{1,0:T(8,128)} %get-tuple-element.20.own), channel_id=1, source_target_pairs={{0,1},{1,0},{2,3},{3,2},{4,5},{5,4},{6,7},{7,6},{8,9},{9,8},{10,11... | collective-permute-start | bytes 49160 | tf_op jit(solution)/shard_map/ppermute | solution.py:424
  78.8 0.6 copy-start.16
  81.1 4.6 %collective-permute-start.22 = (f32[64,64]{1,0:T(8,128)}, f32[64,64]{1,0:T(8,128)S(1)}, u32[]{:S(2)}, u32[]{:S(2)}) collective-permute-start(f32[64,64]{1,0:T(8,128)} %get-tuple-element.22.own), channel_id=1, source_target_pairs={{0,2},{1,3},{2,0},{3,1},{4,6},{5,7},{6,4},{7,5},{8,10},{9,11},{10,... | collective-permute-start | bytes 49160 | tf_op jit(solution)/shard_map/ppermute | solution.py:424
  85.7 0.6 copy-start.13
  86.4 35.8 %copy-start.18 = (f32[64,64]{1,0:T(8,128)S(1)}, f32[64,64]{1,0:T(8,128)}, u32[]{:S(2)}) copy-start(f32[64,64]{1,0:T(8,128)} %get-tuple-element.21) | copy-start | bytes 49156
  88.1 34.1 %copy-start.19 = (f32[64,64]{1,0:T(8,128)S(1)}, f32[64,64]{1,0:T(8,128)}, u32[]{:S(2)}) copy-start(f32[64,64]{1,0:T(8,128)} %get-tuple-element.23) | copy-start | bytes 49156
  88.1 5.3 %collective-permute-start.23 = (f32[64,64]{1,0:T(8,128)}, f32[64,64]{1,0:T(8,128)S(1)}, u32[]{:S(2)}, u32[]{:S(2)}) collective-permute-start(f32[64,64]{1,0:T(8,128)} %get-tuple-element.24.own), channel_id=1, source_target_pairs={{0,6},{1,7},{2,4},{3,5},{4,2},{5,3},{6,0},{7,1},{8,14},{9,15},{10,... | collective-permute-start | bytes 49160 | tf_op jit(solution)/shard_map/ppermute | solution.py:424
  93.4 0.6 copy-start.14
  95.7 26.5 %copy-start.21 = (f32[64,64]{1,0:T(8,128)S(1)}, f32[64,64]{1,0:T(8,128)}, u32[]{:S(2)}) copy-start(f32[64,64]{1,0:T(8,128)} %get-tuple-element.25) | copy-start | bytes 49156
  95.7 4.4 %collective-permute-start.24 = (f32[64,64]{1,0:T(8,128)}, f32[64,64]{1,0:T(8,128)S(1)}, u32[]{:S(2)}, u32[]{:S(2)}) collective-permute-start(f32[64,64]{1,0:T(8,128)} %get-tuple-element.26.own), channel_id=1, source_target_pairs={{0,8},{1,9},{2,10},{3,11},{4,12},{5,13},{6,14},{7,15},{8,0},{9,1},... | collective-permute-start | bytes 49160 | tf_op jit(solution)/shard_map/ppermute | solution.py:424
  100.1 0.6 copy-start.15
  102.4 26.9 %copy-start.20 = (f32[64,64]{1,0:T(8,128)S(1)}, f32[64,64]{1,0:T(8,128)}, u32[]{:S(2)}) copy-start(f32[64,64]{1,0:T(8,128)} %get-tuple-element.27) | copy-start | bytes 49156
  102.4 12.8 %collective-permute-start.25 = (f32[64,64]{1,0:T(8,128)}, f32[64,64]{1,0:T(8,128)S(1)}, u32[]{:S(2)}, u32[]{:S(2)}) collective-permute-start(f32[64,64]{1,0:T(8,128)} %get-tuple-element.28.own), channel_id=1, source_target_pairs={{0,24},{1,25},{2,26},{3,27},{4,28},{5,29},{6,30},{7,31},{8,16},{9,... | collective-permute-start | bytes 49160 | tf_op jit(solution)/shard_map/ppermute | solution.py:424
  115.2 0.6 copy-start.11
  117.5 9.4 %collective-permute-start.26 = (f32[64,64]{1,0:T(8,128)}, f32[64,64]{1,0:T(8,128)S(1)}, u32[]{:S(2)}, u32[]{:S(2)}) collective-permute-start(f32[64,64]{1,0:T(8,128)} %get-tuple-element.30.own), channel_id=1, source_target_pairs={{0,32},{1,33},{2,34},{3,35},{4,36},{5,37},{6,38},{7,39},{8,40},{9,... | collective-permute-start | bytes 49160 | tf_op jit(solution)/shard_map/ppermute | solution.py:424
  127.0 0.6 copy-start.12
  129.3 5.6 %collective-permute-start.27 = (f32[64,64]{1,0:T(8,128)}, f32[64,64]{1,0:T(8,128)S(1)}, u32[]{:S(2)}, u32[]{:S(2)}) collective-permute-start(f32[64,64]{1,0:T(8,128)} %get-tuple-element.32.own), channel_id=1, source_target_pairs={{0,96},{1,97},{2,98},{3,99},{4,100},{5,101},{6,102},{7,103},{8,104... | collective-permute-start | bytes 49160 | tf_op jit(solution)/shard_map/ppermute | solution.py:424
  134.8 0.6 copy-start.17

commit v3 on v1

v3 whole, which is shorter than its diff:
```python
import functools

import jax
import jax.numpy as jnp
from jax import lax
from jax.experimental import pallas as pl
from jax.experimental.pallas import tpu as pltpu
from jax.sharding import PartitionSpec as P

AXES = ("leaf", "near")
HOPS = (1, 2, 6, 8, 24, 32, 96)
RANK = 64


def split_three(x):
    hi = x.astype(jnp.bfloat16)
    rest = x - hi.astype(jnp.float32)
    mid = rest.astype(jnp.bfloat16)
    return hi, mid, (rest - mid.astype(jnp.float32)).astype(jnp.bfloat16)


def dot32(a, b):
    return jnp.dot(a, b, preferred_element_type=jnp.float32)


def dot_last(a, b):
    return lax.dot_general(a, b, (((1,), (1,)), ((), ())), preferred_element_type=jnp.float32)


def congruence(gram, transfer):
    across = jnp.transpose(transfer.astype(jnp.float32)).astype(jnp.bfloat16)
    hi, mid, low = split_three(gram)
    half = dot32(hi, transfer) + (dot32(mid, transfer) + dot32(low, transfer))
    hi, mid, low = split_three(half)
    return dot32(across, hi) + (dot32(across, mid) + dot32(across, low))


def unit_matrix():
    rows = lax.broadcasted_iota(jnp.int32, (RANK, RANK), 0)
    cols = lax.broadcasted_iota(jnp.int32, (RANK, RANK), 1)
    return (rows == cols).astype(jnp.float32)


def factor_panels(matrices):
    shape = (8, RANK)
    work = [list(panels) for panels in matrices]
    rows = lax.broadcasted_iota(jnp.int32, shape, 0)
    cols = lax.broadcasted_iota(jnp.int32, shape, 1)
    factors = [[None] * 8 for _ in work]
    for step in range(8):
        base = 8 * step
        for panels, factor in zip(work, factors):
            panel = panels[step]
            column = [
                jnp.broadcast_to(panel[:, base + k : base + k + 1], shape) for k in range(8)
            ]
            weights = [
                [jnp.broadcast_to(lower[:, base + k : base + k + 1], shape) for k in range(8)]
                for lower in panels[step + 1 :]
            ]
            rows_out = jnp.zeros(shape, jnp.float32)
            for j in range(8):
                here = rows == j
                pivot = jnp.broadcast_to(column[j][j : j + 1, :], shape)
                panel_row = jnp.broadcast_to(panel[j : j + 1, :], shape)
                rows_out = jnp.where(here, panel_row * lax.rsqrt(pivot), rows_out)
                inverse = 1.0 / pivot
                scale = column[j] * inverse
                for k in range(j + 1, 8):
                    entry = jnp.broadcast_to(column[k][j : j + 1, :], shape)
                    column[k] = jnp.where(here, entry * inverse, column[k] - scale * entry)
                panel = jnp.where(here, panel_row * inverse, panel - scale * panel_row)
            factor[step] = jnp.where(cols >= rows + base, rows_out, 0.0)
            for at, weight in enumerate(weights):
                lower = panels[step + 1 + at]
                for k in range(8):
                    lower = lower - weight[k] * jnp.broadcast_to(panel[k : k + 1, :], shape)
                panels[step + 1 + at] = lower
    return factors


def in_vmem(x):
    return pltpu.with_memory_space_constraint(x, pltpu.VMEM)


def panels_of(matrix):
    return [matrix[8 * p : 8 * p + 8, :] for p in range(8)]


def factor_kernel(leaf_grams, inner_grams, leaf_factors, inner_factors):
    count = leaf_grams.shape[0]
    grams = [leaf_grams[n] for n in range(count)] + [inner_grams[n] for n in range(count - 1)]
    for n, panels in enumerate(factor_panels([panels_of(gram) for gram in grams])):
        for p in range(8):
            if n < count:
                leaf_factors[n, 8 * p : 8 * p + 8, :] = panels[p]
            else:
                inner_factors[n - count, 8 * p : 8 * p + 8, :] = panels[p]


def factor_local(leaf_grams, inner_grams):
    return pl.pallas_call(
        factor_kernel,
        in_specs=[pl.BlockSpec(memory_space=pltpu.VMEM)] * 2,
        out_shape=[
            jax.ShapeDtypeStruct(leaf_grams.shape, jnp.float32),
            jax.ShapeDtypeStruct(inner_grams.shape, jnp.float32),
        ],
        compiler_params=limit(4),
        name="factor_local",
    )(in_vmem(leaf_grams), in_vmem(inner_grams))


RING = ((0, 1, 2), (1, 2, 0))


def ring_swap(x, stage, flip, devices):
    pairs = [(d, d ^ flip << 1 + 2 * RING[d & 1][stage]) for d in range(devices)]
    return lax.ppermute(x, AXES, pairs)


def grid_places(device):
    first = (device >> 1 & 1) + 2 * (device >> 4 & 1)
    second = (device >> 2 & 1) + 2 * (device >> 5 & 1)
    third = (device & 1) + 2 * (device >> 3 & 1) + 4 * (device >> 6 & 1)
    return first, second, third


def grid_device(first, second, third):
    low = (third & 1) + 2 * (first & 1) + 4 * (second & 1) + 8 * (third >> 1 & 1)
    return low + 16 * (first >> 1) + 32 * (second >> 1) + 64 * (third >> 2)


def grid_swap(x, dim, shift, devices):
    pairs = []
    for d in range(devices):
        place = list(grid_places(d))
        to = place[dim] + (1 if place[dim] % 2 == shift else -1)
        if 0 <= to < (4, 4, 8)[dim]:
            place[dim] = to
        pairs.append((d, grid_device(*place)))
    return lax.ppermute(x, AXES, pairs)


def neighbours(lower, upper, dim, odd, devices):
    even_pairs = grid_swap(jnp.where(odd, lower, upper), dim, 0, devices)
    odd_pairs = grid_swap(jnp.where(odd, upper, lower), dim, 1, devices)
    return jnp.where(odd, even_pairs, odd_pairs), jnp.where(odd, odd_pairs, even_pairs)


def swap_cores(x, devices):
    return lax.ppermute(x, AXES, [(d, d ^ 1) for d in range(devices)])


def exchange_vectors(own, device, devices):
    first, second, _ = grid_places(device)
    left, right = neighbours(own[0::2], own[1::2], 0, first % 2 == 1, devices)
    rows = jnp.stack([left, own[0::2], own[1::2], right], axis=1)
    before, after = neighbours(rows[0], rows[1], 1, second % 2 == 1, devices)
    plane = jnp.concatenate([before, rows[0], rows[1], after])
    return [plane, swap_cores(plane, devices), grid_swap(plane, 2, 1, devices)]


def vector_slots(near_index, device):
    first, second, third = grid_places(device)
    cell = near_index
    x = (cell & 1) + 2 * (cell >> 3 & 1) + 4 * (cell >> 6 & 1) - 2 * first
    y = (cell >> 1 & 1) + 2 * (cell >> 4 & 1) + 4 * (cell >> 7 & 1) - 2 * second
    z = (cell >> 2 & 1) + 2 * (cell >> 5 & 1) + 4 * (cell >> 8 & 1)
    plane = jnp.where(z == third, 0, jnp.where(z >> 1 == third >> 1, 1, 2))
    return 16 * plane + 4 * (y + 1) + x + 1


def gather_weights(own, devices):
    held = own
    for stage in range(2):
        for flip in (1, 3):
            held = jnp.concatenate([held, ring_swap(held, stage, flip, devices)])
    near = ring_swap(held, 2, 1, devices)
    last = ring_swap(held, 2, 3, devices)
    return [held, near, last]


def gather_far(near, last, devices):
    half = near.shape[0] // 2
    return [ring_swap(last[:half], 2, 1, devices), ring_swap(near[half:], 2, 3, devices)]


def weight_tiles(adm_index, device):
    owner = adm_index >> 2
    label = []
    for axis in range(3):
        apart = (owner ^ device) >> 1 + 2 * axis & 3
        label.append(apart ^ apart >> 1)
    order = [
        label[RING[0][2]] * 16 + label[RING[0][1]] * 4 + label[RING[0][0]],
        label[RING[1][2]] * 16 + label[RING[1][1]] * 4 + label[RING[1][0]],
    ]
    core = owner & 1
    other = core ^ (device & 1)
    return other * 128 + 2 * jnp.where(core == 1, order[1], order[0]) + (adm_index >> 1 & 1)


def join_pieces(pieces, buffer):
    at = 0
    for piece in pieces:
        buffer[at : at + piece.shape[0]] = piece[...]
        at += piece.shape[0]


def limit(mebibytes):
    return pltpu.CompilerParams(vmem_limit_bytes=mebibytes << 20)


def near_kernel(slots, blocks, samples, basis, *rest):
    pieces, (gram, vectors) = rest[:3], rest[3:]
    join_pieces(pieces, vectors)
    for leaf in range(blocks.shape[0]):
        near_leaf(leaf, slots, blocks, samples, basis, vectors, gram)


def near_leaf(leaf, slots, blocks, samples, basis, vectors, gram):
    total = None
    for k in range(8):
        part = dot_last(vectors[slots[8 * leaf + k]], blocks[leaf, k])
        total = part if total is None else total + part
    far = (samples[leaf].astype(jnp.float32) - total).astype(jnp.bfloat16)
    scale = RANK**-0.5
    wide = dot_last(basis[leaf], far) * scale
    tall = dot_last(far, basis[leaf]) * scale
    wide_hi = wide.astype(jnp.bfloat16)
    wide_low = (wide - wide_hi.astype(jnp.float32)).astype(jnp.bfloat16)
    tall_hi = tall.astype(jnp.bfloat16)
    tall_low = (tall - tall_hi.astype(jnp.float32)).astype(jnp.bfloat16)
    gram[leaf] = dot32(tall_hi, wide_hi) + (dot32(tall_hi, wide_low) + dot32(tall_low, wide_hi))


def near_grams(slots, near_blocks, samples, leaf_basis, pieces):
    count, rank, size = samples.shape
    vmem = pl.BlockSpec(memory_space=pltpu.VMEM)
    return pl.pallas_call(
        near_kernel,
        in_specs=[pl.BlockSpec(memory_space=pltpu.SMEM)] + [vmem] * (3 + len(pieces)),
        out_specs=vmem,
        out_shape=pltpu.VMEM((count, rank, rank), jnp.float32),
        scratch_shapes=[pltpu.VMEM((48, rank, size), jnp.bfloat16)],
        compiler_params=limit(8),
        name="near_grams",
    )(
        slots,
        in_vmem(near_blocks),
        in_vmem(samples),
        in_vmem(leaf_basis),
        *[in_vmem(piece) for piece in pieces],
    )


def select_kernel(nodes, upper_transfer, transfers, semaphores):
    copies = [
        pltpu.make_async_copy(upper_transfer.at[nodes[n]], transfers.at[n], semaphores.at[n])
        for n in range(transfers.shape[0])
    ]
    for copy in copies:
        copy.start()
    for copy in copies:
        copy.wait()


def select_transfers(nodes, upper_transfer):
    levels, rank = nodes.shape[0], upper_transfer.shape[1]
    return pl.pallas_call(
        select_kernel,
        in_specs=[
            pl.BlockSpec(memory_space=pltpu.SMEM),
            pl.BlockSpec(memory_space=pl.ANY),
        ],
        out_specs=pl.BlockSpec(memory_space=pltpu.VMEM),
        out_shape=pltpu.VMEM((levels, rank, rank), jnp.bfloat16),
        scratch_shapes=[pltpu.SemaphoreType.DMA((levels,))],
        compiler_params=limit(4),
        name="select_transfers",
    )(nodes, upper_transfer)


def leaf_kernel(tiles, halves, coupling, near_gram, leaf_transfer, inner_transfer, *rest):
    pieces, (leaf_grams, inner_grams, sent, weights, coupled) = rest[:10], rest[10:]
    join_pieces(pieces, weights)
    unit = unit_matrix()
    moved = []
    for leaf in range(leaf_grams.shape[0]):
        sums = coupled_gram(leaf, tiles, halves, coupling, weights, coupled.at[leaf % 2])
        gram = near_gram[leaf] + sums * (1.0 / 2048) + unit
        leaf_grams[leaf] = gram
        moved.append(congruence(gram, leaf_transfer[leaf]))
    first = 0.5 * (moved[0] + moved[1]) + unit
    second = 0.5 * (moved[2] + moved[3]) + unit
    inner_grams[0] = first
    inner_grams[1] = second
    top = congruence(first, inner_transfer[0, 0]) + congruence(second, inner_transfer[0, 1])
    top = 0.5 * top + unit
    inner_grams[2] = top
    sent[...] = congruence(top, inner_transfer[0, 2])


def coupled_gram(leaf, tiles, halves, coupling, weights, coupled):
    side = lax.broadcasted_iota(jnp.int32, (RANK, 2 * RANK), 1) >> 6
    nothing = jnp.zeros((RANK, 2 * RANK), jnp.bfloat16)
    for pair in range(16):
        chosen = []
        for s in (2 * pair, 2 * pair + 1):
            tile = weights[tiles[32 * leaf + s]]
            chosen.append(jnp.where(side == halves[32 * leaf + s], tile, nothing))
        both = jnp.concatenate(
            [
                jnp.concatenate([chosen[0], nothing], axis=1),
                jnp.concatenate([nothing, chosen[1]], axis=1),
            ],
            axis=0,
        )
        product = dot32(coupling[leaf, :, 128 * pair : 128 * pair + 128], both).astype(jnp.bfloat16)
        coupled[128 * pair : 128 * pair + 64, :] = product[:, :128]
        coupled[128 * pair + 64 : 128 * pair + 128, :] = product[:, 128:]
    square = lax.dot_general(
        coupled[...], coupled[...], (((0,), (0,)), ((), ())), preferred_element_type=jnp.float32
    )
    return square[:RANK, :RANK] + square[RANK:, RANK:]


def leaf_levels(tiles, halves, coupling, near_gram, leaf_transfer, inner_transfer, pieces):
    count, rank, width = coupling.shape
    vmem = pl.BlockSpec(memory_space=pltpu.VMEM)
    inputs = [coupling, near_gram, leaf_transfer, inner_transfer] + list(pieces)
    return pl.pallas_call(
        leaf_kernel,
        in_specs=[pl.BlockSpec(memory_space=pltpu.SMEM)] * 2 + [vmem] * len(inputs),
        out_specs=[vmem] * 3,
        out_shape=[
            pltpu.VMEM((count, rank, rank), jnp.float32),
            pltpu.VMEM((count - 1, rank, rank), jnp.float32),
            pltpu.VMEM((rank, rank), jnp.float32),
        ],
        scratch_shapes=[
            pltpu.VMEM((256, rank, 2 * rank), jnp.bfloat16),
            pltpu.VMEM((2, width, 2 * rank), jnp.bfloat16),
        ],
        compiler_params=limit(12),
        name="leaf_levels",
    )(tiles, halves, *[in_vmem(x) for x in inputs])


def merge_kernel(level, own, other, transfers, gram, sent):
    merged = 0.5 * (own[...] + other[...]) + unit_matrix()
    gram[...] = merged
    sent[...] = congruence(merged, transfers[level])


def merge(level, own, other, transfers):
    return pl.pallas_call(
        functools.partial(merge_kernel, level),
        in_specs=[pl.BlockSpec(memory_space=pltpu.VMEM)] * 3,
        out_specs=[pl.BlockSpec(memory_space=pltpu.VMEM)] * 2,
        out_shape=[pltpu.VMEM((RANK, RANK), jnp.float32)] * 2,
        compiler_params=limit(4),
        name="merge",
    )(in_vmem(own), in_vmem(other), in_vmem(transfers))


def last_kernel(own, other, *rest):
    grams, factors = rest[:-1], rest[-1]
    merged = 0.5 * (own[...] + other[...]) + unit_matrix()
    out = factor_panels([panels_of(gram[...]) for gram in grams] + [panels_of(merged)])
    for n, panels in enumerate(out):
        for p in range(8):
            factors[n, 8 * p : 8 * p + 8, :] = panels[p]


def factor_upper(own, other, grams):
    count = len(grams) + 1
    return pl.pallas_call(
        last_kernel,
        in_specs=[pl.BlockSpec(memory_space=pltpu.VMEM)] * (count + 1),
        out_shape=jax.ShapeDtypeStruct((count, RANK, RANK), jnp.float32),
        compiler_params=limit(4),
        name="factor_upper",
    )(in_vmem(own), in_vmem(other), *[in_vmem(gram) for gram in grams])


def body(
    near_blocks,
    near_index,
    test_vectors,
    samples,
    leaf_basis,
    col_weights,
    coupling,
    adm_index,
    adm_count,
    leaf_transfer,
    inner_transfer,
    upper_transfer,
):
    count, rank, size = test_vectors.shape
    slots = adm_index.shape[1]
    devices = lax.axis_size("leaf") * lax.axis_size("near")
    total_levels = devices.bit_length() - 1
    device = lax.axis_index("leaf") * lax.axis_size("near") + lax.axis_index("near")
    paired = jnp.concatenate([col_weights[0::2], col_weights[1::2]], axis=2)
    weights = gather_weights(paired, devices)
    vectors = exchange_vectors(test_vectors, device, devices)
    levels = jnp.arange(1, total_levels)
    nodes = devices - (devices >> levels - 1) + (device >> levels)
    held, upper_transfer = lax.optimization_barrier((weights[0], upper_transfer))
    transfers = select_transfers(nodes, upper_transfer)
    live = jnp.arange(slots)[None, :] < adm_count[:, None]
    halves = jnp.where(live, adm_index & 1, 2).reshape(-1)
    tiles = weight_tiles(adm_index, device).reshape(-1)
    wanted = vector_slots(near_index, device).reshape(-1)
    near, last, transfers, halves, tiles, wanted = lax.optimization_barrier(
        (weights[1], weights[2], transfers, halves, tiles, wanted)
    )
    far = gather_far(near, last, devices)
    weights = [held, near, last]
    swapped = [swap_cores(piece, devices) for piece in weights]
    near_gram = near_grams(wanted, near_blocks, samples, leaf_basis, vectors)
    far_low, far_high, near_gram = lax.optimization_barrier((far[0], far[1], near_gram))
    far = [far_low, far_high]
    weights = weights + far + swapped + [swap_cores(piece, devices) for piece in far]
    gram, inner_grams, sent = leaf_levels(
        tiles,
        halves,
        coupling,
        near_gram,
        leaf_transfer,
        inner_transfer,
        weights,
    )
    grams = []
    for level in range(1, total_levels + 1):
        hop = HOPS[level - 1]
        other = lax.ppermute(sent, AXES, [(d, d ^ hop) for d in range(devices)])
        if level == 1:
            local_factors = factor_local(gram, inner_grams)
            other, local_factors = lax.optimization_barrier((other, local_factors))
        if level < total_levels:
            gram_here, sent = merge(level - 1, sent, other, transfers)
            grams.append(gram_here)
    upper_factors = factor_upper(sent, other, grams)
    leaf_factors, inner_factors = local_factors
    return (leaf_factors, inner_factors[None], upper_factors[None])


def solution(mesh):
    split = P(AXES)
    return jax.shard_map(
        body,
        mesh=mesh,
        in_specs=(split,) * 11 + (P(),),
        out_specs=(split,) * 3,
        check_vma=False,
    )
```

time: 215 us -> 108 us (0.50)
  waiting for transfers between devices: 95.6 us -> 31.9 us
  local copies, waits for them, and re-layouts: 41.5 us -> 11.1 us
  starting transfers between devices: 10.4 us -> 38.1 us
  between operations: 14.1 us -> 0.9 us
  matrix products: 11.3 us -> 0 us
  Pallas kernels: 33 us -> 23.4 us
  other arithmetic: 8.17 us -> 2.09 us
    all_gather x1 -> x0, waiting for transfers between devices: 85.8 us -> none  [body(): everything = lax.all_gather(packed, AXES, axis=0, tiled=True)]
    ppermute x0 -> x19, starting transfers between devices: none -> 27.1 us  [the longest x8 22.9 us: ring_swap(): return lax.ppermute(x, AXES, pairs)]
    slice x2 -> x3, local copies, waits for them, and re-layouts: 18.8 us -> 1.78 us  [the longest x1 0.97 us: gather_far(): last[:half]]
    ppermute x0 -> x19, waiting for transfers between devices: none -> 13.1 us  [the longest x8 11.3 us: ring_swap(): return lax.ppermute(x, AXES, pairs)]
    dot_general x4 -> x0, matrix products: 11.3 us -> none  [the longest x1 4.03 us: body(): jnp.einsum('irse,irsf->ief', coupled, coupled, precision=PRECISE)]
    gather x3 -> x0, local copies, waits for them, and re-layouts: 11.1 us -> none  [the longest x1 6.47 us: body(): neighbours = jnp.take(everything[:, :rank_size], near_index, axis=0)]
    pallas_call x12 -> x11, Pallas kernels: 33 us -> 23.4 us  [the longest x1 5.47 us: factor_upper(): pl.pallas_call(last_kernel, in_specs=[pl.BlockSpec(memory_space=pltpu.VME...]
    ppermute x7, waiting for transfers between devices: 9.74 us -> 18.8 us  [body(): other = lax.ppermute(sent, AXES, [(d, d ^ hop) for d in range(devices)])]
  transfers between devices with their start and end apart: 8 -> 26, of which waited for: 4 -> 15; matrix products, arithmetic and copies ran while one was open for 5% -> 9% of each run, Pallas kernels for 8% -> 10%
where the time goes in v3:
time: 108 us
  starting transfers between devices  38.1 us (35%)
  waiting for transfers between devices  31.9 us (30%)
  Pallas kernels  23.4 us (22%)
  local copies, waits for them, and re-layouts  11.1 us (10%)
  other arithmetic  2.09 us (2%)
    ppermute x8, starting transfers between devices, ring_swap(): return lax.ppermute(x, AXES, pairs)  22.9 us
    ppermute x7, waiting for transfers between devices, body(): other = lax.ppermute(sent, AXES, [(d, d ^ hop) for d in range(devices)])  18.8 us
    ppermute x8, waiting for transfers between devices, ring_swap(): return lax.ppermute(x, AXES, pairs)  11.3 us
    ppermute x7, starting transfers between devices, body(): other = lax.ppermute(sent, AXES, [(d, d ^ hop) for d in range(devices)])  10.9 us
    pallas_call x1, Pallas kernels, factor_upper(): pl.pallas_call(last_kernel, in_specs=[pl.BlockSpec(memory_space=pltpu.VME...  5.47 us
    pallas_call x1, Pallas kernels, factor_local(): pl.pallas_call(factor_kernel, in_specs=[pl.BlockSpec(memory_space=pltpu.V...  5.45 us
    pallas_call x1, Pallas kernels, leaf_levels(): pl.pallas_call(leaf_kernel, in_specs=[pl.BlockSpec(memory_space=pltpu.SME...  5.32 us
    pallas_call x1, Pallas kernels, near_grams(): pl.pallas_call(near_kernel, in_specs=[pl.BlockSpec(memory_space=pltpu.SME...  4.72 us
  transfers between devices with their start and end apart: 26, of which 15 were waited for; matrix products, arithmetic and copies ran while one was open for 9% of the time, Pallas kernels for 10%

profile of v3, /device:TPU:0, one launch (start us, length us, event | category | flops | bytes accessed | tf_op | source)
XLA Modules:
  0.0 107.5 jit_solution(17367473225095418140)
XLA Ops:
  0.7 0.8 fusion
  1.5 0.7 constant_dynamic-update-slice_fusion.4
  2.2 2.0 %collective-permute-start = (bf16[2,64,128]{2,1,0:T(8,128)(2,1)S(1)}, bf16[2,64,128]{2,1,0:T(8,128)(2,1)S(1)}, u32[]{:S(2)}, u32[]{:S(2)}) collective-permute-start(bf16[2,64,128]{2,1,0:T(8,128)(2,1)S(1)} %get-tuple-element.66), channel_id=1, source_target_pairs={{0,2},{1,9},{2,0},{3,11},{4,6},{5,13},{6,4},{7,15},{8,10},{9,1},{1... | collective-permute-start | bytes 98312 | tf_op jit(solution)/shard_map/ppermute | solution.py:119
  4.2 0.9 slice_bitcast_fusion.3
  5.1 0.1 collective-permute-start.8
  5.2 0.7 collective-permute-start.9
  5.9 0.2 collective-permute-done
  6.1 0.1 pad_maximum_fusion.4
  6.2 8.3 %collective-permute-start.1 = (bf16[4,64,128]{2,1,0:T(8,128)(2,1)S(1)}, bf16[4,64,128]{2,1,0:T(8,128)(2,1)S(1)}, u32[]{:S(2)}, u32[]{:S(2)}) collective-permute-start(bf16[4,64,128]{2,1,0:T(8,128)(2,1)S(1)} %pad_maximum_fusion.4), channel_id=1, source_target_pairs={{0,6},{1,25},{2,4},{3,27},{4,2},{5,29},{6,0},{7,31},{8,14},{9,17},... | collective-permute-start | bytes 196616 | tf_op jit(solution)/shard_map/ppermute | solution.py:119
  14.4 0.6 constant_dynamic-update-slice_fusion.3
  15.2 1.5 %collective-permute-done.1 = bf16[4,64,128]{2,1,0:T(8,128)(2,1)S(1)} collective-permute-done((bf16[4,64,128]{2,1,0:T(8,128)(2,1)S(1)}, bf16[4,64,128]{2,1,0:T(8,128)(2,1)S(1)}, u32[]{:S(2)}, u32[]{:S(2)}) %collective-permute-start.1) | collective-permute-done | bytes 65568 | tf_op jit(solution)/shard_map/ppermute | solution.py:119
  16.7 0.1 pad_maximum_fusion.3
  16.8 0.8 collective-permute-start.2
  17.6 0.1 collective-permute-start.10
  17.7 0.7 collective-permute-start.11
  18.3 0.6 constant_dynamic-update-slice_fusion.2
  19.0 2.9 %collective-permute-done.2 = bf16[8,64,128]{2,1,0:T(8,128)(2,1)S(1)} collective-permute-done((bf16[8,64,128]{2,1,0:T(8,128)(2,1)S(1)}, bf16[8,64,128]{2,1,0:T(8,128)(2,1)S(1)}, u32[]{:S(2)}, u32[]{:S(2)}) %collective-permute-start.2) | collective-permute-done | bytes 131104 | tf_op jit(solution)/shard_map/ppermute | solution.py:119
  21.9 1.8 %collective-permute-start.3 = (bf16[16,64,128]{2,1,0:T(8,128)(2,1)S(1)}, bf16[16,64,128]{2,1,0:T(8,128)(2,1)S(1)}, u32[]{:S(2)}, u32[]{:S(2)}) collective-permute-start(bf16[16,64,128]{2,1,0:T(8,128)(2,1)S(1)} %pad_maximum_fusion.1), channel_id=1, source_target_pairs={{0,24},{1,97},{2,26},{3,99},{4,28},{5,101},{6,30},{7,103},{8,16},{... | collective-permute-start | bytes 786440 | tf_op jit(solution)/shard_map/ppermute | solution.py:119
  23.8 0.4 collective-permute-done.10
  24.2 0.1 collective-permute-start.12
  24.3 1.5 %collective-permute-start.13 = (bf16[16,64,256]{2,1,0:T(8,128)(2,1)S(1)}, bf16[16,64,256]{2,1,0:T(8,128)(2,1)}, u32[]{:S(2)}, u32[]{:S(2)}) collective-permute-start(bf16[16,64,256]{2,1,0:T(8,128)(2,1)S(1)} %pad_maximum_fusion.rest_0_), channel_id=1, source_target_pairs={{0,0},{1,8},{2,2},{3,10},{4,4},{5,12},{6,6},{7,14},{8,1},{9,64},{1... | collective-permute-start | bytes 1572872 | tf_op jit(solution)/shard_map/ppermute | solution.py:142
  25.8 0.7 constant_dynamic-update-slice_fusion.1
  26.5 3.1 %collective-permute-done.3 = bf16[16,64,128]{2,1,0:T(8,128)(2,1)S(1)} collective-permute-done((bf16[16,64,128]{2,1,0:T(8,128)(2,1)S(1)}, bf16[16,64,128]{2,1,0:T(8,128)(2,1)S(1)}, u32[]{:S(2)}, u32[]{:S(2)}) %collective-permute-start.3) | collective-permute-done | bytes 262176 | tf_op jit(solution)/shard_map/ppermute | solution.py:119
  29.6 0.7 constant_dynamic-update-slice_fusion.rest_0_
  30.3 3.3 %collective-permute-start.4 = (bf16[32,64,128]{2,1,0:T(8,128)(2,1)}, bf16[32,64,128]{2,1,0:T(8,128)(2,1)S(1)}, u32[]{:S(2)}, u32[]{:S(2)}) collective-permute-start(bf16[32,64,128]{2,1,0:T(8,128)(2,1)} %constant_dynamic-update-slice_fusion.rest_0_), channel_id=1, source_target_pairs={{0,32},{1,3},{2,34},{3,1},{4,36},{5,7},{6,38},{7,5},{8,40},{9,11},... | collective-permute-start | bytes 1572872 | tf_op jit(solution)/shard_map/ppermute | solution.py:119
  33.6 1.9 %collective-permute-start.5 = (bf16[32,64,128]{2,1,0:T(8,128)(2,1)}, bf16[32,64,128]{2,1,0:T(8,128)(2,1)}, u32[]{:S(2)}, u32[]{:S(2)}) collective-permute-start(bf16[32,64,128]{2,1,0:T(8,128)(2,1)} %constant_dynamic-update-slice_fusion.rest_0_), channel_id=1, source_target_pairs={{0,96},{1,7},{2,98},{3,5},{4,100},{5,3},{6,102},{7,1},{8,104},{9,1... | collective-permute-start | bytes 1572872 | tf_op jit(solution)/shard_map/ppermute | solution.py:119
  35.5 0.1 reshape.18.slots
  35.7 0.1 reshape.16.halves
  35.8 4.2 %copy.15.upper_transfer = bf16[126,64,64]{2,1,0:T(8,128)(2,1)S(1)} copy(bf16[126,64,64]{0,2,1:T(8,128)(2,1)} %param.23) | data formatting | bytes 2064384 | tf_op jit(solution)/shard_map/optimization_barrier | solution.py:412
  40.0 0.7 select_transfers.1.transfers
  40.8 0.2 collective-permute-done.4.rest_1_
  41.0 3.3 %collective-permute-done.5.rest_2_ = bf16[32,64,128]{2,1,0:T(8,128)(2,1)} collective-permute-done((bf16[32,64,128]{2,1,0:T(8,128)(2,1)}, bf16[32,64,128]{2,1,0:T(8,128)(2,1)}, u32[]{:S(2)}, u32[]{:S(2)}) %collective-permute-start.5) | collective-permute-done | bytes 524320 | tf_op jit(solution)/shard_map/ppermute | solution.py:119
  44.3 1.0 slice.30
  45.3 3.6 %collective-permute-start.6 = (bf16[16,64,128]{2,1,0:T(8,128)(2,1)S(1)}, bf16[16,64,128]{2,1,0:T(8,128)(2,1)S(1)}, u32[]{:S(2)}, u32[]{:S(2)}) collective-permute-start(bf16[16,64,128]{2,1,0:T(8,128)(2,1)S(1)} %slice.30), channel_id=1, source_target_pairs={{0,32},{1,3},{2,34},{3,1},{4,36},{5,7},{6,38},{7,5},{8,40},{9,11},... | collective-permute-start | bytes 786440 | tf_op jit(solution)/shard_map/ppermute | solution.py:119
  48.9 1.2 %collective-permute-start.7 = (bf16[16,64,128]{2,1,0:T(8,128)(2,1)S(1)}, bf16[16,64,128]{2,1,0:T(8,128)(2,1)S(1)}, u32[]{:S(2)}, u32[]{:S(2)}) collective-permute-start(bf16[16,64,128]{2,1,0:T(8,128)(2,1)S(1)} %slice.31), channel_id=1, source_target_pairs={{0,96},{1,7},{2,98},{3,5},{4,100},{5,3},{6,102},{7,1},{8,104},{9,1... | collective-permute-start | bytes 786440 | tf_op jit(solution)/shard_map/ppermute | solution.py:119
  50.1 0.5 collective-permute-start.15
  50.6 0.1 collective-permute-start.16
  50.7 2.2 %copy-done = bf16[4,8,256,256]{3,2,1,0:T(8,128)(2,1)S(1)} copy-done((bf16[4,8,256,256]{3,2,1,0:T(8,128)(2,1)S(1)}, bf16[4,8,256,256]{3,2,1,0:T(8,128)(2,1)}, u32[]{:S(2)}) %copy-start) | copy-done | bytes 4194328
  52.9 4.7 %near_grams.1.near_gram = f32[4,64,64]{2,1,0:T(8,128)S(1)} custom-call(s32[32]{0:T(128)S(1)} %reshape.18.slots, bf16[4,8,256,256]{3,2,1,0:T(8,128)(2,1)S(1)} %copy-done, bf16[4,64,256]{2,1,0:T(8,128)(2,1)S(1)} %copy-done.2, bf16[4,64,256]{2,1,0:T(8,128)(2,1)S(1)} %copy-done.3, bf16[16,64,256]{2,1,0:T(8,128)(2,1)S(1)} %pad_maximum_fusion.rest_0_, ...), custom_call_target="tpu_custom_call" | custom-call | tf_op jit(solution)/shard_map/near_grams/pallas_call | solution.py:241
  57.7 0.5 collective-permute-start.17
  58.2 0.1 collective-permute-start.18
  58.3 1.1 collective-permute-done.17.rest_8_
  59.3 0.4 collective-permute-done.18.rest_9_
  59.7 5.3 %leaf_levels.1 = (f32[4,64,64]{2,1,0:T(8,128)S(1)}, f32[3,64,64]{2,1,0:T(8,128)S(1)}, f32[64,64]{1,0:T(8,128)S(1)}) custom-call(s32[128]{0:T(128)S(1)} %reshape.17.tiles, s32[128]{0:T(128)S(1)} %reshape.16.halves, bf16[4,64,2048]{2,1,0:T(8,128)(2,1)S(1)} %copy-done.1, f32[4,64,64]{2,1,0:T(8,128)S(1)} %near_grams.1.near_gram, ...), custom_call_target="tpu_custom_call" | custom-call | tf_op jit(solution)/shard_map/leaf_levels/pallas_call | solution.py:333
  65.1 0.5 collective-permute-start.19
  65.6 5.4 %factor_local.1 = (f32[4,64,64]{2,1,0:T(8,128)}, f32[3,64,64]{2,1,0:T(8,128)}) custom-call(f32[4,64,64]{2,1,0:T(8,128)S(1)} %get-tuple-element.45.leaf_grams, f32[3,64,64]{2,1,0:T(8,128)S(1)} %get-tuple-element.46.inner_grams), custom_call_target="tpu_custom_call" | custom-call | tf_op jit(solution)/shard_map/factor_local/pallas_call | solution.py:102
  71.0 0.3 merge.6
  71.3 4.1 %collective-permute-start.20 = (f32[64,64]{1,0:T(8,128)S(1)}, f32[64,64]{1,0:T(8,128)S(1)}, u32[]{:S(2)}, u32[]{:S(2)}) collective-permute-start(f32[64,64]{1,0:T(8,128)S(1)} %get-tuple-element.53.own), channel_id=1, source_target_pairs={{0,2},{1,3},{2,0},{3,1},{4,6},{5,7},{6,4},{7,5},{8,10},{9,11},{10,... | collective-permute-start | bytes 49160 | tf_op jit(solution)/shard_map/ppermute | solution.py:440
  75.4 1.9 %collective-permute-done.20.other = f32[64,64]{1,0:T(8,128)S(1)} collective-permute-done((f32[64,64]{1,0:T(8,128)S(1)}, f32[64,64]{1,0:T(8,128)S(1)}, u32[]{:S(2)}, u32[]{:S(2)}) %collective-permute-start.20) | collective-permute-done | bytes 16416 | tf_op jit(solution)/shard_map/ppermute | solution.py:440
  77.3 0.3 merge.7
  77.6 5.1 %collective-permute-done.21.other = f32[64,64]{1,0:T(8,128)S(1)} collective-permute-done((f32[64,64]{1,0:T(8,128)S(1)}, f32[64,64]{1,0:T(8,128)S(1)}, u32[]{:S(2)}, u32[]{:S(2)}) %collective-permute-start.21) | collective-permute-done | bytes 16416 | tf_op jit(solution)/shard_map/ppermute | solution.py:440
  82.7 0.3 merge.8
  83.0 1.1 %collective-permute-start.22 = (f32[64,64]{1,0:T(8,128)S(1)}, f32[64,64]{1,0:T(8,128)S(1)}, u32[]{:S(2)}, u32[]{:S(2)}) collective-permute-start(f32[64,64]{1,0:T(8,128)S(1)} %get-tuple-element.55.own), channel_id=1, source_target_pairs={{0,8},{1,9},{2,10},{3,11},{4,12},{5,13},{6,14},{7,15},{8,0},{9,1},... | collective-permute-start | bytes 49160 | tf_op jit(solution)/shard_map/ppermute | solution.py:440
  84.1 2.9 %collective-permute-done.22.other = f32[64,64]{1,0:T(8,128)S(1)} collective-permute-done((f32[64,64]{1,0:T(8,128)S(1)}, f32[64,64]{1,0:T(8,128)S(1)}, u32[]{:S(2)}, u32[]{:S(2)}) %collective-permute-start.22) | collective-permute-done | bytes 16416 | tf_op jit(solution)/shard_map/ppermute | solution.py:440
  87.0 0.3 merge.9
  87.2 2.5 %collective-permute-start.23 = (f32[64,64]{1,0:T(8,128)S(1)}, f32[64,64]{1,0:T(8,128)S(1)}, u32[]{:S(2)}, u32[]{:S(2)}) collective-permute-start(f32[64,64]{1,0:T(8,128)S(1)} %get-tuple-element.56.own), channel_id=1, source_target_pairs={{0,24},{1,25},{2,26},{3,27},{4,28},{5,29},{6,30},{7,31},{8,16},{9,... | collective-permute-start | bytes 49160 | tf_op jit(solution)/shard_map/ppermute | solution.py:440
  89.7 2.7 %collective-permute-done.23.other = f32[64,64]{1,0:T(8,128)S(1)} collective-permute-done((f32[64,64]{1,0:T(8,128)S(1)}, f32[64,64]{1,0:T(8,128)S(1)}, u32[]{:S(2)}, u32[]{:S(2)}) %collective-permute-start.23) | collective-permute-done | bytes 16416 | tf_op jit(solution)/shard_map/ppermute | solution.py:440
  92.4 0.3 merge.10
  92.7 0.6 collective-permute-start.24
  93.3 3.3 %collective-permute-done.24.other = f32[64,64]{1,0:T(8,128)S(1)} collective-permute-done((f32[64,64]{1,0:T(8,128)S(1)}, f32[64,64]{1,0:T(8,128)S(1)}, u32[]{:S(2)}, u32[]{:S(2)}) %collective-permute-start.24) | collective-permute-done | bytes 16416 | tf_op jit(solution)/shard_map/ppermute | solution.py:440
  96.6 0.3 merge.11
  96.9 2.1 %collective-permute-start.25 = (f32[64,64]{1,0:T(8,128)S(1)}, f32[64,64]{1,0:T(8,128)S(1)}, u32[]{:S(2)}, u32[]{:S(2)}) collective-permute-start(f32[64,64]{1,0:T(8,128)S(1)} %get-tuple-element.58.own), channel_id=1, source_target_pairs={{0,96},{1,97},{2,98},{3,99},{4,100},{5,101},{6,102},{7,103},{8,104... | collective-permute-start | bytes 49160 | tf_op jit(solution)/shard_map/ppermute | solution.py:440
  99.0 3.0 %collective-permute-done.25.other = f32[64,64]{1,0:T(8,128)S(1)} collective-permute-done((f32[64,64]{1,0:T(8,128)S(1)}, f32[64,64]{1,0:T(8,128)S(1)}, u32[]{:S(2)}, u32[]{:S(2)}) %collective-permute-start.25) | collective-permute-done | bytes 16416 | tf_op jit(solution)/shard_map/ppermute | solution.py:440
  102.0 5.5 %factor_upper.1 = f32[7,64,64]{2,1,0:T(8,128)} custom-call(f32[64,64]{1,0:T(8,128)S(1)} %get-tuple-element.58.own, f32[64,64]{1,0:T(8,128)S(1)} %collective-permute-done.25.other, f32[64,64]{1,0:T(8,128)S(1)} %get-tuple-element.59.rest_0_, f32[64,64]{1,0:T(8,128)S(1)} %get-tuple-element.60.rest_1_, f32[64,64]{1,0:T(8,128)S(1)} %get-tuple-element.61.rest_2_, ...), custom_call_target="tpu_custom_call" | custom-call | tf_op jit(solution)/shard_map/factor_upper/pallas_call | solution.py:379
  (42 shorter events, 0.5 us)
Async XLA Ops:
  0.6 34.9 %copy-start.6 = (s32[4,8]{1,0:T(4,128)S(1)}, s32[4,8]{1,0:T(4,128)}, u32[]{:S(2)}) copy-start(s32[4,8]{1,0:T(4,128)} %param.13) | copy-start | bytes 388
  0.6 35.0 %copy-start.7 = (s32[4,32]{1,0:T(4,128)S(1)}, s32[4,32]{1,0:T(4,128)}, u32[]{:S(2)}) copy-start(s32[4,32]{1,0:T(4,128)} %param.19) | copy-start | bytes 1540
  0.7 35.0 %copy-start.8 = (s32[4]{0:T(128)S(1)}, s32[4]{0:T(128)}, u32[]{:S(2)}) copy-start(s32[4]{0:T(128)} %param.20) | copy-start | bytes 52
  2.2 3.9 %collective-permute-start = (bf16[2,64,128]{2,1,0:T(8,128)(2,1)S(1)}, bf16[2,64,128]{2,1,0:T(8,128)(2,1)S(1)}, u32[]{:S(2)}, u32[]{:S(2)}) collective-permute-start(bf16[2,64,128]{2,1,0:T(8,128)(2,1)S(1)} %get-tuple-element.66), channel_id=1, source_target_pairs={{0,2},{1,9},{2,0},{3,11},{4,6},{5,13},{6,4},{7,15},{8,10},{9,1},{1... | collective-permute-start | bytes 98312 | tf_op jit(solution)/shard_map/ppermute | solution.py:119
  5.1 10.0 %collective-permute-start.8 = (bf16[2,64,256]{2,1,0:T(8,128)(2,1)S(1)}, bf16[2,64,256]{2,1,0:T(8,128)(2,1)S(1)}, u32[]{:S(2)}, u32[]{:S(2)}) collective-permute-start(bf16[2,64,256]{2,1,0:T(8,128)(2,1)S(1)} %get-tuple-element.78), channel_id=1, source_target_pairs={{0,2},{1,3},{2,0},{3,1},{4,6},{5,7},{6,4},{7,5},{8,10},{9,11},{10,... | collective-permute-start | bytes 196616 | tf_op jit(solution)/shard_map/ppermute | solution.py:142
  5.2 9.9 %collective-permute-start.9 = (bf16[2,64,256]{2,1,0:T(8,128)(2,1)S(1)}, bf16[2,64,256]{2,1,0:T(8,128)(2,1)S(1)}, u32[]{:S(2)}, u32[]{:S(2)}) collective-permute-start(bf16[2,64,256]{2,1,0:T(8,128)(2,1)S(1)} %get-tuple-element.76), channel_id=1, source_target_pairs={{0,0},{1,1},{2,16},{3,17},{4,4},{5,5},{6,20},{7,21},{8,8},{9,9},{1... | collective-permute-start | bytes 196616 | tf_op jit(solution)/shard_map/ppermute | solution.py:142
  6.2 10.5 %collective-permute-start.1 = (bf16[4,64,128]{2,1,0:T(8,128)(2,1)S(1)}, bf16[4,64,128]{2,1,0:T(8,128)(2,1)S(1)}, u32[]{:S(2)}, u32[]{:S(2)}) collective-permute-start(bf16[4,64,128]{2,1,0:T(8,128)(2,1)S(1)} %pad_maximum_fusion.4), channel_id=1, source_target_pairs={{0,6},{1,25},{2,4},{3,27},{4,2},{5,29},{6,0},{7,31},{8,14},{9,17},... | collective-permute-start | bytes 196616 | tf_op jit(solution)/shard_map/ppermute | solution.py:119
  16.8 5.0 %collective-permute-start.2 = (bf16[8,64,128]{2,1,0:T(8,128)(2,1)S(1)}, bf16[8,64,128]{2,1,0:T(8,128)(2,1)S(1)}, u32[]{:S(2)}, u32[]{:S(2)}) collective-permute-start(bf16[8,64,128]{2,1,0:T(8,128)(2,1)S(1)} %pad_maximum_fusion.3), channel_id=1, source_target_pairs={{0,8},{1,33},{2,10},{3,35},{4,12},{5,37},{6,14},{7,39},{8,0},{9,41... | collective-permute-start | bytes 393224 | tf_op jit(solution)/shard_map/ppermute | solution.py:119
  17.6 6.6 %collective-permute-start.10 = (bf16[4,64,256]{2,1,0:T(8,128)(2,1)S(1)}, bf16[4,64,256]{2,1,0:T(8,128)(2,1)S(1)}, u32[]{:S(2)}, u32[]{:S(2)}) collective-permute-start(bf16[4,64,256]{2,1,0:T(8,128)(2,1)S(1)} %get-tuple-element.71), channel_id=1, source_target_pairs={{0,4},{1,5},{2,6},{3,7},{4,0},{5,1},{6,2},{7,3},{8,12},{9,13},{10,... | collective-permute-start | bytes 393224 | tf_op jit(solution)/shard_map/ppermute | solution.py:142
  17.7 6.5 %collective-permute-start.11 = (bf16[4,64,256]{2,1,0:T(8,128)(2,1)S(1)}, bf16[4,64,256]{2,1,0:T(8,128)(2,1)S(1)}, u32[]{:S(2)}, u32[]{:S(2)}) collective-permute-start(bf16[4,64,256]{2,1,0:T(8,128)(2,1)S(1)} %get-tuple-element.72), channel_id=1, source_target_pairs={{0,0},{1,1},{2,2},{3,3},{4,32},{5,33},{6,34},{7,35},{8,8},{9,9},{1... | collective-permute-start | bytes 393224 | tf_op jit(solution)/shard_map/ppermute | solution.py:142
  21.9 7.7 %collective-permute-start.3 = (bf16[16,64,128]{2,1,0:T(8,128)(2,1)S(1)}, bf16[16,64,128]{2,1,0:T(8,128)(2,1)S(1)}, u32[]{:S(2)}, u32[]{:S(2)}) collective-permute-start(bf16[16,64,128]{2,1,0:T(8,128)(2,1)S(1)} %pad_maximum_fusion.1), channel_id=1, source_target_pairs={{0,24},{1,97},{2,26},{3,99},{4,28},{5,101},{6,30},{7,103},{8,16},{... | collective-permute-start | bytes 786440 | tf_op jit(solution)/shard_map/ppermute | solution.py:119
  24.1 26.6 %copy-start.2 = (bf16[4,64,256]{2,1,0:T(8,128)(2,1)S(1)}, bf16[4,64,256]{2,1,0:T(8,128)(2,1)}, u32[]{:S(2)}) copy-start(bf16[4,64,256]{2,1,0:T(8,128)(2,1)} %samples.1) | copy-start | bytes 393220
  24.2 26.6 %copy-start.3 = (bf16[4,64,256]{2,1,0:T(8,128)(2,1)S(1)}, bf16[4,64,256]{2,1,0:T(8,128)(2,1)}, u32[]{:S(2)}) copy-start(bf16[4,64,256]{2,1,0:T(8,128)(2,1)} %basis.1) | copy-start | bytes 393220
  24.2 25.9 %collective-permute-start.12 = (bf16[16,64,256]{2,1,0:T(8,128)(2,1)S(1)}, bf16[16,64,256]{2,1,0:T(8,128)(2,1)}, u32[]{:S(2)}, u32[]{:S(2)}) collective-permute-start(bf16[16,64,256]{2,1,0:T(8,128)(2,1)S(1)} %pad_maximum_fusion.rest_0_), channel_id=1, source_target_pairs={{0,1},{1,0},{2,3},{3,2},{4,5},{5,4},{6,7},{7,6},{8,9},{9,8},{10,11... | collective-permute-start | bytes 1572872 | tf_op jit(solution)/shard_map/ppermute | solution.py:152
  24.3 26.3 %collective-permute-start.13 = (bf16[16,64,256]{2,1,0:T(8,128)(2,1)S(1)}, bf16[16,64,256]{2,1,0:T(8,128)(2,1)}, u32[]{:S(2)}, u32[]{:S(2)}) collective-permute-start(bf16[16,64,256]{2,1,0:T(8,128)(2,1)S(1)} %pad_maximum_fusion.rest_0_), channel_id=1, source_target_pairs={{0,0},{1,8},{2,2},{3,10},{4,4},{5,12},{6,6},{7,14},{8,1},{9,64},{1... | collective-permute-start | bytes 1572872 | tf_op jit(solution)/shard_map/ppermute | solution.py:142
  30.3 10.7 %collective-permute-start.4 = (bf16[32,64,128]{2,1,0:T(8,128)(2,1)}, bf16[32,64,128]{2,1,0:T(8,128)(2,1)S(1)}, u32[]{:S(2)}, u32[]{:S(2)}) collective-permute-start(bf16[32,64,128]{2,1,0:T(8,128)(2,1)} %constant_dynamic-update-slice_fusion.rest_0_), channel_id=1, source_target_pairs={{0,32},{1,3},{2,34},{3,1},{4,36},{5,7},{6,38},{7,5},{8,40},{9,11},... | collective-permute-start | bytes 1572872 | tf_op jit(solution)/shard_map/ppermute | solution.py:119
  33.6 10.7 %collective-permute-start.5 = (bf16[32,64,128]{2,1,0:T(8,128)(2,1)}, bf16[32,64,128]{2,1,0:T(8,128)(2,1)}, u32[]{:S(2)}, u32[]{:S(2)}) collective-permute-start(bf16[32,64,128]{2,1,0:T(8,128)(2,1)} %constant_dynamic-update-slice_fusion.rest_0_), channel_id=1, source_target_pairs={{0,96},{1,7},{2,98},{3,5},{4,100},{5,3},{6,102},{7,1},{8,104},{9,1... | collective-permute-start | bytes 1572872 | tf_op jit(solution)/shard_map/ppermute | solution.py:119
  40.0 19.7 %copy-start.1 = (bf16[4,64,2048]{2,1,0:T(8,128)(2,1)S(1)}, bf16[4,64,2048]{2,1,0:T(8,128)(2,1)}, u32[]{:S(2)}) copy-start(bf16[4,64,2048]{2,1,0:T(8,128)(2,1)} %coupling.1) | copy-start | bytes 3145732
  40.0 19.7 %copy-start.4 = (bf16[4,64,64]{2,1,0:T(8,128)(2,1)S(1)}, bf16[4,64,64]{2,1,0:T(8,128)(2,1)}, u32[]{:S(2)}) copy-start(bf16[4,64,64]{2,1,0:T(8,128)(2,1)} %leaf_transfer.1) | copy-start | bytes 98308
  40.0 19.7 %copy-start.5 = (bf16[1,3,64,64]{3,2,1,0:T(8,128)(2,1)S(1)}, bf16[1,3,64,64]{3,2,1,0:T(8,128)(2,1)}, u32[]{:S(2)}) copy-start(bf16[1,3,64,64]{3,2,1,0:T(8,128)(2,1)} %inner_transfer.1) | copy-start | bytes 73732
  45.3 12.3 %collective-permute-start.6 = (bf16[16,64,128]{2,1,0:T(8,128)(2,1)S(1)}, bf16[16,64,128]{2,1,0:T(8,128)(2,1)S(1)}, u32[]{:S(2)}, u32[]{:S(2)}) collective-permute-start(bf16[16,64,128]{2,1,0:T(8,128)(2,1)S(1)} %slice.30), channel_id=1, source_target_pairs={{0,32},{1,3},{2,34},{3,1},{4,36},{5,7},{6,38},{7,5},{8,40},{9,11},... | collective-permute-start | bytes 786440 | tf_op jit(solution)/shard_map/ppermute | solution.py:119
  48.9 8.7 %collective-permute-start.7 = (bf16[16,64,128]{2,1,0:T(8,128)(2,1)S(1)}, bf16[16,64,128]{2,1,0:T(8,128)(2,1)S(1)}, u32[]{:S(2)}, u32[]{:S(2)}) collective-permute-start(bf16[16,64,128]{2,1,0:T(8,128)(2,1)S(1)} %slice.31), channel_id=1, source_target_pairs={{0,96},{1,7},{2,98},{3,5},{4,100},{5,3},{6,102},{7,1},{8,104},{9,1... | collective-permute-start | bytes 786440 | tf_op jit(solution)/shard_map/ppermute | solution.py:119
  50.1 8.2 %collective-permute-start.14 = (bf16[32,64,128]{2,1,0:T(8,128)(2,1)}, bf16[32,64,128]{2,1,0:T(8,128)(2,1)S(1)}, u32[]{:S(2)}, u32[]{:S(2)}) collective-permute-start(bf16[32,64,128]{2,1,0:T(8,128)(2,1)} %constant_dynamic-update-slice_fusion.rest_0_), channel_id=1, source_target_pairs={{0,1},{1,0},{2,3},{3,2},{4,5},{5,4},{6,7},{7,6},{8,9},{9,8},{10,11... | collective-permute-start | bytes 1572872 | tf_op jit(solution)/shard_map/ppermute | solution.py:152
  50.1 9.6 %collective-permute-start.15 = (bf16[32,64,128]{2,1,0:T(8,128)(2,1)S(1)}, bf16[32,64,128]{2,1,0:T(8,128)(2,1)S(1)}, u32[]{:S(2)}, u32[]{:S(2)}) collective-permute-start(bf16[32,64,128]{2,1,0:T(8,128)(2,1)S(1)} %collective-permute-done.4.rest_1_), channel_id=1, source_target_pairs={{0,1},{1,0},{2,3},{3,2},{4,5},{5,4},{6,7},{7,6},{8,9},{9,8},{10,11... | collective-permute-start | bytes 1572872 | tf_op jit(solution)/shard_map/ppermute | solution.py:152
  50.6 9.1 %collective-permute-start.16 = (bf16[32,64,128]{2,1,0:T(8,128)(2,1)}, bf16[32,64,128]{2,1,0:T(8,128)(2,1)S(1)}, u32[]{:S(2)}, u32[]{:S(2)}) collective-permute-start(bf16[32,64,128]{2,1,0:T(8,128)(2,1)} %collective-permute-done.5.rest_2_), channel_id=1, source_target_pairs={{0,1},{1,0},{2,3},{3,2},{4,5},{5,4},{6,7},{7,6},{8,9},{9,8},{10,11... | collective-permute-start | bytes 1572872 | tf_op jit(solution)/shard_map/ppermute | solution.py:152
  50.7 2.2 %copy-start = (bf16[4,8,256,256]{3,2,1,0:T(8,128)(2,1)S(1)}, bf16[4,8,256,256]{3,2,1,0:T(8,128)(2,1)}, u32[]{:S(2)}) copy-start(bf16[4,8,256,256]{3,2,1,0:T(8,128)(2,1)} %blocks.1) | copy-start | bytes 12582916
  57.7 1.7 %collective-permute-start.17 = (bf16[16,64,128]{2,1,0:T(8,128)(2,1)S(1)}, bf16[16,64,128]{2,1,0:T(8,128)(2,1)S(1)}, u32[]{:S(2)}, u32[]{:S(2)}) collective-permute-start(bf16[16,64,128]{2,1,0:T(8,128)(2,1)S(1)} %collective-permute-done.6.rest_3_), channel_id=1, source_target_pairs={{0,1},{1,0},{2,3},{3,2},{4,5},{5,4},{6,7},{7,6},{8,9},{9,8},{10,11... | collective-permute-start | bytes 786440 | tf_op jit(solution)/shard_map/ppermute | solution.py:152
  58.2 1.5 %collective-permute-start.18 = (bf16[16,64,128]{2,1,0:T(8,128)(2,1)S(1)}, bf16[16,64,128]{2,1,0:T(8,128)(2,1)S(1)}, u32[]{:S(2)}, u32[]{:S(2)}) collective-permute-start(bf16[16,64,128]{2,1,0:T(8,128)(2,1)S(1)} %collective-permute-done.7.rest_4_), channel_id=1, source_target_pairs={{0,1},{1,0},{2,3},{3,2},{4,5},{5,4},{6,7},{7,6},{8,9},{9,8},{10,11... | collective-permute-start | bytes 786440 | tf_op jit(solution)/shard_map/ppermute | solution.py:152
  65.1 6.0 %collective-permute-start.19 = (f32[64,64]{1,0:T(8,128)S(1)}, f32[64,64]{1,0:T(8,128)S(1)}, u32[]{:S(2)}, u32[]{:S(2)}) collective-permute-start(f32[64,64]{1,0:T(8,128)S(1)} %get-tuple-element.44.own), channel_id=1, source_target_pairs={{0,1},{1,0},{2,3},{3,2},{4,5},{5,4},{6,7},{7,6},{8,9},{9,8},{10,11... | collective-permute-start | bytes 49160 | tf_op jit(solution)/shard_map/ppermute | solution.py:440
  71.3 6.0 %collective-permute-start.20 = (f32[64,64]{1,0:T(8,128)S(1)}, f32[64,64]{1,0:T(8,128)S(1)}, u32[]{:S(2)}, u32[]{:S(2)}) collective-permute-start(f32[64,64]{1,0:T(8,128)S(1)} %get-tuple-element.53.own), channel_id=1, source_target_pairs={{0,2},{1,3},{2,0},{3,1},{4,6},{5,7},{6,4},{7,5},{8,10},{9,11},{10,... | collective-permute-start | bytes 49160 | tf_op jit(solution)/shard_map/ppermute | solution.py:440
  77.6 5.1 %collective-permute-start.21 = (f32[64,64]{1,0:T(8,128)S(1)}, f32[64,64]{1,0:T(8,128)S(1)}, u32[]{:S(2)}, u32[]{:S(2)}) collective-permute-start(f32[64,64]{1,0:T(8,128)S(1)} %get-tuple-element.54.own), channel_id=1, source_target_pairs={{0,6},{1,7},{2,4},{3,5},{4,2},{5,3},{6,0},{7,1},{8,14},{9,15},{10,... | collective-permute-start | bytes 49160 | tf_op jit(solution)/shard_map/ppermute | solution.py:440
  83.0 3.9 %collective-permute-start.22 = (f32[64,64]{1,0:T(8,128)S(1)}, f32[64,64]{1,0:T(8,128)S(1)}, u32[]{:S(2)}, u32[]{:S(2)}) collective-permute-start(f32[64,64]{1,0:T(8,128)S(1)} %get-tuple-element.55.own), channel_id=1, source_target_pairs={{0,8},{1,9},{2,10},{3,11},{4,12},{5,13},{6,14},{7,15},{8,0},{9,1},... | collective-permute-start | bytes 49160 | tf_op jit(solution)/shard_map/ppermute | solution.py:440
  87.2 5.1 %collective-permute-start.23 = (f32[64,64]{1,0:T(8,128)S(1)}, f32[64,64]{1,0:T(8,128)S(1)}, u32[]{:S(2)}, u32[]{:S(2)}) collective-permute-start(f32[64,64]{1,0:T(8,128)S(1)} %get-tuple-element.56.own), channel_id=1, source_target_pairs={{0,24},{1,25},{2,26},{3,27},{4,28},{5,29},{6,30},{7,31},{8,16},{9,... | collective-permute-start | bytes 49160 | tf_op jit(solution)/shard_map/ppermute | solution.py:440
  92.7 3.9 %collective-permute-start.24 = (f32[64,64]{1,0:T(8,128)S(1)}, f32[64,64]{1,0:T(8,128)S(1)}, u32[]{:S(2)}, u32[]{:S(2)}) collective-permute-start(f32[64,64]{1,0:T(8,128)S(1)} %get-tuple-element.57.own), channel_id=1, source_target_pairs={{0,32},{1,33},{2,34},{3,35},{4,36},{5,37},{6,38},{7,39},{8,40},{9,... | collective-permute-start | bytes 49160 | tf_op jit(solution)/shard_map/ppermute | solution.py:440
  96.9 5.1 %collective-permute-start.25 = (f32[64,64]{1,0:T(8,128)S(1)}, f32[64,64]{1,0:T(8,128)S(1)}, u32[]{:S(2)}, u32[]{:S(2)}) collective-permute-start(f32[64,64]{1,0:T(8,128)S(1)} %get-tuple-element.58.own), channel_id=1, source_target_pairs={{0,96},{1,97},{2,98},{3,99},{4,100},{5,101},{6,102},{7,103},{8,104... | collective-permute-start | bytes 49160 | tf_op jit(solution)/shard_map/ppermute | solution.py:440

commit v4 on v3

--- a/solution.py
+++ b/solution.py
@@ -8,7 +8,6 @@
 from jax.sharding import PartitionSpec as P
 
 AXES = ("leaf", "near")
-HOPS = (1, 2, 6, 8, 24, 32, 96)
 RANK = 64
 
 
@@ -87,28 +86,39 @@
     return [matrix[8 * p : 8 * p + 8, :] for p in range(8)]
 
 
-def factor_kernel(leaf_grams, inner_grams, leaf_factors, inner_factors):
-    count = leaf_grams.shape[0]
-    grams = [leaf_grams[n] for n in range(count)] + [inner_grams[n] for n in range(count - 1)]
-    for n, panels in enumerate(factor_panels([panels_of(gram) for gram in grams])):
-        for p in range(8):
-            if n < count:
-                leaf_factors[n, 8 * p : 8 * p + 8, :] = panels[p]
-            else:
-                inner_factors[n - count, 8 * p : 8 * p + 8, :] = panels[p]
-
-
-def factor_local(leaf_grams, inner_grams):
+def store_panels(ref, n, panels):
+    for p in range(8):
+        ref[n, 8 * p : 8 * p + 8, :] = panels[p]
+
+
+def factor_kernel(*refs):
+    grams, factors = refs[:-1], refs[-1]
+    matrices = []
+    for gram in grams:
+        if len(gram.shape) == 2:
+            matrices.append(panels_of(gram[...]))
+        else:
+            matrices += [panels_of(gram[n]) for n in range(gram.shape[0])]
+    for n, panels in enumerate(factor_panels(matrices)):
+        store_panels(factors, n, panels)
+
+
+def factor(*grams, keep=False):
+    count = sum(1 if gram.ndim == 2 else gram.shape[0] for gram in grams)
+    vmem = pl.BlockSpec(memory_space=pltpu.VMEM)
+    kind = pltpu.VMEM if keep else jax.ShapeDtypeStruct
     return pl.pallas_call(
         factor_kernel,
-        in_specs=[pl.BlockSpec(memory_space=pltpu.VMEM)] * 2,
-        out_shape=[
-            jax.ShapeDtypeStruct(leaf_grams.shape, jnp.float32),
-            jax.ShapeDtypeStruct(inner_grams.shape, jnp.float32),
-        ],
+        in_specs=[vmem] * len(grams),
+        out_specs=vmem,
+        out_shape=kind((count, RANK, RANK), jnp.float32),
         compiler_params=limit(4),
-        name="factor_local",
-    )(in_vmem(leaf_grams), in_vmem(inner_grams))
+        name="factor",
+    )(*[in_vmem(gram) for gram in grams])
+
+
+def limit(mebibytes):
+    return pltpu.CompilerParams(vmem_limit_bytes=mebibytes << 20)
 
 
 RING = ((0, 1, 2), (1, 2, 0))
@@ -206,10 +216,6 @@
     for piece in pieces:
         buffer[at : at + piece.shape[0]] = piece[...]
         at += piece.shape[0]
-
-
-def limit(mebibytes):
-    return pltpu.CompilerParams(vmem_limit_bytes=mebibytes << 20)
 
 
 def near_kernel(slots, blocks, samples, basis, *rest):
@@ -348,41 +354,76 @@
     )(tiles, halves, *[in_vmem(x) for x in inputs])
 
 
-def merge_kernel(level, own, other, transfers, gram, sent):
-    merged = 0.5 * (own[...] + other[...]) + unit_matrix()
-    gram[...] = merged
-    sent[...] = congruence(merged, transfers[level])
-
-
-def merge(level, own, other, transfers):
-    return pl.pallas_call(
-        functools.partial(merge_kernel, level),
-        in_specs=[pl.BlockSpec(memory_space=pltpu.VMEM)] * 3,
-        out_specs=[pl.BlockSpec(memory_space=pltpu.VMEM)] * 2,
+def merged(one, other):
+    return 0.5 * (one + other) + unit_matrix()
+
+
+def pair_kernel(own, other, transfers, gram, sent):
+    here = merged(own[...], other[...])
+    gram[...] = here
+    sent[...] = congruence(here, transfers[0])
+
+
+def merge_pair(own, other, transfers):
+    vmem = pl.BlockSpec(memory_space=pltpu.VMEM)
+    return pl.pallas_call(
+        pair_kernel,
+        in_specs=[vmem] * 3,
+        out_specs=[vmem] * 2,
         out_shape=[pltpu.VMEM((RANK, RANK), jnp.float32)] * 2,
         compiler_params=limit(4),
-        name="merge",
+        name="merge_pair",
     )(in_vmem(own), in_vmem(other), in_vmem(transfers))
 
 
-def last_kernel(own, other, *rest):
-    grams, factors = rest[:-1], rest[-1]
-    merged = 0.5 * (own[...] + other[...]) + unit_matrix()
-    out = factor_panels([panels_of(gram[...]) for gram in grams] + [panels_of(merged)])
-    for n, panels in enumerate(out):
-        for p in range(8):
-            factors[n, 8 * p : 8 * p + 8, :] = panels[p]
-
-
-def factor_upper(own, other, grams):
-    count = len(grams) + 1
-    return pl.pallas_call(
-        last_kernel,
-        in_specs=[pl.BlockSpec(memory_space=pltpu.VMEM)] * (count + 1),
-        out_shape=jax.ShapeDtypeStruct((count, RANK, RANK), jnp.float32),
+def two_levels(own, others, transfers, at, beside):
+    sibling, cousin, partner = others
+    here = merged(own[...], sibling[...])
+    there = merged(cousin[...], partner[...])
+    above = merged(congruence(here, transfers[at]), congruence(there, transfers[beside]))
+    return here, above
+
+
+def quad_kernel(at, beside, own, *rest):
+    others, transfers, (low, high, sent) = rest[:3], rest[3], rest[4:]
+    here, above = two_levels(own, others, transfers, at, beside)
+    low[...] = here
+    high[...] = above
+    sent[...] = congruence(above, transfers[at + 1])
+
+
+def merge_quad(at, beside, own, others, transfers):
+    vmem = pl.BlockSpec(memory_space=pltpu.VMEM)
+    return pl.pallas_call(
+        functools.partial(quad_kernel, at, beside),
+        in_specs=[vmem] * 5,
+        out_specs=[vmem] * 3,
+        out_shape=[pltpu.VMEM((RANK, RANK), jnp.float32)] * 3,
         compiler_params=limit(4),
-        name="factor_upper",
-    )(in_vmem(own), in_vmem(other), *[in_vmem(gram) for gram in grams])
+        name="merge_quad",
+    )(in_vmem(own), *[in_vmem(x) for x in others], in_vmem(transfers))
+
+
+def root_kernel(at, beside, own, *rest):
+    others, transfers, done, factors = rest[:3], rest[3], rest[4], rest[5]
+    pair = two_levels(own, others, transfers, at, beside)
+    count = done.shape[0]
+    for n, panels in enumerate(factor_panels([panels_of(gram) for gram in pair])):
+        store_panels(factors, count + n, panels)
+    for n in range(count):
+        factors[n] = done[n]
+
+
+def factor_root(at, beside, own, others, transfers, done):
+    vmem = pl.BlockSpec(memory_space=pltpu.VMEM)
+    return pl.pallas_call(
+        functools.partial(root_kernel, at, beside),
+        in_specs=[vmem] * 6,
+        out_specs=vmem,
+        out_shape=jax.ShapeDtypeStruct((done.shape[0] + 2, RANK, RANK), jnp.float32),
+        compiler_params=limit(4),
+        name="factor_root",
+    )(in_vmem(own), *[in_vmem(x) for x in others], in_vmem(transfers), in_vmem(done))
 
 
 def body(
@@ -408,7 +449,10 @@
     weights = gather_weights(paired, devices)
     vectors = exchange_vectors(test_vectors, device, devices)
     levels = jnp.arange(1, total_levels)
-    nodes = devices - (devices >> levels - 1) + (device >> levels)
+    starts = devices - (devices >> levels - 1)
+    nodes = jnp.concatenate(
+        [starts + (device >> levels), starts[1::2] + (device >> levels[1::2] ^ 1)]
+    )
     held, upper_transfer = lax.optimization_barrier((weights[0], upper_transfer))
     transfers = select_transfers(nodes, upper_transfer)
     live = jnp.arange(slots)[None, :] < adm_count[:, None]
@@ -434,19 +478,31 @@
         inner_transfer,
         weights,
     )
-    grams = []
-    for level in range(1, total_levels + 1):
-        hop = HOPS[level - 1]
-        other = lax.ppermute(sent, AXES, [(d, d ^ hop) for d in range(devices)])
-        if level == 1:
-            local_factors = factor_local(gram, inner_grams)
-            other, local_factors = lax.optimization_barrier((other, local_factors))
-        if level < total_levels:
-            gram_here, sent = merge(level - 1, sent, other, transfers)
-            grams.append(gram_here)
-    upper_factors = factor_upper(sent, other, grams)
-    leaf_factors, inner_factors = local_factors
-    return (leaf_factors, inner_factors[None], upper_factors[None])
+    def swapped_with(x, flip):
+        return lax.ppermute(x, AXES, [(d, d ^ flip) for d in range(devices)])
+
+    other = swapped_with(sent, 1)
+    first, sent = merge_pair(sent, other, transfers)
+    grams = [first]
+    local = []
+    for axis in range(3):
+        own = sent
+        others = [swapped_with(own, flip << 1 + 2 * axis) for flip in (1, 2, 3)]
+        if axis == 0:
+            ready = factor(gram)
+        elif axis == 1:
+            ready = factor(inner_grams)
+        else:
+            ready = factor(*grams, keep=True)
+        others[1], ready = lax.optimization_barrier((others[1], ready))
+        at = 1 + 2 * axis
+        if axis < 2:
+            local.append(ready)
+            low, high, sent = merge_quad(at, total_levels - 1 + axis, own, others, transfers)
+            grams += [low, high]
+        else:
+            upper_factors = factor_root(at, total_levels - 1 + axis, own, others, transfers, ready)
+    return (local[0], local[1][None], upper_factors[None])
 
 
 def solution(mesh):

time: 108 us -> 101 us (0.935)
  waiting for transfers between devices: 31.9 us -> 13.8 us
  starting transfers between devices: 38.1 us -> 44.9 us
  Pallas kernels: 23.4 us -> 26.1 us
  other arithmetic: 2.09 us -> 3.56 us
    ppermute x7 -> x10, waiting for transfers between devices: 18.8 us -> 1.31 us  [swapped_with(): return lax.ppermute(x, AXES, [(d, d ^ flip) for d in range(devices)])]
    ppermute x7 -> x10, starting transfers between devices: 10.9 us -> 13.9 us  [swapped_with(): return lax.ppermute(x, AXES, [(d, d ^ flip) for d in range(devices)])]
    ppermute x8, waiting for transfers between devices: 11.3 us -> 8.45 us  [ring_swap(): return lax.ppermute(x, AXES, pairs)]
    pallas_call x8 -> x7, Pallas kernels: 12.7 us -> 15.2 us  [the longest x3 10.5 us: factor(): pl.pallas_call(factor_kernel, in_specs=[vmem] * len(grams), out_specs=vme...]
    ppermute x5, waiting for transfers between devices: 0.36 us -> 2.58 us  [grid_swap(): return lax.ppermute(x, AXES, pairs)]
    ppermute x5, starting transfers between devices: 2.98 us -> 5.04 us  [grid_swap(): return lax.ppermute(x, AXES, pairs)]
    ppermute x8, starting transfers between devices: 22.9 us -> 24.6 us  [ring_swap(): return lax.ppermute(x, AXES, pairs)]
    unnamed x21 -> x15, local copies, waits for them, and re-layouts: 4.13 us -> 4.12 us
  transfers between devices with their start and end apart: 26 -> 29, of which waited for: 15 -> 10; matrix products, arithmetic and copies ran while one was open for 9% -> 12% of each run, Pallas kernels for 10% -> 16%
where the time goes in v4:
time: 101 us; the launch traced here: 100 us
  starting transfers between devices  44.9 us (44%)
  Pallas kernels  26.1 us (26%)
  waiting for transfers between devices  13.8 us (14%)
  local copies, waits for them, and re-layouts  11.2 us (11%)
  other arithmetic  3.56 us (4%)
    ppermute x8, starting transfers between devices, ring_swap(): return lax.ppermute(x, AXES, pairs)  24.6 us
    ppermute x10, starting transfers between devices, swapped_with(): return lax.ppermute(x, AXES, [(d, d ^ flip) for d in range(devices)])  13.9 us
    pallas_call x3, Pallas kernels, factor(): pl.pallas_call(factor_kernel, in_specs=[vmem] * len(grams), out_specs=vme...  10.5 us
    ppermute x8, waiting for transfers between devices, ring_swap(): return lax.ppermute(x, AXES, pairs)  8.45 us
    pallas_call x1, Pallas kernels, leaf_levels(): pl.pallas_call(leaf_kernel, in_specs=[pl.BlockSpec(memory_space=pltpu.SME...  5.32 us
    ppermute x5, starting transfers between devices, grid_swap(): return lax.ppermute(x, AXES, pairs)  5.04 us
    pallas_call x1, Pallas kernels, near_grams(): pl.pallas_call(near_kernel, in_specs=[pl.BlockSpec(memory_space=pltpu.SME...  4.72 us
    optimization_barrier x1, local copies, waits for them, and re-layouts, body(): lax.optimization_barrier((weights[0], upper_transfer))  4.16 us
  transfers between devices with their start and end apart: 29, of which 10 were waited for; matrix products, arithmetic and copies ran while one was open for 12% of the time, Pallas kernels for 16%

profile of v4, /device:TPU:0, one launch (start us, length us, event | category | flops | bytes accessed | tf_op | source)
XLA Modules:
  0.0 100.5 jit_solution(3038020127385887289)
XLA Ops:
  0.6 0.9 slice_bitcast_fusion.3
  1.6 2.1 %collective-permute-start.8 = (bf16[2,64,256]{2,1,0:T(8,128)(2,1)S(1)}, bf16[2,64,256]{2,1,0:T(8,128)(2,1)S(1)}, u32[]{:S(2)}, u32[]{:S(2)}) collective-permute-start(bf16[2,64,256]{2,1,0:T(8,128)(2,1)S(1)} %get-tuple-element.72), channel_id=1, source_target_pairs={{0,2},{1,3},{2,0},{3,1},{4,6},{5,7},{6,4},{7,5},{8,10},{9,11},{10,... | collective-permute-start | bytes 196616 | tf_op jit(solution)/shard_map/ppermute | solution.py:152
  3.7 0.7 collective-permute-start.9
  4.3 0.8 fusion
  5.1 0.7 constant_dynamic-update-slice_fusion.4
  5.8 5.9 %collective-permute-start = (bf16[2,64,128]{2,1,0:T(8,128)(2,1)S(1)}, bf16[2,64,128]{2,1,0:T(8,128)(2,1)S(1)}, u32[]{:S(2)}, u32[]{:S(2)}) collective-permute-start(bf16[2,64,128]{2,1,0:T(8,128)(2,1)S(1)} %get-tuple-element.60), channel_id=1, source_target_pairs={{0,2},{1,9},{2,0},{3,11},{4,6},{5,13},{6,4},{7,15},{8,10},{9,1},{1... | collective-permute-start | bytes 98312 | tf_op jit(solution)/shard_map/ppermute | solution.py:129
  11.7 0.8 and_add_fusion
  12.5 0.7 add_add_fusion
  13.2 0.1 slice.36
  13.3 0.3 collective-permute-done
  13.6 0.1 pad_maximum_fusion.4
  13.7 4.2 %collective-permute-start.1 = (bf16[4,64,128]{2,1,0:T(8,128)(2,1)S(1)}, bf16[4,64,128]{2,1,0:T(8,128)(2,1)S(1)}, u32[]{:S(2)}, u32[]{:S(2)}) collective-permute-start(bf16[4,64,128]{2,1,0:T(8,128)(2,1)S(1)} %pad_maximum_fusion.4), channel_id=1, source_target_pairs={{0,6},{1,25},{2,4},{3,27},{4,2},{5,29},{6,0},{7,31},{8,14},{9,17},... | collective-permute-start | bytes 196616 | tf_op jit(solution)/shard_map/ppermute | solution.py:129
  17.9 0.6 constant_dynamic-update-slice_fusion.3
  18.6 1.5 %collective-permute-done.1 = bf16[4,64,128]{2,1,0:T(8,128)(2,1)S(1)} collective-permute-done((bf16[4,64,128]{2,1,0:T(8,128)(2,1)S(1)}, bf16[4,64,128]{2,1,0:T(8,128)(2,1)S(1)}, u32[]{:S(2)}, u32[]{:S(2)}) %collective-permute-start.1) | collective-permute-done | bytes 65568 | tf_op jit(solution)/shard_map/ppermute | solution.py:129
  20.2 0.1 pad_maximum_fusion.3
  20.2 2.2 %collective-permute-start.2 = (bf16[8,64,128]{2,1,0:T(8,128)(2,1)S(1)}, bf16[8,64,128]{2,1,0:T(8,128)(2,1)S(1)}, u32[]{:S(2)}, u32[]{:S(2)}) collective-permute-start(bf16[8,64,128]{2,1,0:T(8,128)(2,1)S(1)} %pad_maximum_fusion.3), channel_id=1, source_target_pairs={{0,8},{1,33},{2,10},{3,35},{4,12},{5,37},{6,14},{7,39},{8,0},{9,41... | collective-permute-start | bytes 393224 | tf_op jit(solution)/shard_map/ppermute | solution.py:129
  22.4 0.1 collective-permute-start.10
  22.6 0.7 collective-permute-start.11
  23.2 0.6 constant_dynamic-update-slice_fusion.2
  23.9 1.5 %collective-permute-done.2 = bf16[8,64,128]{2,1,0:T(8,128)(2,1)S(1)} collective-permute-done((bf16[8,64,128]{2,1,0:T(8,128)(2,1)S(1)}, bf16[8,64,128]{2,1,0:T(8,128)(2,1)S(1)}, u32[]{:S(2)}, u32[]{:S(2)}) %collective-permute-start.2) | collective-permute-done | bytes 131104 | tf_op jit(solution)/shard_map/ppermute | solution.py:129
  25.4 1.0 collective-permute-start.3
  26.4 2.6 %collective-permute-done.10 = bf16[4,64,256]{2,1,0:T(8,128)(2,1)S(1)} collective-permute-done((bf16[4,64,256]{2,1,0:T(8,128)(2,1)S(1)}, bf16[4,64,256]{2,1,0:T(8,128)(2,1)S(1)}, u32[]{:S(2)}, u32[]{:S(2)}) %collective-permute-start.10) | collective-permute-done | bytes 131104 | tf_op jit(solution)/shard_map/ppermute | solution.py:152
  29.1 0.1 collective-permute-start.12
  29.2 1.5 %collective-permute-start.13 = (bf16[16,64,256]{2,1,0:T(8,128)(2,1)S(1)}, bf16[16,64,256]{2,1,0:T(8,128)(2,1)}, u32[]{:S(2)}, u32[]{:S(2)}) collective-permute-start(bf16[16,64,256]{2,1,0:T(8,128)(2,1)S(1)} %pad_maximum_fusion.rest_0_), channel_id=1, source_target_pairs={{0,0},{1,8},{2,2},{3,10},{4,4},{5,12},{6,6},{7,14},{8,1},{9,64},{1... | collective-permute-start | bytes 1572872 | tf_op jit(solution)/shard_map/ppermute | solution.py:152
  30.7 0.7 constant_dynamic-update-slice_fusion.1
  31.4 1.7 %collective-permute-done.3 = bf16[16,64,128]{2,1,0:T(8,128)(2,1)S(1)} collective-permute-done((bf16[16,64,128]{2,1,0:T(8,128)(2,1)S(1)}, bf16[16,64,128]{2,1,0:T(8,128)(2,1)S(1)}, u32[]{:S(2)}, u32[]{:S(2)}) %collective-permute-start.3) | collective-permute-done | bytes 262176 | tf_op jit(solution)/shard_map/ppermute | solution.py:129
  33.1 0.7 constant_dynamic-update-slice_fusion.rest_0_
  33.8 4.7 %collective-permute-start.4 = (bf16[32,64,128]{2,1,0:T(8,128)(2,1)}, bf16[32,64,128]{2,1,0:T(8,128)(2,1)S(1)}, u32[]{:S(2)}, u32[]{:S(2)}) collective-permute-start(bf16[32,64,128]{2,1,0:T(8,128)(2,1)} %constant_dynamic-update-slice_fusion.rest_0_), channel_id=1, source_target_pairs={{0,32},{1,3},{2,34},{3,1},{4,36},{5,7},{6,38},{7,5},{8,40},{9,11},... | collective-permute-start | bytes 1572872 | tf_op jit(solution)/shard_map/ppermute | solution.py:129
  38.5 1.9 %collective-permute-start.5 = (bf16[32,64,128]{2,1,0:T(8,128)(2,1)}, bf16[32,64,128]{2,1,0:T(8,128)(2,1)}, u32[]{:S(2)}, u32[]{:S(2)}) collective-permute-start(bf16[32,64,128]{2,1,0:T(8,128)(2,1)} %constant_dynamic-update-slice_fusion.rest_0_), channel_id=1, source_target_pairs={{0,96},{1,7},{2,98},{3,5},{4,100},{5,3},{6,102},{7,1},{8,104},{9,1... | collective-permute-start | bytes 1572872 | tf_op jit(solution)/shard_map/ppermute | solution.py:129
  40.4 0.1 slice.37
  40.8 4.2 %copy.15.upper_transfer = bf16[126,64,64]{2,1,0:T(8,128)(2,1)S(1)} copy(bf16[126,64,64]{0,2,1:T(8,128)(2,1)} %param.23) | data formatting | bytes 2064384 | tf_op jit(solution)/shard_map/optimization_barrier | solution.py:456
  45.0 0.8 select_transfers.1.transfers.rest_3_
  45.9 3.3 %collective-permute-done.5.rest_2_ = bf16[32,64,128]{2,1,0:T(8,128)(2,1)} collective-permute-done((bf16[32,64,128]{2,1,0:T(8,128)(2,1)}, bf16[32,64,128]{2,1,0:T(8,128)(2,1)}, u32[]{:S(2)}, u32[]{:S(2)}) %collective-permute-start.5) | collective-permute-done | bytes 524320 | tf_op jit(solution)/shard_map/ppermute | solution.py:129
  49.2 1.0 slice.38
  50.2 3.6 %collective-permute-start.6 = (bf16[16,64,128]{2,1,0:T(8,128)(2,1)S(1)}, bf16[16,64,128]{2,1,0:T(8,128)(2,1)S(1)}, u32[]{:S(2)}, u32[]{:S(2)}) collective-permute-start(bf16[16,64,128]{2,1,0:T(8,128)(2,1)S(1)} %slice.38), channel_id=1, source_target_pairs={{0,32},{1,3},{2,34},{3,1},{4,36},{5,7},{6,38},{7,5},{8,40},{9,11},... | collective-permute-start | bytes 786440 | tf_op jit(solution)/shard_map/ppermute | solution.py:129
  53.8 1.2 %collective-permute-start.7 = (bf16[16,64,128]{2,1,0:T(8,128)(2,1)S(1)}, bf16[16,64,128]{2,1,0:T(8,128)(2,1)S(1)}, u32[]{:S(2)}, u32[]{:S(2)}) collective-permute-start(bf16[16,64,128]{2,1,0:T(8,128)(2,1)S(1)} %slice.39), channel_id=1, source_target_pairs={{0,96},{1,7},{2,98},{3,5},{4,100},{5,3},{6,102},{7,1},{8,104},{9,1... | collective-permute-start | bytes 786440 | tf_op jit(solution)/shard_map/ppermute | solution.py:129
  55.0 0.5 collective-permute-start.15
  55.5 0.1 collective-permute-start.16
  55.6 2.2 %copy-done = bf16[4,8,256,256]{3,2,1,0:T(8,128)(2,1)S(1)} copy-done((bf16[4,8,256,256]{3,2,1,0:T(8,128)(2,1)S(1)}, bf16[4,8,256,256]{3,2,1,0:T(8,128)(2,1)}, u32[]{:S(2)}) %copy-start) | copy-done | bytes 4194328
  57.8 4.7 %near_grams.1.near_gram = f32[4,64,64]{2,1,0:T(8,128)S(1)} custom-call(s32[32]{0:T(128)S(1)} %reshape.18.slots, bf16[4,8,256,256]{3,2,1,0:T(8,128)(2,1)S(1)} %copy-done, bf16[4,64,256]{2,1,0:T(8,128)(2,1)S(1)} %copy-done.2, bf16[4,64,256]{2,1,0:T(8,128)(2,1)S(1)} %copy-done.3, bf16[16,64,256]{2,1,0:T(8,128)(2,1)S(1)} %pad_maximum_fusion.rest_0_, ...), custom_call_target="tpu_custom_call" | custom-call | tf_op jit(solution)/shard_map/near_grams/pallas_call | solution.py:247
  62.6 0.5 collective-permute-start.17
  63.1 0.1 collective-permute-start.18
  63.2 1.1 %collective-permute-done.17.rest_8_ = bf16[16,64,128]{2,1,0:T(8,128)(2,1)S(1)} collective-permute-done((bf16[16,64,128]{2,1,0:T(8,128)(2,1)S(1)}, bf16[16,64,128]{2,1,0:T(8,128)(2,1)S(1)}, u32[]{:S(2)}, u32[]{:S(2)}) %collective-permute-start.17) | collective-permute-done | bytes 262176 | tf_op jit(solution)/shard_map/ppermute | solution.py:162
  64.2 0.4 collective-permute-done.18.rest_9_
  64.6 5.3 %leaf_levels.1 = (f32[4,64,64]{2,1,0:T(8,128)S(1)}, f32[3,64,64]{2,1,0:T(8,128)S(1)}, f32[64,64]{1,0:T(8,128)S(1)}) custom-call(s32[128]{0:T(128)S(1)} %reshape.17.tiles, s32[128]{0:T(128)S(1)} %reshape.16.halves, bf16[4,64,2048]{2,1,0:T(8,128)(2,1)S(1)} %copy-done.1, f32[4,64,64]{2,1,0:T(8,128)S(1)} %near_grams.1.near_gram, ...), custom_call_target="tpu_custom_call" | custom-call | tf_op jit(solution)/shard_map/leaf_levels/pallas_call | solution.py:339
  70.0 0.4 collective-permute-start.19
  70.3 0.9 collective-permute-done.19.other
  71.2 0.3 merge_pair.1
  71.5 0.1 collective-permute-start.20
  71.6 2.6 %collective-permute-start.21 = (f32[64,64]{1,0:T(8,128)S(1)}, f32[64,64]{1,0:T(8,128)S(1)}, u32[]{:S(2)}, u32[]{:S(2)}) collective-permute-start(f32[64,64]{1,0:T(8,128)S(1)} %get-tuple-element.43.own), channel_id=1, source_target_pairs={{0,2},{1,3},{2,0},{3,1},{4,6},{5,7},{6,4},{7,5},{8,10},{9,11},{10,... | collective-permute-start | bytes 49160 | tf_op jit(solution)/shard_map/ppermute | solution.py:482
  74.2 2.6 %collective-permute-start.22 = (f32[64,64]{1,0:T(8,128)S(1)}, f32[64,64]{1,0:T(8,128)S(1)}, u32[]{:S(2)}, u32[]{:S(2)}) collective-permute-start(f32[64,64]{1,0:T(8,128)S(1)} %get-tuple-element.43.own), channel_id=1, source_target_pairs={{0,6},{1,7},{2,4},{3,5},{4,2},{5,3},{6,0},{7,1},{8,14},{9,15},{10,... | collective-permute-start | bytes 49160 | tf_op jit(solution)/shard_map/ppermute | solution.py:482
  76.8 3.7 %factor.3 = f32[4,64,64]{2,1,0:T(8,128)} custom-call(f32[4,64,64]{2,1,0:T(8,128)S(1)} %get-tuple-element.44.refs_0_), custom_call_target="tpu_custom_call" | custom-call | tf_op jit(solution)/shard_map/factor/pallas_call | solution.py:110
  80.5 0.6 merge_quad.2
  81.2 0.2 collective-permute-start.23
  81.4 1.8 %collective-permute-start.24 = (f32[64,64]{1,0:T(8,128)S(1)}, f32[64,64]{1,0:T(8,128)S(1)}, u32[]{:S(2)}, u32[]{:S(2)}) collective-permute-start(f32[64,64]{1,0:T(8,128)S(1)} %get-tuple-element.47.own), channel_id=1, source_target_pairs={{0,8},{1,9},{2,10},{3,11},{4,12},{5,13},{6,14},{7,15},{8,0},{9,1},... | collective-permute-start | bytes 49160 | tf_op jit(solution)/shard_map/ppermute | solution.py:482
  83.2 2.1 %collective-permute-start.25 = (f32[64,64]{1,0:T(8,128)S(1)}, f32[64,64]{1,0:T(8,128)S(1)}, u32[]{:S(2)}, u32[]{:S(2)}) collective-permute-start(f32[64,64]{1,0:T(8,128)S(1)} %get-tuple-element.47.own), channel_id=1, source_target_pairs={{0,24},{1,25},{2,26},{3,27},{4,28},{5,29},{6,30},{7,31},{8,16},{9,... | collective-permute-start | bytes 49160 | tf_op jit(solution)/shard_map/ppermute | solution.py:482
  85.3 3.2 %factor.4 = f32[3,64,64]{2,1,0:T(8,128)} custom-call(f32[3,64,64]{2,1,0:T(8,128)S(1)} %get-tuple-element.48.refs_0_), custom_call_target="tpu_custom_call" | custom-call | tf_op jit(solution)/shard_map/factor/pallas_call | solution.py:110
  88.5 0.6 merge_quad.3
  89.1 1.3 %collective-permute-start.27 = (f32[64,64]{1,0:T(8,128)S(1)}, f32[64,64]{1,0:T(8,128)S(1)}, u32[]{:S(2)}, u32[]{:S(2)}) collective-permute-start(f32[64,64]{1,0:T(8,128)S(1)} %get-tuple-element.51.own), channel_id=1, source_target_pairs={{0,64},{1,65},{2,66},{3,67},{4,68},{5,69},{6,70},{7,71},{8,72},{9,... | collective-permute-start | bytes 49160 | tf_op jit(solution)/shard_map/ppermute | solution.py:482
  90.5 1.7 %collective-permute-start.26 = (f32[64,64]{1,0:T(8,128)S(1)}, f32[64,64]{1,0:T(8,128)S(1)}, u32[]{:S(2)}, u32[]{:S(2)}) collective-permute-start(f32[64,64]{1,0:T(8,128)S(1)} %get-tuple-element.51.own), channel_id=1, source_target_pairs={{0,32},{1,33},{2,34},{3,35},{4,36},{5,37},{6,38},{7,39},{8,40},{9,... | collective-permute-start | bytes 49160 | tf_op jit(solution)/shard_map/ppermute | solution.py:482
  92.1 1.1 %collective-permute-start.28 = (f32[64,64]{1,0:T(8,128)S(1)}, f32[64,64]{1,0:T(8,128)S(1)}, u32[]{:S(2)}, u32[]{:S(2)}) collective-permute-start(f32[64,64]{1,0:T(8,128)S(1)} %get-tuple-element.51.own), channel_id=1, source_target_pairs={{0,96},{1,97},{2,98},{3,99},{4,100},{5,101},{6,102},{7,103},{8,104... | collective-permute-start | bytes 49160 | tf_op jit(solution)/shard_map/ppermute | solution.py:482
  93.2 3.6 %factor.5.rest_4_ = f32[5,64,64]{2,1,0:T(8,128)S(1)} custom-call(f32[64,64]{1,0:T(8,128)S(1)} %get-tuple-element.52.refs_0_, f32[64,64]{1,0:T(8,128)S(1)} %get-tuple-element.53.refs_1_, f32[64,64]{1,0:T(8,128)S(1)} %get-tuple-element.54.refs_2_, f32[64,64]{1,0:T(8,128)S(1)} %get-tuple-element.55.refs_3_, f32[64,64]{1,0:T(8,128)S(1)} %get-tuple-element.56.refs_4_), custom_call_target="tpu_custom_call" | custom-call | tf_op jit(solution)/shard_map/factor/pallas_call | solution.py:110
  96.8 0.4 collective-permute-done.28.rest_2_
  97.2 3.2 %factor_root.1 = f32[7,64,64]{2,1,0:T(8,128)} custom-call(f32[64,64]{1,0:T(8,128)S(1)} %get-tuple-element.51.own, f32[64,64]{1,0:T(8,128)S(1)} %collective-permute-done.26.rest_0_, f32[64,64]{1,0:T(8,128)S(1)} %collective-permute-done.27.rest_1_, f32[64,64]{1,0:T(8,128)S(1)} %collective-permute-done.28.rest_2_, ...), custom_call_target="tpu_custom_call" | custom-call | tf_op jit(solution)/shard_map/factor_root/pallas_call | solution.py:419
  (47 shorter events, 0.7 us)
Async XLA Ops:
  1.6 17.0 %collective-permute-start.8 = (bf16[2,64,256]{2,1,0:T(8,128)(2,1)S(1)}, bf16[2,64,256]{2,1,0:T(8,128)(2,1)S(1)}, u32[]{:S(2)}, u32[]{:S(2)}) collective-permute-start(bf16[2,64,256]{2,1,0:T(8,128)(2,1)S(1)} %get-tuple-element.72), channel_id=1, source_target_pairs={{0,2},{1,3},{2,0},{3,1},{4,6},{5,7},{6,4},{7,5},{8,10},{9,11},{10,... | collective-permute-start | bytes 196616 | tf_op jit(solution)/shard_map/ppermute | solution.py:152
  3.7 14.9 %collective-permute-start.9 = (bf16[2,64,256]{2,1,0:T(8,128)(2,1)S(1)}, bf16[2,64,256]{2,1,0:T(8,128)(2,1)S(1)}, u32[]{:S(2)}, u32[]{:S(2)}) collective-permute-start(bf16[2,64,256]{2,1,0:T(8,128)(2,1)S(1)} %get-tuple-element.70), channel_id=1, source_target_pairs={{0,0},{1,1},{2,16},{3,17},{4,4},{5,5},{6,20},{7,21},{8,8},{9,9},{1... | collective-permute-start | bytes 196616 | tf_op jit(solution)/shard_map/ppermute | solution.py:152
  5.8 7.8 %collective-permute-start = (bf16[2,64,128]{2,1,0:T(8,128)(2,1)S(1)}, bf16[2,64,128]{2,1,0:T(8,128)(2,1)S(1)}, u32[]{:S(2)}, u32[]{:S(2)}) collective-permute-start(bf16[2,64,128]{2,1,0:T(8,128)(2,1)S(1)} %get-tuple-element.60), channel_id=1, source_target_pairs={{0,2},{1,9},{2,0},{3,11},{4,6},{5,13},{6,4},{7,15},{8,10},{9,1},{1... | collective-permute-start | bytes 98312 | tf_op jit(solution)/shard_map/ppermute | solution.py:129
  13.7 6.5 %collective-permute-start.1 = (bf16[4,64,128]{2,1,0:T(8,128)(2,1)S(1)}, bf16[4,64,128]{2,1,0:T(8,128)(2,1)S(1)}, u32[]{:S(2)}, u32[]{:S(2)}) collective-permute-start(bf16[4,64,128]{2,1,0:T(8,128)(2,1)S(1)} %pad_maximum_fusion.4), channel_id=1, source_target_pairs={{0,6},{1,25},{2,4},{3,27},{4,2},{5,29},{6,0},{7,31},{8,14},{9,17},... | collective-permute-start | bytes 196616 | tf_op jit(solution)/shard_map/ppermute | solution.py:129
  20.2 5.1 %collective-permute-start.2 = (bf16[8,64,128]{2,1,0:T(8,128)(2,1)S(1)}, bf16[8,64,128]{2,1,0:T(8,128)(2,1)S(1)}, u32[]{:S(2)}, u32[]{:S(2)}) collective-permute-start(bf16[8,64,128]{2,1,0:T(8,128)(2,1)S(1)} %pad_maximum_fusion.3), channel_id=1, source_target_pairs={{0,8},{1,33},{2,10},{3,35},{4,12},{5,37},{6,14},{7,39},{8,0},{9,41... | collective-permute-start | bytes 393224 | tf_op jit(solution)/shard_map/ppermute | solution.py:129
  22.4 6.6 %collective-permute-start.10 = (bf16[4,64,256]{2,1,0:T(8,128)(2,1)S(1)}, bf16[4,64,256]{2,1,0:T(8,128)(2,1)S(1)}, u32[]{:S(2)}, u32[]{:S(2)}) collective-permute-start(bf16[4,64,256]{2,1,0:T(8,128)(2,1)S(1)} %get-tuple-element.65), channel_id=1, source_target_pairs={{0,4},{1,5},{2,6},{3,7},{4,0},{5,1},{6,2},{7,3},{8,12},{9,13},{10,... | collective-permute-start | bytes 393224 | tf_op jit(solution)/shard_map/ppermute | solution.py:152
  22.6 6.4 %collective-permute-start.11 = (bf16[4,64,256]{2,1,0:T(8,128)(2,1)S(1)}, bf16[4,64,256]{2,1,0:T(8,128)(2,1)S(1)}, u32[]{:S(2)}, u32[]{:S(2)}) collective-permute-start(bf16[4,64,256]{2,1,0:T(8,128)(2,1)S(1)} %get-tuple-element.66), channel_id=1, source_target_pairs={{0,0},{1,1},{2,2},{3,3},{4,32},{5,33},{6,34},{7,35},{8,8},{9,9},{1... | collective-permute-start | bytes 393224 | tf_op jit(solution)/shard_map/ppermute | solution.py:152
  25.4 7.7 %collective-permute-start.3 = (bf16[16,64,128]{2,1,0:T(8,128)(2,1)S(1)}, bf16[16,64,128]{2,1,0:T(8,128)(2,1)S(1)}, u32[]{:S(2)}, u32[]{:S(2)}) collective-permute-start(bf16[16,64,128]{2,1,0:T(8,128)(2,1)S(1)} %pad_maximum_fusion.1), channel_id=1, source_target_pairs={{0,24},{1,97},{2,26},{3,99},{4,28},{5,101},{6,30},{7,103},{8,16},{... | collective-permute-start | bytes 786440 | tf_op jit(solution)/shard_map/ppermute | solution.py:129
  29.0 26.6 %copy-start.2 = (bf16[4,64,256]{2,1,0:T(8,128)(2,1)S(1)}, bf16[4,64,256]{2,1,0:T(8,128)(2,1)}, u32[]{:S(2)}) copy-start(bf16[4,64,256]{2,1,0:T(8,128)(2,1)} %samples.1) | copy-start | bytes 393220
  29.0 26.6 %copy-start.3 = (bf16[4,64,256]{2,1,0:T(8,128)(2,1)S(1)}, bf16[4,64,256]{2,1,0:T(8,128)(2,1)}, u32[]{:S(2)}) copy-start(bf16[4,64,256]{2,1,0:T(8,128)(2,1)} %basis.1) | copy-start | bytes 393220
  29.1 25.9 %collective-permute-start.12 = (bf16[16,64,256]{2,1,0:T(8,128)(2,1)S(1)}, bf16[16,64,256]{2,1,0:T(8,128)(2,1)}, u32[]{:S(2)}, u32[]{:S(2)}) collective-permute-start(bf16[16,64,256]{2,1,0:T(8,128)(2,1)S(1)} %pad_maximum_fusion.rest_0_), channel_id=1, source_target_pairs={{0,1},{1,0},{2,3},{3,2},{4,5},{5,4},{6,7},{7,6},{8,9},{9,8},{10,11... | collective-permute-start | bytes 1572872 | tf_op jit(solution)/shard_map/ppermute | solution.py:162
  29.2 26.3 %collective-permute-start.13 = (bf16[16,64,256]{2,1,0:T(8,128)(2,1)S(1)}, bf16[16,64,256]{2,1,0:T(8,128)(2,1)}, u32[]{:S(2)}, u32[]{:S(2)}) collective-permute-start(bf16[16,64,256]{2,1,0:T(8,128)(2,1)S(1)} %pad_maximum_fusion.rest_0_), channel_id=1, source_target_pairs={{0,0},{1,8},{2,2},{3,10},{4,4},{5,12},{6,6},{7,14},{8,1},{9,64},{1... | collective-permute-start | bytes 1572872 | tf_op jit(solution)/shard_map/ppermute | solution.py:152
  33.8 12.1 %collective-permute-start.4 = (bf16[32,64,128]{2,1,0:T(8,128)(2,1)}, bf16[32,64,128]{2,1,0:T(8,128)(2,1)S(1)}, u32[]{:S(2)}, u32[]{:S(2)}) collective-permute-start(bf16[32,64,128]{2,1,0:T(8,128)(2,1)} %constant_dynamic-update-slice_fusion.rest_0_), channel_id=1, source_target_pairs={{0,32},{1,3},{2,34},{3,1},{4,36},{5,7},{6,38},{7,5},{8,40},{9,11},... | collective-permute-start | bytes 1572872 | tf_op jit(solution)/shard_map/ppermute | solution.py:129
  38.5 10.7 %collective-permute-start.5 = (bf16[32,64,128]{2,1,0:T(8,128)(2,1)}, bf16[32,64,128]{2,1,0:T(8,128)(2,1)}, u32[]{:S(2)}, u32[]{:S(2)}) collective-permute-start(bf16[32,64,128]{2,1,0:T(8,128)(2,1)} %constant_dynamic-update-slice_fusion.rest_0_), channel_id=1, source_target_pairs={{0,96},{1,7},{2,98},{3,5},{4,100},{5,3},{6,102},{7,1},{8,104},{9,1... | collective-permute-start | bytes 1572872 | tf_op jit(solution)/shard_map/ppermute | solution.py:129
  45.0 19.6 %copy-start.1 = (bf16[4,64,2048]{2,1,0:T(8,128)(2,1)S(1)}, bf16[4,64,2048]{2,1,0:T(8,128)(2,1)}, u32[]{:S(2)}) copy-start(bf16[4,64,2048]{2,1,0:T(8,128)(2,1)} %coupling.1) | copy-start | bytes 3145732
  45.0 19.6 %copy-start.4 = (bf16[4,64,64]{2,1,0:T(8,128)(2,1)S(1)}, bf16[4,64,64]{2,1,0:T(8,128)(2,1)}, u32[]{:S(2)}) copy-start(bf16[4,64,64]{2,1,0:T(8,128)(2,1)} %leaf_transfer.1) | copy-start | bytes 98308
  45.0 19.6 %copy-start.5 = (bf16[1,3,64,64]{3,2,1,0:T(8,128)(2,1)S(1)}, bf16[1,3,64,64]{3,2,1,0:T(8,128)(2,1)}, u32[]{:S(2)}) copy-start(bf16[1,3,64,64]{3,2,1,0:T(8,128)(2,1)} %inner_transfer.1) | copy-start | bytes 73732
  50.2 12.3 %collective-permute-start.6 = (bf16[16,64,128]{2,1,0:T(8,128)(2,1)S(1)}, bf16[16,64,128]{2,1,0:T(8,128)(2,1)S(1)}, u32[]{:S(2)}, u32[]{:S(2)}) collective-permute-start(bf16[16,64,128]{2,1,0:T(8,128)(2,1)S(1)} %slice.38), channel_id=1, source_target_pairs={{0,32},{1,3},{2,34},{3,1},{4,36},{5,7},{6,38},{7,5},{8,40},{9,11},... | collective-permute-start | bytes 786440 | tf_op jit(solution)/shard_map/ppermute | solution.py:129
  53.8 8.7 %collective-permute-start.7 = (bf16[16,64,128]{2,1,0:T(8,128)(2,1)S(1)}, bf16[16,64,128]{2,1,0:T(8,128)(2,1)S(1)}, u32[]{:S(2)}, u32[]{:S(2)}) collective-permute-start(bf16[16,64,128]{2,1,0:T(8,128)(2,1)S(1)} %slice.39), channel_id=1, source_target_pairs={{0,96},{1,7},{2,98},{3,5},{4,100},{5,3},{6,102},{7,1},{8,104},{9,1... | collective-permute-start | bytes 786440 | tf_op jit(solution)/shard_map/ppermute | solution.py:129
  55.0 8.1 %collective-permute-start.14 = (bf16[32,64,128]{2,1,0:T(8,128)(2,1)}, bf16[32,64,128]{2,1,0:T(8,128)(2,1)S(1)}, u32[]{:S(2)}, u32[]{:S(2)}) collective-permute-start(bf16[32,64,128]{2,1,0:T(8,128)(2,1)} %constant_dynamic-update-slice_fusion.rest_0_), channel_id=1, source_target_pairs={{0,1},{1,0},{2,3},{3,2},{4,5},{5,4},{6,7},{7,6},{8,9},{9,8},{10,11... | collective-permute-start | bytes 1572872 | tf_op jit(solution)/shard_map/ppermute | solution.py:162
  55.0 9.6 %collective-permute-start.15 = (bf16[32,64,128]{2,1,0:T(8,128)(2,1)S(1)}, bf16[32,64,128]{2,1,0:T(8,128)(2,1)S(1)}, u32[]{:S(2)}, u32[]{:S(2)}) collective-permute-start(bf16[32,64,128]{2,1,0:T(8,128)(2,1)S(1)} %collective-permute-done.4.rest_1_), channel_id=1, source_target_pairs={{0,1},{1,0},{2,3},{3,2},{4,5},{5,4},{6,7},{7,6},{8,9},{9,8},{10,11... | collective-permute-start | bytes 1572872 | tf_op jit(solution)/shard_map/ppermute | solution.py:162
  55.5 9.1 %collective-permute-start.16 = (bf16[32,64,128]{2,1,0:T(8,128)(2,1)}, bf16[32,64,128]{2,1,0:T(8,128)(2,1)S(1)}, u32[]{:S(2)}, u32[]{:S(2)}) collective-permute-start(bf16[32,64,128]{2,1,0:T(8,128)(2,1)} %collective-permute-done.5.rest_2_), channel_id=1, source_target_pairs={{0,1},{1,0},{2,3},{3,2},{4,5},{5,4},{6,7},{7,6},{8,9},{9,8},{10,11... | collective-permute-start | bytes 1572872 | tf_op jit(solution)/shard_map/ppermute | solution.py:162
  55.6 2.2 %copy-start = (bf16[4,8,256,256]{3,2,1,0:T(8,128)(2,1)S(1)}, bf16[4,8,256,256]{3,2,1,0:T(8,128)(2,1)}, u32[]{:S(2)}) copy-start(bf16[4,8,256,256]{3,2,1,0:T(8,128)(2,1)} %blocks.1) | copy-start | bytes 12582916
  62.6 1.7 %collective-permute-start.17 = (bf16[16,64,128]{2,1,0:T(8,128)(2,1)S(1)}, bf16[16,64,128]{2,1,0:T(8,128)(2,1)S(1)}, u32[]{:S(2)}, u32[]{:S(2)}) collective-permute-start(bf16[16,64,128]{2,1,0:T(8,128)(2,1)S(1)} %collective-permute-done.6.rest_3_), channel_id=1, source_target_pairs={{0,1},{1,0},{2,3},{3,2},{4,5},{5,4},{6,7},{7,6},{8,9},{9,8},{10,11... | collective-permute-start | bytes 786440 | tf_op jit(solution)/shard_map/ppermute | solution.py:162
  63.1 1.5 %collective-permute-start.18 = (bf16[16,64,128]{2,1,0:T(8,128)(2,1)S(1)}, bf16[16,64,128]{2,1,0:T(8,128)(2,1)S(1)}, u32[]{:S(2)}, u32[]{:S(2)}) collective-permute-start(bf16[16,64,128]{2,1,0:T(8,128)(2,1)S(1)} %collective-permute-done.7.rest_4_), channel_id=1, source_target_pairs={{0,1},{1,0},{2,3},{3,2},{4,5},{5,4},{6,7},{7,6},{8,9},{9,8},{10,11... | collective-permute-start | bytes 786440 | tf_op jit(solution)/shard_map/ppermute | solution.py:162
  70.0 1.3 %collective-permute-start.19 = (f32[64,64]{1,0:T(8,128)S(1)}, f32[64,64]{1,0:T(8,128)S(1)}, u32[]{:S(2)}, u32[]{:S(2)}) collective-permute-start(f32[64,64]{1,0:T(8,128)S(1)} %get-tuple-element.41.own), channel_id=1, source_target_pairs={{0,1},{1,0},{2,3},{3,2},{4,5},{5,4},{6,7},{7,6},{8,9},{9,8},{10,11... | collective-permute-start | bytes 49160 | tf_op jit(solution)/shard_map/ppermute | solution.py:482
  71.5 9.0 %collective-permute-start.20 = (f32[64,64]{1,0:T(8,128)S(1)}, f32[64,64]{1,0:T(8,128)S(1)}, u32[]{:S(2)}, u32[]{:S(2)}) collective-permute-start(f32[64,64]{1,0:T(8,128)S(1)} %get-tuple-element.43.own), channel_id=1, source_target_pairs={{0,4},{1,5},{2,6},{3,7},{4,0},{5,1},{6,2},{7,3},{8,12},{9,13},{10,... | collective-permute-start | bytes 49160 | tf_op jit(solution)/shard_map/ppermute | solution.py:482
  71.6 9.0 %collective-permute-start.21 = (f32[64,64]{1,0:T(8,128)S(1)}, f32[64,64]{1,0:T(8,128)S(1)}, u32[]{:S(2)}, u32[]{:S(2)}) collective-permute-start(f32[64,64]{1,0:T(8,128)S(1)} %get-tuple-element.43.own), channel_id=1, source_target_pairs={{0,2},{1,3},{2,0},{3,1},{4,6},{5,7},{6,4},{7,5},{8,10},{9,11},{10,... | collective-permute-start | bytes 49160 | tf_op jit(solution)/shard_map/ppermute | solution.py:482
  74.2 6.3 %collective-permute-start.22 = (f32[64,64]{1,0:T(8,128)S(1)}, f32[64,64]{1,0:T(8,128)S(1)}, u32[]{:S(2)}, u32[]{:S(2)}) collective-permute-start(f32[64,64]{1,0:T(8,128)S(1)} %get-tuple-element.43.own), channel_id=1, source_target_pairs={{0,6},{1,7},{2,4},{3,5},{4,2},{5,3},{6,0},{7,1},{8,14},{9,15},{10,... | collective-permute-start | bytes 49160 | tf_op jit(solution)/shard_map/ppermute | solution.py:482
  81.2 7.3 %collective-permute-start.23 = (f32[64,64]{1,0:T(8,128)S(1)}, f32[64,64]{1,0:T(8,128)S(1)}, u32[]{:S(2)}, u32[]{:S(2)}) collective-permute-start(f32[64,64]{1,0:T(8,128)S(1)} %get-tuple-element.47.own), channel_id=1, source_target_pairs={{0,16},{1,17},{2,18},{3,19},{4,20},{5,21},{6,22},{7,23},{8,24},{9,... | collective-permute-start | bytes 49160 | tf_op jit(solution)/shard_map/ppermute | solution.py:482
  81.4 7.1 %collective-permute-start.24 = (f32[64,64]{1,0:T(8,128)S(1)}, f32[64,64]{1,0:T(8,128)S(1)}, u32[]{:S(2)}, u32[]{:S(2)}) collective-permute-start(f32[64,64]{1,0:T(8,128)S(1)} %get-tuple-element.47.own), channel_id=1, source_target_pairs={{0,8},{1,9},{2,10},{3,11},{4,12},{5,13},{6,14},{7,15},{8,0},{9,1},... | collective-permute-start | bytes 49160 | tf_op jit(solution)/shard_map/ppermute | solution.py:482
  83.2 5.3 %collective-permute-start.25 = (f32[64,64]{1,0:T(8,128)S(1)}, f32[64,64]{1,0:T(8,128)S(1)}, u32[]{:S(2)}, u32[]{:S(2)}) collective-permute-start(f32[64,64]{1,0:T(8,128)S(1)} %get-tuple-element.47.own), channel_id=1, source_target_pairs={{0,24},{1,25},{2,26},{3,27},{4,28},{5,29},{6,30},{7,31},{8,16},{9,... | collective-permute-start | bytes 49160 | tf_op jit(solution)/shard_map/ppermute | solution.py:482
  89.1 7.7 %collective-permute-start.27 = (f32[64,64]{1,0:T(8,128)S(1)}, f32[64,64]{1,0:T(8,128)S(1)}, u32[]{:S(2)}, u32[]{:S(2)}) collective-permute-start(f32[64,64]{1,0:T(8,128)S(1)} %get-tuple-element.51.own), channel_id=1, source_target_pairs={{0,64},{1,65},{2,66},{3,67},{4,68},{5,69},{6,70},{7,71},{8,72},{9,... | collective-permute-start | bytes 49160 | tf_op jit(solution)/shard_map/ppermute | solution.py:482
  90.5 6.3 %collective-permute-start.26 = (f32[64,64]{1,0:T(8,128)S(1)}, f32[64,64]{1,0:T(8,128)S(1)}, u32[]{:S(2)}, u32[]{:S(2)}) collective-permute-start(f32[64,64]{1,0:T(8,128)S(1)} %get-tuple-element.51.own), channel_id=1, source_target_pairs={{0,32},{1,33},{2,34},{3,35},{4,36},{5,37},{6,38},{7,39},{8,40},{9,... | collective-permute-start | bytes 49160 | tf_op jit(solution)/shard_map/ppermute | solution.py:482
  92.1 5.1 %collective-permute-start.28 = (f32[64,64]{1,0:T(8,128)S(1)}, f32[64,64]{1,0:T(8,128)S(1)}, u32[]{:S(2)}, u32[]{:S(2)}) collective-permute-start(f32[64,64]{1,0:T(8,128)S(1)} %get-tuple-element.51.own), channel_id=1, source_target_pairs={{0,96},{1,97},{2,98},{3,99},{4,100},{5,101},{6,102},{7,103},{8,104... | collective-permute-start | bytes 49160 | tf_op jit(solution)/shard_map/ppermute | solution.py:482

commit v5 on v4

--- a/solution.py
+++ b/solution.py
@@ -184,8 +184,8 @@
 def gather_weights(own, devices):
     held = own
     for stage in range(2):
-        for flip in (1, 3):
-            held = jnp.concatenate([held, ring_swap(held, stage, flip, devices)])
+        others = [ring_swap(held, stage, flip, devices) for flip in (1, 3, 2)]
+        held = jnp.concatenate([held] + others)
     near = ring_swap(held, 2, 1, devices)
     last = ring_swap(held, 2, 3, devices)
     return [held, near, last]

time: 101 us -> 96.5 us (0.955)
  waiting for transfers between devices: 13.8 us -> 10.7 us
  starting transfers between devices: 44.9 us -> 42.4 us
  local copies, waits for them, and re-layouts: 11.2 us -> 12.4 us
    ppermute x8 -> x10, starting transfers between devices: 24.6 us -> 18.5 us  [ring_swap(): return lax.ppermute(x, AXES, pairs)]
    ppermute x5, waiting for transfers between devices: 2.58 us -> 0.01 us  [grid_swap(): return lax.ppermute(x, AXES, pairs)]
    ppermute x10, starting transfers between devices: 13.9 us -> 15.8 us  [swapped_with(): return lax.ppermute(x, AXES, [(d, d ^ flip) for d in range(devices)])]
    unnamed x15 -> x17, local copies, waits for them, and re-layouts: 4.12 us -> 5.38 us
    ppermute x8 -> x10, waiting for transfers between devices: 8.45 us -> 7.24 us  [ring_swap(): return lax.ppermute(x, AXES, pairs)]
  transfers between devices with their start and end apart: 29 -> 31, of which waited for: 10 -> 6; matrix products, arithmetic and copies ran while one was open for 12% -> 13% of each run, Pallas kernels for 16% -> 17%
where the time goes in v5:
time: 96.5 us; the launch traced here: 96 us
  starting transfers between devices  42.4 us (44%)
  Pallas kernels  26.1 us (27%)
  local copies, waits for them, and re-layouts  12.4 us (13%)
  waiting for transfers between devices  10.7 us (11%)
  other arithmetic  3.38 us (4%)
    ppermute x10, starting transfers between devices, ring_swap(): return lax.ppermute(x, AXES, pairs)  18.5 us
    ppermute x10, starting transfers between devices, swapped_with(): return lax.ppermute(x, AXES, [(d, d ^ flip) for d in range(devices)])  15.8 us
    pallas_call x3, Pallas kernels, factor(): pl.pallas_call(factor_kernel, in_specs=[vmem] * len(grams), out_specs=vme...  10.5 us
    ppermute x10, waiting for transfers between devices, ring_swap(): return lax.ppermute(x, AXES, pairs)  7.24 us
    ppermute x5, starting transfers between devices, grid_swap(): return lax.ppermute(x, AXES, pairs)  5.93 us
    unnamed x17, local copies, waits for them, and re-layouts  5.38 us
    pallas_call x1, Pallas kernels, leaf_levels(): pl.pallas_call(leaf_kernel, in_specs=[pl.BlockSpec(memory_space=pltpu.SME...  5.32 us
    pallas_call x1, Pallas kernels, near_grams(): pl.pallas_call(near_kernel, in_specs=[pl.BlockSpec(memory_space=pltpu.SME...  4.72 us
  transfers between devices with their start and end apart: 31, of which 6 were waited for; matrix products, arithmetic and copies ran while one was open for 13% of the time, Pallas kernels for 17%

profile of v5, /device:TPU:0, one launch (start us, length us, event | category | flops | bytes accessed | tf_op | source)
XLA Modules:
  0.0 96.0 jit_solution(17334203369274044052)
XLA Ops:
  0.6 0.8 fusion
  1.4 0.7 constant_dynamic-update-slice_fusion.6
  2.1 2.0 %collective-permute-start = (bf16[2,64,128]{2,1,0:T(8,128)(2,1)S(1)}, bf16[2,64,128]{2,1,0:T(8,128)(2,1)S(1)}, u32[]{:S(2)}, u32[]{:S(2)}) collective-permute-start(bf16[2,64,128]{2,1,0:T(8,128)(2,1)S(1)} %get-tuple-element.60), channel_id=1, source_target_pairs={{0,2},{1,9},{2,0},{3,11},{4,6},{5,13},{6,4},{7,15},{8,10},{9,1},{1... | collective-permute-start | bytes 98312 | tf_op jit(solution)/shard_map/ppermute | solution.py:129
  4.1 2.5 %collective-permute-start.1 = (bf16[2,64,128]{2,1,0:T(8,128)(2,1)S(1)}, bf16[2,64,128]{2,1,0:T(8,128)(2,1)S(1)}, u32[]{:S(2)}, u32[]{:S(2)}) collective-permute-start(bf16[2,64,128]{2,1,0:T(8,128)(2,1)S(1)} %get-tuple-element.60), channel_id=1, source_target_pairs={{0,6},{1,25},{2,4},{3,27},{4,2},{5,29},{6,0},{7,31},{8,14},{9,17},... | collective-permute-start | bytes 98312 | tf_op jit(solution)/shard_map/ppermute | solution.py:129
  6.7 1.1 %collective-permute-start.2 = (bf16[2,64,128]{2,1,0:T(8,128)(2,1)S(1)}, bf16[2,64,128]{2,1,0:T(8,128)(2,1)S(1)}, u32[]{:S(2)}, u32[]{:S(2)}) collective-permute-start(bf16[2,64,128]{2,1,0:T(8,128)(2,1)S(1)} %get-tuple-element.60), channel_id=1, source_target_pairs={{0,4},{1,17},{2,6},{3,19},{4,0},{5,21},{6,2},{7,23},{8,12},{9,25},... | collective-permute-start | bytes 98312 | tf_op jit(solution)/shard_map/ppermute | solution.py:129
  7.7 0.9 slice_bitcast_fusion.3
  8.6 0.6 collective-permute-start.10
  9.2 0.7 collective-permute-start.11
  9.9 0.8 and_add_fusion
  10.6 0.7 add_add_fusion
  11.4 0.1 slice.36
  11.5 0.6 collective-permute-done.2
  12.1 0.1 pad_maximum_fusion.2
  12.2 1.7 %collective-permute-start.3 = (bf16[8,64,128]{2,1,0:T(8,128)(2,1)S(1)}, bf16[8,64,128]{2,1,0:T(8,128)(2,1)S(1)}, u32[]{:S(2)}, u32[]{:S(2)}) collective-permute-start(bf16[8,64,128]{2,1,0:T(8,128)(2,1)S(1)} %pad_maximum_fusion.2), channel_id=1, source_target_pairs={{0,8},{1,33},{2,10},{3,35},{4,12},{5,37},{6,14},{7,39},{8,0},{9,41... | collective-permute-start | bytes 393224 | tf_op jit(solution)/shard_map/ppermute | solution.py:129
  13.8 4.3 %collective-permute-start.4 = (bf16[8,64,128]{2,1,0:T(8,128)(2,1)S(1)}, bf16[8,64,128]{2,1,0:T(8,128)(2,1)S(1)}, u32[]{:S(2)}, u32[]{:S(2)}) collective-permute-start(bf16[8,64,128]{2,1,0:T(8,128)(2,1)S(1)} %pad_maximum_fusion.2), channel_id=1, source_target_pairs={{0,24},{1,97},{2,26},{3,99},{4,28},{5,101},{6,30},{7,103},{8,16},{... | collective-permute-start | bytes 393224 | tf_op jit(solution)/shard_map/ppermute | solution.py:129
  18.2 1.4 %collective-permute-start.5 = (bf16[8,64,128]{2,1,0:T(8,128)(2,1)S(1)}, bf16[8,64,128]{2,1,0:T(8,128)(2,1)S(1)}, u32[]{:S(2)}, u32[]{:S(2)}) collective-permute-start(bf16[8,64,128]{2,1,0:T(8,128)(2,1)S(1)} %pad_maximum_fusion.2), channel_id=1, source_target_pairs={{0,16},{1,65},{2,18},{3,67},{4,20},{5,69},{6,22},{7,71},{8,24},{9,... | collective-permute-start | bytes 393224 | tf_op jit(solution)/shard_map/ppermute | solution.py:129
  19.5 0.6 constant_dynamic-update-slice_fusion.5
  20.2 0.6 constant_dynamic-update-slice_fusion.4
  20.8 0.6 constant_dynamic-update-slice_fusion.3
  21.5 2.5 %collective-permute-start.12 = (bf16[4,64,256]{2,1,0:T(8,128)(2,1)S(1)}, bf16[4,64,256]{2,1,0:T(8,128)(2,1)S(1)}, u32[]{:S(2)}, u32[]{:S(2)}) collective-permute-start(bf16[4,64,256]{2,1,0:T(8,128)(2,1)S(1)} %get-tuple-element.65), channel_id=1, source_target_pairs={{0,4},{1,5},{2,6},{3,7},{4,0},{5,1},{6,2},{7,3},{8,12},{9,13},{10,... | collective-permute-start | bytes 393224 | tf_op jit(solution)/shard_map/ppermute | solution.py:152
  24.1 0.7 collective-permute-start.13
  24.7 0.7 constant_dynamic-update-slice_fusion.2
  25.4 0.7 constant_dynamic-update-slice_fusion.1
  26.1 0.7 constant_dynamic-update-slice_fusion.rest_0_
  26.7 3.8 %collective-permute-start.6 = (bf16[32,64,128]{2,1,0:T(8,128)(2,1)}, bf16[32,64,128]{2,1,0:T(8,128)(2,1)S(1)}, u32[]{:S(2)}, u32[]{:S(2)}) collective-permute-start(bf16[32,64,128]{2,1,0:T(8,128)(2,1)} %constant_dynamic-update-slice_fusion.rest_0_), channel_id=1, source_target_pairs={{0,32},{1,3},{2,34},{3,1},{4,36},{5,7},{6,38},{7,5},{8,40},{9,11},... | collective-permute-start | bytes 1572872 | tf_op jit(solution)/shard_map/ppermute | solution.py:129
  30.5 1.6 %collective-permute-start.7 = (bf16[32,64,128]{2,1,0:T(8,128)(2,1)}, bf16[32,64,128]{2,1,0:T(8,128)(2,1)}, u32[]{:S(2)}, u32[]{:S(2)}) collective-permute-start(bf16[32,64,128]{2,1,0:T(8,128)(2,1)} %constant_dynamic-update-slice_fusion.rest_0_), channel_id=1, source_target_pairs={{0,96},{1,7},{2,98},{3,5},{4,100},{5,3},{6,102},{7,1},{8,104},{9,1... | collective-permute-start | bytes 1572872 | tf_op jit(solution)/shard_map/ppermute | solution.py:129
  32.2 0.1 collective-permute-start.14
  32.3 1.5 %collective-permute-start.15 = (bf16[16,64,256]{2,1,0:T(8,128)(2,1)S(1)}, bf16[16,64,256]{2,1,0:T(8,128)(2,1)}, u32[]{:S(2)}, u32[]{:S(2)}) collective-permute-start(bf16[16,64,256]{2,1,0:T(8,128)(2,1)S(1)} %pad_maximum_fusion.rest_0_), channel_id=1, source_target_pairs={{0,0},{1,8},{2,2},{3,10},{4,4},{5,12},{6,6},{7,14},{8,1},{9,64},{1... | collective-permute-start | bytes 1572872 | tf_op jit(solution)/shard_map/ppermute | solution.py:152
  33.8 0.1 slice.37
  34.2 4.2 %copy.15.upper_transfer = bf16[126,64,64]{2,1,0:T(8,128)(2,1)S(1)} copy(bf16[126,64,64]{0,2,1:T(8,128)(2,1)} %param.23) | data formatting | bytes 2064384 | tf_op jit(solution)/shard_map/optimization_barrier | solution.py:456
  38.4 1.0 %collective-permute-start.16 = (bf16[32,64,128]{2,1,0:T(8,128)(2,1)}, bf16[32,64,128]{2,1,0:T(8,128)(2,1)S(1)}, u32[]{:S(2)}, u32[]{:S(2)}) collective-permute-start(bf16[32,64,128]{2,1,0:T(8,128)(2,1)} %constant_dynamic-update-slice_fusion.rest_0_), channel_id=1, source_target_pairs={{0,1},{1,0},{2,3},{3,2},{4,5},{5,4},{6,7},{7,6},{8,9},{9,8},{10,11... | collective-permute-start | bytes 1572872 | tf_op jit(solution)/shard_map/ppermute | solution.py:162
  39.4 0.8 select_transfers.1.transfers.rest_3_
  40.3 6.6 %collective-permute-done.7.rest_2_ = bf16[32,64,128]{2,1,0:T(8,128)(2,1)} collective-permute-done((bf16[32,64,128]{2,1,0:T(8,128)(2,1)}, bf16[32,64,128]{2,1,0:T(8,128)(2,1)}, u32[]{:S(2)}, u32[]{:S(2)}) %collective-permute-start.7) | collective-permute-done | bytes 524320 | tf_op jit(solution)/shard_map/ppermute | solution.py:129
  46.8 1.0 %slice.38 = bf16[16,64,128]{2,1,0:T(8,128)(2,1)S(1)} slice(bf16[32,64,128]{2,1,0:T(8,128)(2,1)} %collective-permute-done.7.rest_2_), slice={[0:16], [0:64], [0:128]} | slice | bytes 524288 | tf_op jit(solution)/shard_map/slice | solution.py:196
  47.8 0.1 collective-permute-start.8
  47.9 0.1 collective-permute-start.9
  48.0 0.1 collective-permute-start.17
  48.1 0.5 collective-permute-start.18
  48.6 2.2 %copy-done = bf16[4,8,256,256]{3,2,1,0:T(8,128)(2,1)S(1)} copy-done((bf16[4,8,256,256]{3,2,1,0:T(8,128)(2,1)S(1)}, bf16[4,8,256,256]{3,2,1,0:T(8,128)(2,1)}, u32[]{:S(2)}) %copy-start) | copy-done | bytes 4194328
  50.8 4.7 %near_grams.1.near_gram = f32[4,64,64]{2,1,0:T(8,128)S(1)} custom-call(s32[32]{0:T(128)S(1)} %reshape.18.slots, bf16[4,8,256,256]{3,2,1,0:T(8,128)(2,1)S(1)} %copy-done, bf16[4,64,256]{2,1,0:T(8,128)(2,1)S(1)} %copy-done.2, bf16[4,64,256]{2,1,0:T(8,128)(2,1)S(1)} %copy-done.3, bf16[16,64,256]{2,1,0:T(8,128)(2,1)S(1)} %pad_maximum_fusion.rest_0_, ...), custom_call_target="tpu_custom_call" | custom-call | tf_op jit(solution)/shard_map/near_grams/pallas_call | solution.py:247
  55.6 0.2 collective-permute-start.19
  55.8 0.4 collective-permute-start.20
  56.2 1.0 %collective-permute-done.19.rest_8_ = bf16[16,64,128]{2,1,0:T(8,128)(2,1)S(1)} collective-permute-done((bf16[16,64,128]{2,1,0:T(8,128)(2,1)S(1)}, bf16[16,64,128]{2,1,0:T(8,128)(2,1)S(1)}, u32[]{:S(2)}, u32[]{:S(2)}) %collective-permute-start.19) | collective-permute-done | bytes 262176 | tf_op jit(solution)/shard_map/ppermute | solution.py:162
  57.2 0.4 collective-permute-done.20.rest_9_
  57.6 5.3 %leaf_levels.1 = (f32[4,64,64]{2,1,0:T(8,128)S(1)}, f32[3,64,64]{2,1,0:T(8,128)S(1)}, f32[64,64]{1,0:T(8,128)S(1)}) custom-call(s32[128]{0:T(128)S(1)} %reshape.17.tiles, s32[128]{0:T(128)S(1)} %reshape.16.halves, bf16[4,64,2048]{2,1,0:T(8,128)(2,1)S(1)} %copy-done.1, f32[4,64,64]{2,1,0:T(8,128)S(1)} %near_grams.1.near_gram, ...), custom_call_target="tpu_custom_call" | custom-call | tf_op jit(solution)/shard_map/leaf_levels/pallas_call | solution.py:339
  62.9 0.2 collective-permute-start.21
  63.0 1.1 %collective-permute-done.21.other = f32[64,64]{1,0:T(8,128)S(1)} collective-permute-done((f32[64,64]{1,0:T(8,128)S(1)}, f32[64,64]{1,0:T(8,128)S(1)}, u32[]{:S(2)}, u32[]{:S(2)}) %collective-permute-start.21) | collective-permute-done | bytes 16416 | tf_op jit(solution)/shard_map/ppermute | solution.py:482
  64.1 0.3 merge_pair.1
  64.4 2.0 %collective-permute-start.22 = (f32[64,64]{1,0:T(8,128)S(1)}, f32[64,64]{1,0:T(8,128)S(1)}, u32[]{:S(2)}, u32[]{:S(2)}) collective-permute-start(f32[64,64]{1,0:T(8,128)S(1)} %get-tuple-element.43.own), channel_id=1, source_target_pairs={{0,4},{1,5},{2,6},{3,7},{4,0},{5,1},{6,2},{7,3},{8,12},{9,13},{10,... | collective-permute-start | bytes 49160 | tf_op jit(solution)/shard_map/ppermute | solution.py:482
  66.4 2.3 %collective-permute-start.23 = (f32[64,64]{1,0:T(8,128)S(1)}, f32[64,64]{1,0:T(8,128)S(1)}, u32[]{:S(2)}, u32[]{:S(2)}) collective-permute-start(f32[64,64]{1,0:T(8,128)S(1)} %get-tuple-element.43.own), channel_id=1, source_target_pairs={{0,2},{1,3},{2,0},{3,1},{4,6},{5,7},{6,4},{7,5},{8,10},{9,11},{10,... | collective-permute-start | bytes 49160 | tf_op jit(solution)/shard_map/ppermute | solution.py:482
  68.8 0.4 collective-permute-start.24
  69.2 3.7 %factor.3 = f32[4,64,64]{2,1,0:T(8,128)} custom-call(f32[4,64,64]{2,1,0:T(8,128)S(1)} %get-tuple-element.44.refs_0_), custom_call_target="tpu_custom_call" | custom-call | tf_op jit(solution)/shard_map/factor/pallas_call | solution.py:110
  72.9 1.0 %collective-permute-done.24.rest_2_ = f32[64,64]{1,0:T(8,128)S(1)} collective-permute-done((f32[64,64]{1,0:T(8,128)S(1)}, f32[64,64]{1,0:T(8,128)S(1)}, u32[]{:S(2)}, u32[]{:S(2)}) %collective-permute-start.24) | collective-permute-done | bytes 16416 | tf_op jit(solution)/shard_map/ppermute | solution.py:482
  73.9 0.6 merge_quad.2
  74.5 1.4 %collective-permute-start.25 = (f32[64,64]{1,0:T(8,128)S(1)}, f32[64,64]{1,0:T(8,128)S(1)}, u32[]{:S(2)}, u32[]{:S(2)}) collective-permute-start(f32[64,64]{1,0:T(8,128)S(1)} %get-tuple-element.47.own), channel_id=1, source_target_pairs={{0,16},{1,17},{2,18},{3,19},{4,20},{5,21},{6,22},{7,23},{8,24},{9,... | collective-permute-start | bytes 49160 | tf_op jit(solution)/shard_map/ppermute | solution.py:482
  75.9 3.4 %collective-permute-start.26 = (f32[64,64]{1,0:T(8,128)S(1)}, f32[64,64]{1,0:T(8,128)S(1)}, u32[]{:S(2)}, u32[]{:S(2)}) collective-permute-start(f32[64,64]{1,0:T(8,128)S(1)} %get-tuple-element.47.own), channel_id=1, source_target_pairs={{0,8},{1,9},{2,10},{3,11},{4,12},{5,13},{6,14},{7,15},{8,0},{9,1},... | collective-permute-start | bytes 49160 | tf_op jit(solution)/shard_map/ppermute | solution.py:482
  79.4 1.9 %collective-permute-start.27 = (f32[64,64]{1,0:T(8,128)S(1)}, f32[64,64]{1,0:T(8,128)S(1)}, u32[]{:S(2)}, u32[]{:S(2)}) collective-permute-start(f32[64,64]{1,0:T(8,128)S(1)} %get-tuple-element.47.own), channel_id=1, source_target_pairs={{0,24},{1,25},{2,26},{3,27},{4,28},{5,29},{6,30},{7,31},{8,16},{9,... | collective-permute-start | bytes 49160 | tf_op jit(solution)/shard_map/ppermute | solution.py:482
  81.2 3.2 %factor.4 = f32[3,64,64]{2,1,0:T(8,128)} custom-call(f32[3,64,64]{2,1,0:T(8,128)S(1)} %get-tuple-element.48.refs_0_), custom_call_target="tpu_custom_call" | custom-call | tf_op jit(solution)/shard_map/factor/pallas_call | solution.py:110
  84.5 0.6 merge_quad.3
  85.1 1.7 %collective-permute-start.29 = (f32[64,64]{1,0:T(8,128)S(1)}, f32[64,64]{1,0:T(8,128)S(1)}, u32[]{:S(2)}, u32[]{:S(2)}) collective-permute-start(f32[64,64]{1,0:T(8,128)S(1)} %get-tuple-element.51.own), channel_id=1, source_target_pairs={{0,64},{1,65},{2,66},{3,67},{4,68},{5,69},{6,70},{7,71},{8,72},{9,... | collective-permute-start | bytes 49160 | tf_op jit(solution)/shard_map/ppermute | solution.py:482
  86.8 0.8 collective-permute-start.28
  87.5 1.7 %collective-permute-start.30 = (f32[64,64]{1,0:T(8,128)S(1)}, f32[64,64]{1,0:T(8,128)S(1)}, u32[]{:S(2)}, u32[]{:S(2)}) collective-permute-start(f32[64,64]{1,0:T(8,128)S(1)} %get-tuple-element.51.own), channel_id=1, source_target_pairs={{0,96},{1,97},{2,98},{3,99},{4,100},{5,101},{6,102},{7,103},{8,104... | collective-permute-start | bytes 49160 | tf_op jit(solution)/shard_map/ppermute | solution.py:482
  89.2 3.6 %factor.5.rest_4_ = f32[5,64,64]{2,1,0:T(8,128)S(1)} custom-call(f32[64,64]{1,0:T(8,128)S(1)} %get-tuple-element.52.refs_0_, f32[64,64]{1,0:T(8,128)S(1)} %get-tuple-element.53.refs_1_, f32[64,64]{1,0:T(8,128)S(1)} %get-tuple-element.54.refs_2_, f32[64,64]{1,0:T(8,128)S(1)} %get-tuple-element.55.refs_3_, f32[64,64]{1,0:T(8,128)S(1)} %get-tuple-element.56.refs_4_), custom_call_target="tpu_custom_call" | custom-call | tf_op jit(solution)/shard_map/factor/pallas_call | solution.py:110
  92.8 3.2 %factor_root.1 = f32[7,64,64]{2,1,0:T(8,128)} custom-call(f32[64,64]{1,0:T(8,128)S(1)} %get-tuple-element.51.own, f32[64,64]{1,0:T(8,128)S(1)} %collective-permute-done.28.rest_0_, f32[64,64]{1,0:T(8,128)S(1)} %collective-permute-done.29.rest_1_, f32[64,64]{1,0:T(8,128)S(1)} %collective-permute-done.30.rest_2_, ...), custom_call_target="tpu_custom_call" | custom-call | tf_op jit(solution)/shard_map/factor_root/pallas_call | solution.py:419
  (51 shorter events, 0.7 us)
Async XLA Ops:
  2.1 9.3 %collective-permute-start = (bf16[2,64,128]{2,1,0:T(8,128)(2,1)S(1)}, bf16[2,64,128]{2,1,0:T(8,128)(2,1)S(1)}, u32[]{:S(2)}, u32[]{:S(2)}) collective-permute-start(bf16[2,64,128]{2,1,0:T(8,128)(2,1)S(1)} %get-tuple-element.60), channel_id=1, source_target_pairs={{0,2},{1,9},{2,0},{3,11},{4,6},{5,13},{6,4},{7,15},{8,10},{9,1},{1... | collective-permute-start | bytes 98312 | tf_op jit(solution)/shard_map/ppermute | solution.py:129
  4.1 7.3 %collective-permute-start.1 = (bf16[2,64,128]{2,1,0:T(8,128)(2,1)S(1)}, bf16[2,64,128]{2,1,0:T(8,128)(2,1)S(1)}, u32[]{:S(2)}, u32[]{:S(2)}) collective-permute-start(bf16[2,64,128]{2,1,0:T(8,128)(2,1)S(1)} %get-tuple-element.60), channel_id=1, source_target_pairs={{0,6},{1,25},{2,4},{3,27},{4,2},{5,29},{6,0},{7,31},{8,14},{9,17},... | collective-permute-start | bytes 98312 | tf_op jit(solution)/shard_map/ppermute | solution.py:129
  6.7 5.4 %collective-permute-start.2 = (bf16[2,64,128]{2,1,0:T(8,128)(2,1)S(1)}, bf16[2,64,128]{2,1,0:T(8,128)(2,1)S(1)}, u32[]{:S(2)}, u32[]{:S(2)}) collective-permute-start(bf16[2,64,128]{2,1,0:T(8,128)(2,1)S(1)} %get-tuple-element.60), channel_id=1, source_target_pairs={{0,4},{1,17},{2,6},{3,19},{4,0},{5,21},{6,2},{7,23},{8,12},{9,25},... | collective-permute-start | bytes 98312 | tf_op jit(solution)/shard_map/ppermute | solution.py:129
  8.6 12.8 %collective-permute-start.10 = (bf16[2,64,256]{2,1,0:T(8,128)(2,1)S(1)}, bf16[2,64,256]{2,1,0:T(8,128)(2,1)S(1)}, u32[]{:S(2)}, u32[]{:S(2)}) collective-permute-start(bf16[2,64,256]{2,1,0:T(8,128)(2,1)S(1)} %get-tuple-element.72), channel_id=1, source_target_pairs={{0,2},{1,3},{2,0},{3,1},{4,6},{5,7},{6,4},{7,5},{8,10},{9,11},{10,... | collective-permute-start | bytes 196616 | tf_op jit(solution)/shard_map/ppermute | solution.py:152
  9.2 12.2 %collective-permute-start.11 = (bf16[2,64,256]{2,1,0:T(8,128)(2,1)S(1)}, bf16[2,64,256]{2,1,0:T(8,128)(2,1)S(1)}, u32[]{:S(2)}, u32[]{:S(2)}) collective-permute-start(bf16[2,64,256]{2,1,0:T(8,128)(2,1)S(1)} %get-tuple-element.70), channel_id=1, source_target_pairs={{0,0},{1,1},{2,16},{3,17},{4,4},{5,5},{6,20},{7,21},{8,8},{9,9},{1... | collective-permute-start | bytes 196616 | tf_op jit(solution)/shard_map/ppermute | solution.py:152
  12.2 12.6 %collective-permute-start.3 = (bf16[8,64,128]{2,1,0:T(8,128)(2,1)S(1)}, bf16[8,64,128]{2,1,0:T(8,128)(2,1)S(1)}, u32[]{:S(2)}, u32[]{:S(2)}) collective-permute-start(bf16[8,64,128]{2,1,0:T(8,128)(2,1)S(1)} %pad_maximum_fusion.2), channel_id=1, source_target_pairs={{0,8},{1,33},{2,10},{3,35},{4,12},{5,37},{6,14},{7,39},{8,0},{9,41... | collective-permute-start | bytes 393224 | tf_op jit(solution)/shard_map/ppermute | solution.py:129
  13.8 11.6 %collective-permute-start.4 = (bf16[8,64,128]{2,1,0:T(8,128)(2,1)S(1)}, bf16[8,64,128]{2,1,0:T(8,128)(2,1)S(1)}, u32[]{:S(2)}, u32[]{:S(2)}) collective-permute-start(bf16[8,64,128]{2,1,0:T(8,128)(2,1)S(1)} %pad_maximum_fusion.2), channel_id=1, source_target_pairs={{0,24},{1,97},{2,26},{3,99},{4,28},{5,101},{6,30},{7,103},{8,16},{... | collective-permute-start | bytes 393224 | tf_op jit(solution)/shard_map/ppermute | solution.py:129
  18.2 7.9 %collective-permute-start.5 = (bf16[8,64,128]{2,1,0:T(8,128)(2,1)S(1)}, bf16[8,64,128]{2,1,0:T(8,128)(2,1)S(1)}, u32[]{:S(2)}, u32[]{:S(2)}) collective-permute-start(bf16[8,64,128]{2,1,0:T(8,128)(2,1)S(1)} %pad_maximum_fusion.2), channel_id=1, source_target_pairs={{0,16},{1,65},{2,18},{3,67},{4,20},{5,69},{6,22},{7,71},{8,24},{9,... | collective-permute-start | bytes 393224 | tf_op jit(solution)/shard_map/ppermute | solution.py:129
  21.5 10.6 %collective-permute-start.12 = (bf16[4,64,256]{2,1,0:T(8,128)(2,1)S(1)}, bf16[4,64,256]{2,1,0:T(8,128)(2,1)S(1)}, u32[]{:S(2)}, u32[]{:S(2)}) collective-permute-start(bf16[4,64,256]{2,1,0:T(8,128)(2,1)S(1)} %get-tuple-element.65), channel_id=1, source_target_pairs={{0,4},{1,5},{2,6},{3,7},{4,0},{5,1},{6,2},{7,3},{8,12},{9,13},{10,... | collective-permute-start | bytes 393224 | tf_op jit(solution)/shard_map/ppermute | solution.py:152
  24.1 8.0 %collective-permute-start.13 = (bf16[4,64,256]{2,1,0:T(8,128)(2,1)S(1)}, bf16[4,64,256]{2,1,0:T(8,128)(2,1)S(1)}, u32[]{:S(2)}, u32[]{:S(2)}) collective-permute-start(bf16[4,64,256]{2,1,0:T(8,128)(2,1)S(1)} %get-tuple-element.66), channel_id=1, source_target_pairs={{0,0},{1,1},{2,2},{3,3},{4,32},{5,33},{6,34},{7,35},{8,8},{9,9},{1... | collective-permute-start | bytes 393224 | tf_op jit(solution)/shard_map/ppermute | solution.py:152
  25.4 23.2 %copy-start.2 = (bf16[4,64,256]{2,1,0:T(8,128)(2,1)S(1)}, bf16[4,64,256]{2,1,0:T(8,128)(2,1)}, u32[]{:S(2)}) copy-start(bf16[4,64,256]{2,1,0:T(8,128)(2,1)} %samples.1) | copy-start | bytes 393220
  25.4 23.2 %copy-start.3 = (bf16[4,64,256]{2,1,0:T(8,128)(2,1)S(1)}, bf16[4,64,256]{2,1,0:T(8,128)(2,1)}, u32[]{:S(2)}) copy-start(bf16[4,64,256]{2,1,0:T(8,128)(2,1)} %basis.1) | copy-start | bytes 393220
  26.7 13.5 %collective-permute-start.6 = (bf16[32,64,128]{2,1,0:T(8,128)(2,1)}, bf16[32,64,128]{2,1,0:T(8,128)(2,1)S(1)}, u32[]{:S(2)}, u32[]{:S(2)}) collective-permute-start(bf16[32,64,128]{2,1,0:T(8,128)(2,1)} %constant_dynamic-update-slice_fusion.rest_0_), channel_id=1, source_target_pairs={{0,32},{1,3},{2,34},{3,1},{4,36},{5,7},{6,38},{7,5},{8,40},{9,11},... | collective-permute-start | bytes 1572872 | tf_op jit(solution)/shard_map/ppermute | solution.py:129
  30.5 16.3 %collective-permute-start.7 = (bf16[32,64,128]{2,1,0:T(8,128)(2,1)}, bf16[32,64,128]{2,1,0:T(8,128)(2,1)}, u32[]{:S(2)}, u32[]{:S(2)}) collective-permute-start(bf16[32,64,128]{2,1,0:T(8,128)(2,1)} %constant_dynamic-update-slice_fusion.rest_0_), channel_id=1, source_target_pairs={{0,96},{1,7},{2,98},{3,5},{4,100},{5,3},{6,102},{7,1},{8,104},{9,1... | collective-permute-start | bytes 1572872 | tf_op jit(solution)/shard_map/ppermute | solution.py:129
  32.2 15.8 %collective-permute-start.14 = (bf16[16,64,256]{2,1,0:T(8,128)(2,1)S(1)}, bf16[16,64,256]{2,1,0:T(8,128)(2,1)}, u32[]{:S(2)}, u32[]{:S(2)}) collective-permute-start(bf16[16,64,256]{2,1,0:T(8,128)(2,1)S(1)} %pad_maximum_fusion.rest_0_), channel_id=1, source_target_pairs={{0,1},{1,0},{2,3},{3,2},{4,5},{5,4},{6,7},{7,6},{8,9},{9,8},{10,11... | collective-permute-start | bytes 1572872 | tf_op jit(solution)/shard_map/ppermute | solution.py:162
  32.3 15.8 %collective-permute-start.15 = (bf16[16,64,256]{2,1,0:T(8,128)(2,1)S(1)}, bf16[16,64,256]{2,1,0:T(8,128)(2,1)}, u32[]{:S(2)}, u32[]{:S(2)}) collective-permute-start(bf16[16,64,256]{2,1,0:T(8,128)(2,1)S(1)} %pad_maximum_fusion.rest_0_), channel_id=1, source_target_pairs={{0,0},{1,8},{2,2},{3,10},{4,4},{5,12},{6,6},{7,14},{8,1},{9,64},{1... | collective-permute-start | bytes 1572872 | tf_op jit(solution)/shard_map/ppermute | solution.py:152
  38.4 19.2 %copy-start.1 = (bf16[4,64,2048]{2,1,0:T(8,128)(2,1)S(1)}, bf16[4,64,2048]{2,1,0:T(8,128)(2,1)}, u32[]{:S(2)}) copy-start(bf16[4,64,2048]{2,1,0:T(8,128)(2,1)} %coupling.1) | copy-start | bytes 3145732
  38.4 19.2 %copy-start.4 = (bf16[4,64,64]{2,1,0:T(8,128)(2,1)S(1)}, bf16[4,64,64]{2,1,0:T(8,128)(2,1)}, u32[]{:S(2)}) copy-start(bf16[4,64,64]{2,1,0:T(8,128)(2,1)} %leaf_transfer.1) | copy-start | bytes 98308
  38.4 19.2 %copy-start.5 = (bf16[1,3,64,64]{3,2,1,0:T(8,128)(2,1)S(1)}, bf16[1,3,64,64]{3,2,1,0:T(8,128)(2,1)}, u32[]{:S(2)}) copy-start(bf16[1,3,64,64]{3,2,1,0:T(8,128)(2,1)} %inner_transfer.1) | copy-start | bytes 73732
  38.4 17.8 %collective-permute-start.16 = (bf16[32,64,128]{2,1,0:T(8,128)(2,1)}, bf16[32,64,128]{2,1,0:T(8,128)(2,1)S(1)}, u32[]{:S(2)}, u32[]{:S(2)}) collective-permute-start(bf16[32,64,128]{2,1,0:T(8,128)(2,1)} %constant_dynamic-update-slice_fusion.rest_0_), channel_id=1, source_target_pairs={{0,1},{1,0},{2,3},{3,2},{4,5},{5,4},{6,7},{7,6},{8,9},{9,8},{10,11... | collective-permute-start | bytes 1572872 | tf_op jit(solution)/shard_map/ppermute | solution.py:162
  47.8 7.7 %collective-permute-start.8 = (bf16[16,64,128]{2,1,0:T(8,128)(2,1)S(1)}, bf16[16,64,128]{2,1,0:T(8,128)(2,1)S(1)}, u32[]{:S(2)}, u32[]{:S(2)}) collective-permute-start(bf16[16,64,128]{2,1,0:T(8,128)(2,1)S(1)} %slice.38), channel_id=1, source_target_pairs={{0,32},{1,3},{2,34},{3,1},{4,36},{5,7},{6,38},{7,5},{8,40},{9,11},... | collective-permute-start | bytes 786440 | tf_op jit(solution)/shard_map/ppermute | solution.py:129
  47.9 7.7 %collective-permute-start.9 = (bf16[16,64,128]{2,1,0:T(8,128)(2,1)S(1)}, bf16[16,64,128]{2,1,0:T(8,128)(2,1)S(1)}, u32[]{:S(2)}, u32[]{:S(2)}) collective-permute-start(bf16[16,64,128]{2,1,0:T(8,128)(2,1)S(1)} %slice.39), channel_id=1, source_target_pairs={{0,96},{1,7},{2,98},{3,5},{4,100},{5,3},{6,102},{7,1},{8,104},{9,1... | collective-permute-start | bytes 786440 | tf_op jit(solution)/shard_map/ppermute | solution.py:129
  48.0 8.1 %collective-permute-start.17 = (bf16[32,64,128]{2,1,0:T(8,128)(2,1)S(1)}, bf16[32,64,128]{2,1,0:T(8,128)(2,1)S(1)}, u32[]{:S(2)}, u32[]{:S(2)}) collective-permute-start(bf16[32,64,128]{2,1,0:T(8,128)(2,1)S(1)} %collective-permute-done.6.rest_1_), channel_id=1, source_target_pairs={{0,1},{1,0},{2,3},{3,2},{4,5},{5,4},{6,7},{7,6},{8,9},{9,8},{10,11... | collective-permute-start | bytes 1572872 | tf_op jit(solution)/shard_map/ppermute | solution.py:162
  48.1 8.0 %collective-permute-start.18 = (bf16[32,64,128]{2,1,0:T(8,128)(2,1)}, bf16[32,64,128]{2,1,0:T(8,128)(2,1)S(1)}, u32[]{:S(2)}, u32[]{:S(2)}) collective-permute-start(bf16[32,64,128]{2,1,0:T(8,128)(2,1)} %collective-permute-done.7.rest_2_), channel_id=1, source_target_pairs={{0,1},{1,0},{2,3},{3,2},{4,5},{5,4},{6,7},{7,6},{8,9},{9,8},{10,11... | collective-permute-start | bytes 1572872 | tf_op jit(solution)/shard_map/ppermute | solution.py:162
  48.6 2.2 %copy-start = (bf16[4,8,256,256]{3,2,1,0:T(8,128)(2,1)S(1)}, bf16[4,8,256,256]{3,2,1,0:T(8,128)(2,1)}, u32[]{:S(2)}) copy-start(bf16[4,8,256,256]{3,2,1,0:T(8,128)(2,1)} %blocks.1) | copy-start | bytes 12582916
  55.6 1.6 %collective-permute-start.19 = (bf16[16,64,128]{2,1,0:T(8,128)(2,1)S(1)}, bf16[16,64,128]{2,1,0:T(8,128)(2,1)S(1)}, u32[]{:S(2)}, u32[]{:S(2)}) collective-permute-start(bf16[16,64,128]{2,1,0:T(8,128)(2,1)S(1)} %collective-permute-done.8.rest_3_), channel_id=1, source_target_pairs={{0,1},{1,0},{2,3},{3,2},{4,5},{5,4},{6,7},{7,6},{8,9},{9,8},{10,11... | collective-permute-start | bytes 786440 | tf_op jit(solution)/shard_map/ppermute | solution.py:162
  55.8 1.8 %collective-permute-start.20 = (bf16[16,64,128]{2,1,0:T(8,128)(2,1)S(1)}, bf16[16,64,128]{2,1,0:T(8,128)(2,1)S(1)}, u32[]{:S(2)}, u32[]{:S(2)}) collective-permute-start(bf16[16,64,128]{2,1,0:T(8,128)(2,1)S(1)} %collective-permute-done.9.rest_4_), channel_id=1, source_target_pairs={{0,1},{1,0},{2,3},{3,2},{4,5},{5,4},{6,7},{7,6},{8,9},{9,8},{10,11... | collective-permute-start | bytes 786440 | tf_op jit(solution)/shard_map/ppermute | solution.py:162
  62.9 1.2 %collective-permute-start.21 = (f32[64,64]{1,0:T(8,128)S(1)}, f32[64,64]{1,0:T(8,128)S(1)}, u32[]{:S(2)}, u32[]{:S(2)}) collective-permute-start(f32[64,64]{1,0:T(8,128)S(1)} %get-tuple-element.41.own), channel_id=1, source_target_pairs={{0,1},{1,0},{2,3},{3,2},{4,5},{5,4},{6,7},{7,6},{8,9},{9,8},{10,11... | collective-permute-start | bytes 49160 | tf_op jit(solution)/shard_map/ppermute | solution.py:482
  64.4 8.5 %collective-permute-start.22 = (f32[64,64]{1,0:T(8,128)S(1)}, f32[64,64]{1,0:T(8,128)S(1)}, u32[]{:S(2)}, u32[]{:S(2)}) collective-permute-start(f32[64,64]{1,0:T(8,128)S(1)} %get-tuple-element.43.own), channel_id=1, source_target_pairs={{0,4},{1,5},{2,6},{3,7},{4,0},{5,1},{6,2},{7,3},{8,12},{9,13},{10,... | collective-permute-start | bytes 49160 | tf_op jit(solution)/shard_map/ppermute | solution.py:482
  66.4 6.4 %collective-permute-start.23 = (f32[64,64]{1,0:T(8,128)S(1)}, f32[64,64]{1,0:T(8,128)S(1)}, u32[]{:S(2)}, u32[]{:S(2)}) collective-permute-start(f32[64,64]{1,0:T(8,128)S(1)} %get-tuple-element.43.own), channel_id=1, source_target_pairs={{0,2},{1,3},{2,0},{3,1},{4,6},{5,7},{6,4},{7,5},{8,10},{9,11},{10,... | collective-permute-start | bytes 49160 | tf_op jit(solution)/shard_map/ppermute | solution.py:482
  68.8 5.1 %collective-permute-start.24 = (f32[64,64]{1,0:T(8,128)S(1)}, f32[64,64]{1,0:T(8,128)S(1)}, u32[]{:S(2)}, u32[]{:S(2)}) collective-permute-start(f32[64,64]{1,0:T(8,128)S(1)} %get-tuple-element.43.own), channel_id=1, source_target_pairs={{0,6},{1,7},{2,4},{3,5},{4,2},{5,3},{6,0},{7,1},{8,14},{9,15},{10,... | collective-permute-start | bytes 49160 | tf_op jit(solution)/shard_map/ppermute | solution.py:482
  74.5 10.0 %collective-permute-start.25 = (f32[64,64]{1,0:T(8,128)S(1)}, f32[64,64]{1,0:T(8,128)S(1)}, u32[]{:S(2)}, u32[]{:S(2)}) collective-permute-start(f32[64,64]{1,0:T(8,128)S(1)} %get-tuple-element.47.own), channel_id=1, source_target_pairs={{0,16},{1,17},{2,18},{3,19},{4,20},{5,21},{6,22},{7,23},{8,24},{9,... | collective-permute-start | bytes 49160 | tf_op jit(solution)/shard_map/ppermute | solution.py:482
  75.9 8.6 %collective-permute-start.26 = (f32[64,64]{1,0:T(8,128)S(1)}, f32[64,64]{1,0:T(8,128)S(1)}, u32[]{:S(2)}, u32[]{:S(2)}) collective-permute-start(f32[64,64]{1,0:T(8,128)S(1)} %get-tuple-element.47.own), channel_id=1, source_target_pairs={{0,8},{1,9},{2,10},{3,11},{4,12},{5,13},{6,14},{7,15},{8,0},{9,1},... | collective-permute-start | bytes 49160 | tf_op jit(solution)/shard_map/ppermute | solution.py:482
  79.4 5.1 %collective-permute-start.27 = (f32[64,64]{1,0:T(8,128)S(1)}, f32[64,64]{1,0:T(8,128)S(1)}, u32[]{:S(2)}, u32[]{:S(2)}) collective-permute-start(f32[64,64]{1,0:T(8,128)S(1)} %get-tuple-element.47.own), channel_id=1, source_target_pairs={{0,24},{1,25},{2,26},{3,27},{4,28},{5,29},{6,30},{7,31},{8,16},{9,... | collective-permute-start | bytes 49160 | tf_op jit(solution)/shard_map/ppermute | solution.py:482
  85.1 7.7 %collective-permute-start.29 = (f32[64,64]{1,0:T(8,128)S(1)}, f32[64,64]{1,0:T(8,128)S(1)}, u32[]{:S(2)}, u32[]{:S(2)}) collective-permute-start(f32[64,64]{1,0:T(8,128)S(1)} %get-tuple-element.51.own), channel_id=1, source_target_pairs={{0,64},{1,65},{2,66},{3,67},{4,68},{5,69},{6,70},{7,71},{8,72},{9,... | collective-permute-start | bytes 49160 | tf_op jit(solution)/shard_map/ppermute | solution.py:482
  86.8 6.0 %collective-permute-start.28 = (f32[64,64]{1,0:T(8,128)S(1)}, f32[64,64]{1,0:T(8,128)S(1)}, u32[]{:S(2)}, u32[]{:S(2)}) collective-permute-start(f32[64,64]{1,0:T(8,128)S(1)} %get-tuple-element.51.own), channel_id=1, source_target_pairs={{0,32},{1,33},{2,34},{3,35},{4,36},{5,37},{6,38},{7,39},{8,40},{9,... | collective-permute-start | bytes 49160 | tf_op jit(solution)/shard_map/ppermute | solution.py:482
  87.5 5.3 %collective-permute-start.30 = (f32[64,64]{1,0:T(8,128)S(1)}, f32[64,64]{1,0:T(8,128)S(1)}, u32[]{:S(2)}, u32[]{:S(2)}) collective-permute-start(f32[64,64]{1,0:T(8,128)S(1)} %get-tuple-element.51.own), channel_id=1, source_target_pairs={{0,96},{1,97},{2,98},{3,99},{4,100},{5,101},{6,102},{7,103},{8,104... | collective-permute-start | bytes 49160 | tf_op jit(solution)/shard_map/ppermute | solution.py:482

commit v6 on v5

--- a/solution.py
+++ b/solution.py
@@ -124,6 +124,46 @@
 RING = ((0, 1, 2), (1, 2, 0))
 
 
+def join_pieces(pieces, buffer):
+    at = 0
+    for piece in pieces:
+        buffer[at : at + piece.shape[0]] = piece[...]
+        at += piece.shape[0]
+
+
+def join_kernel(*refs):
+    join_pieces(refs[:-1], refs[-1])
+
+
+def join(pieces):
+    vmem = pl.BlockSpec(memory_space=pltpu.VMEM)
+    shape = (sum(piece.shape[0] for piece in pieces),) + pieces[0].shape[1:]
+    return pl.pallas_call(
+        join_kernel,
+        in_specs=[vmem] * len(pieces),
+        out_specs=vmem,
+        out_shape=pltpu.VMEM(shape, pieces[0].dtype),
+        compiler_params=limit(4),
+        name="join",
+    )(*[in_vmem(piece) for piece in pieces])
+
+
+def part_kernel(start, whole, part):
+    part[...] = whole[start : start + part.shape[0]]
+
+
+def part_of(whole, start, size):
+    vmem = pl.BlockSpec(memory_space=pltpu.VMEM)
+    return pl.pallas_call(
+        functools.partial(part_kernel, start),
+        in_specs=[vmem],
+        out_specs=vmem,
+        out_shape=pltpu.VMEM((size,) + whole.shape[1:], whole.dtype),
+        compiler_params=limit(4),
+        name="part",
+    )(in_vmem(whole))
+
+
 def ring_swap(x, stage, flip, devices):
     pairs = [(d, d ^ flip << 1 + 2 * RING[d & 1][stage]) for d in range(devices)]
     return lax.ppermute(x, AXES, pairs)
@@ -185,7 +225,7 @@
     held = own
     for stage in range(2):
         others = [ring_swap(held, stage, flip, devices) for flip in (1, 3, 2)]
-        held = jnp.concatenate([held] + others)
+        held = join([held] + others)
     near = ring_swap(held, 2, 1, devices)
     last = ring_swap(held, 2, 3, devices)
     return [held, near, last]
@@ -193,7 +233,8 @@
 
 def gather_far(near, last, devices):
     half = near.shape[0] // 2
-    return [ring_swap(last[:half], 2, 1, devices), ring_swap(near[half:], 2, 3, devices)]
+    low, high = part_of(last, 0, half), part_of(near, half, half)
+    return [ring_swap(low, 2, 1, devices), ring_swap(high, 2, 3, devices)]
 
 
 def weight_tiles(adm_index, device):
@@ -209,13 +250,6 @@
     core = owner & 1
     other = core ^ (device & 1)
     return other * 128 + 2 * jnp.where(core == 1, order[1], order[0]) + (adm_index >> 1 & 1)
-
-
-def join_pieces(pieces, buffer):
-    at = 0
-    for piece in pieces:
-        buffer[at : at + piece.shape[0]] = piece[...]
-        at += piece.shape[0]
 
 
 def near_kernel(slots, blocks, samples, basis, *rest):
@@ -448,6 +482,10 @@
     paired = jnp.concatenate([col_weights[0::2], col_weights[1::2]], axis=2)
     weights = gather_weights(paired, devices)
     vectors = exchange_vectors(test_vectors, device, devices)
+    held, near_index, adm_index, adm_count = lax.optimization_barrier(
+        (weights[0], near_index, adm_index, adm_count)
+    )
+    weights[0] = held
     levels = jnp.arange(1, total_levels)
     starts = devices - (devices >> levels - 1)
     nodes = jnp.concatenate(

time: 96.5 us -> 94.3 us (0.977)
  local copies, waits for them, and re-layouts: 12.4 us -> 7.64 us
  starting transfers between devices: 42.4 us -> 47.1 us
  waiting for transfers between devices: 10.7 us -> 8.43 us
  other arithmetic: 3.38 us -> 2.15 us
  Pallas kernels: 26.1 us -> 27.3 us
    ppermute x5, starting transfers between devices: 5.93 us -> 9.8 us  [grid_swap(): return lax.ppermute(x, AXES, pairs)]
    ppermute x10, waiting for transfers between devices: 7.24 us -> 3.72 us  [ring_swap(): return lax.ppermute(x, AXES, pairs)]
    unnamed x17 -> x18, local copies, waits for them, and re-layouts: 5.38 us -> 2.23 us
    ppermute x10, starting transfers between devices: 18.5 us -> 20.2 us  [ring_swap(): return lax.ppermute(x, AXES, pairs)]
    ppermute x10, starting transfers between devices: 15.8 us -> 14.5 us  [swapped_with(): return lax.ppermute(x, AXES, [(d, d ^ flip) for d in range(devices)])]
    pallas_call x0 -> x4, Pallas kernels: none -> 1.2 us  [the longest x2 1.16 us: part_of(): pl.pallas_call(functools.partial(part_kernel, start), in_specs=[vmem], ou...]
    ppermute x10, waiting for transfers between devices: 2.09 us -> 3.26 us  [swapped_with(): return lax.ppermute(x, AXES, [(d, d ^ flip) for d in range(devices)])]
    slice x2 -> x0, local copies, waits for them, and re-layouts: 0.99 us -> none  [the longest x1 0.97 us: gather_far(): last[:half]]
  transfers between devices with their start and end apart: 31 -> 31, of which waited for: 6 -> 8; matrix products, arithmetic and copies ran while one was open for 13% -> 7% of each run, Pallas kernels for 17% -> 19%
where the time goes in v6:
time: 94.3 us; the launch traced here: 93.6 us
  starting transfers between devices  47.1 us (50%)
  Pallas kernels  27.3 us (29%)
  waiting for transfers between devices  8.43 us (9%)
  local copies, waits for them, and re-layouts  7.64 us (8%)
  other arithmetic  2.15 us (2%)
  between operations  0.97 us (1%)
    ppermute x10, starting transfers between devices, ring_swap(): return lax.ppermute(x, AXES, pairs)  20.2 us
    ppermute x10, starting transfers between devices, swapped_with(): return lax.ppermute(x, AXES, [(d, d ^ flip) for d in range(devices)])  14.5 us
    pallas_call x3, Pallas kernels, factor(): pl.pallas_call(factor_kernel, in_specs=[vmem] * len(grams), out_specs=vme...  10.5 us
    ppermute x5, starting transfers between devices, grid_swap(): return lax.ppermute(x, AXES, pairs)  9.8 us
    pallas_call x1, Pallas kernels, leaf_levels(): pl.pallas_call(leaf_kernel, in_specs=[pl.BlockSpec(memory_space=pltpu.SME...  5.16 us
    pallas_call x1, Pallas kernels, near_grams(): pl.pallas_call(near_kernel, in_specs=[pl.BlockSpec(memory_space=pltpu.SME...  4.87 us
    optimization_barrier x1, local copies, waits for them, and re-layouts, body(): lax.optimization_barrier((weights[0], upper_transfer))  4.16 us
    ppermute x10, waiting for transfers between devices, ring_swap(): return lax.ppermute(x, AXES, pairs)  3.72 us
  transfers between devices with their start and end apart: 31, of which 8 were waited for; matrix products, arithmetic and copies ran while one was open for 7% of the time, Pallas kernels for 19%

profile of v6, /device:TPU:0, one launch (start us, length us, event | category | flops | bytes accessed | tf_op | source)
XLA Modules:
  0.0 93.6 jit_solution(14813037854710114388)
XLA Ops:
  0.7 0.8 fusion
  1.5 0.1 pad_maximum_fusion.2.refs_0_
  1.5 2.1 %collective-permute-start = (bf16[2,64,128]{2,1,0:T(8,128)(2,1)S(1)}, bf16[2,64,128]{2,1,0:T(8,128)(2,1)S(1)}, u32[]{:S(2)}, u32[]{:S(2)}) collective-permute-start(bf16[2,64,128]{2,1,0:T(8,128)(2,1)S(1)} %pad_maximum_fusion.2.refs_0_), channel_id=1, source_target_pairs={{0,2},{1,9},{2,0},{3,11},{4,6},{5,13},{6,4},{7,15},{8,10},{9,1},{1... | collective-permute-start | bytes 98312 | tf_op jit(solution)/shard_map/ppermute | solution.py:169
  3.7 2.5 %collective-permute-start.1 = (bf16[2,64,128]{2,1,0:T(8,128)(2,1)S(1)}, bf16[2,64,128]{2,1,0:T(8,128)(2,1)S(1)}, u32[]{:S(2)}, u32[]{:S(2)}) collective-permute-start(bf16[2,64,128]{2,1,0:T(8,128)(2,1)S(1)} %pad_maximum_fusion.2.refs_0_), channel_id=1, source_target_pairs={{0,6},{1,25},{2,4},{3,27},{4,2},{5,29},{6,0},{7,31},{8,14},{9,17},... | collective-permute-start | bytes 98312 | tf_op jit(solution)/shard_map/ppermute | solution.py:169
  6.2 1.1 %collective-permute-start.2 = (bf16[2,64,128]{2,1,0:T(8,128)(2,1)S(1)}, bf16[2,64,128]{2,1,0:T(8,128)(2,1)S(1)}, u32[]{:S(2)}, u32[]{:S(2)}) collective-permute-start(bf16[2,64,128]{2,1,0:T(8,128)(2,1)S(1)} %pad_maximum_fusion.2.refs_0_), channel_id=1, source_target_pairs={{0,4},{1,17},{2,6},{3,19},{4,0},{5,21},{6,2},{7,23},{8,12},{9,25},... | collective-permute-start | bytes 98312 | tf_op jit(solution)/shard_map/ppermute | solution.py:169
  7.2 0.9 slice_bitcast_fusion.3
  8.1 0.6 collective-permute-start.10
  8.7 0.7 collective-permute-start.11
  9.4 0.1 slice.30
  9.5 0.1 slice.31
  9.7 1.9 %collective-permute-done.2.refs_3_ = bf16[2,64,128]{2,1,0:T(8,128)(2,1)S(1)} collective-permute-done((bf16[2,64,128]{2,1,0:T(8,128)(2,1)S(1)}, bf16[2,64,128]{2,1,0:T(8,128)(2,1)S(1)}, u32[]{:S(2)}, u32[]{:S(2)}) %collective-permute-start.2) | collective-permute-done | bytes 32800 | tf_op jit(solution)/shard_map/ppermute | solution.py:169
  11.6 1.7 %collective-permute-start.3 = (bf16[8,64,128]{2,1,0:T(8,128)(2,1)S(1)}, bf16[8,64,128]{2,1,0:T(8,128)(2,1)S(1)}, u32[]{:S(2)}, u32[]{:S(2)}) collective-permute-start(bf16[8,64,128]{2,1,0:T(8,128)(2,1)S(1)} %join.2.refs_0_), channel_id=1, source_target_pairs={{0,8},{1,33},{2,10},{3,35},{4,12},{5,37},{6,14},{7,39},{8,0},{9,41... | collective-permute-start | bytes 393224 | tf_op jit(solution)/shard_map/ppermute | solution.py:169
  13.3 3.0 %collective-permute-start.4 = (bf16[8,64,128]{2,1,0:T(8,128)(2,1)S(1)}, bf16[8,64,128]{2,1,0:T(8,128)(2,1)S(1)}, u32[]{:S(2)}, u32[]{:S(2)}) collective-permute-start(bf16[8,64,128]{2,1,0:T(8,128)(2,1)S(1)} %join.2.refs_0_), channel_id=1, source_target_pairs={{0,24},{1,97},{2,26},{3,99},{4,28},{5,101},{6,30},{7,103},{8,16},{... | collective-permute-start | bytes 393224 | tf_op jit(solution)/shard_map/ppermute | solution.py:169
  16.3 1.4 %collective-permute-start.5 = (bf16[8,64,128]{2,1,0:T(8,128)(2,1)S(1)}, bf16[8,64,128]{2,1,0:T(8,128)(2,1)S(1)}, u32[]{:S(2)}, u32[]{:S(2)}) collective-permute-start(bf16[8,64,128]{2,1,0:T(8,128)(2,1)S(1)} %join.2.refs_0_), channel_id=1, source_target_pairs={{0,16},{1,65},{2,18},{3,67},{4,20},{5,69},{6,22},{7,71},{8,24},{9,... | collective-permute-start | bytes 393224 | tf_op jit(solution)/shard_map/ppermute | solution.py:169
  17.8 2.5 %collective-permute-start.12 = (bf16[4,64,256]{2,1,0:T(8,128)(2,1)S(1)}, bf16[4,64,256]{2,1,0:T(8,128)(2,1)S(1)}, u32[]{:S(2)}, u32[]{:S(2)}) collective-permute-start(bf16[4,64,256]{2,1,0:T(8,128)(2,1)S(1)} %get-tuple-element.71), channel_id=1, source_target_pairs={{0,4},{1,5},{2,6},{3,7},{4,0},{5,1},{6,2},{7,3},{8,12},{9,13},{10,... | collective-permute-start | bytes 393224 | tf_op jit(solution)/shard_map/ppermute | solution.py:192
  20.3 0.7 collective-permute-start.13
  21.0 1.7 %collective-permute-done.5.refs_3_ = bf16[8,64,128]{2,1,0:T(8,128)(2,1)S(1)} collective-permute-done((bf16[8,64,128]{2,1,0:T(8,128)(2,1)S(1)}, bf16[8,64,128]{2,1,0:T(8,128)(2,1)S(1)}, u32[]{:S(2)}, u32[]{:S(2)}) %collective-permute-start.5) | collective-permute-done | bytes 131104 | tf_op jit(solution)/shard_map/ppermute | solution.py:169
  22.8 2.1 %collective-permute-start.6 = (bf16[32,64,128]{2,1,0:T(8,128)(2,1)S(1)}, bf16[32,64,128]{2,1,0:T(8,128)(2,1)S(1)}, u32[]{:S(2)}, u32[]{:S(2)}) collective-permute-start(bf16[32,64,128]{2,1,0:T(8,128)(2,1)S(1)} %join.3.rest_0_), channel_id=1, source_target_pairs={{0,32},{1,3},{2,34},{3,1},{4,36},{5,7},{6,38},{7,5},{8,40},{9,11},... | collective-permute-start | bytes 1572872 | tf_op jit(solution)/shard_map/ppermute | solution.py:169
  25.0 1.7 %collective-permute-start.7 = (bf16[32,64,128]{2,1,0:T(8,128)(2,1)S(1)}, bf16[32,64,128]{2,1,0:T(8,128)(2,1)}, u32[]{:S(2)}, u32[]{:S(2)}) collective-permute-start(bf16[32,64,128]{2,1,0:T(8,128)(2,1)S(1)} %join.3.rest_0_), channel_id=1, source_target_pairs={{0,96},{1,7},{2,98},{3,5},{4,100},{5,3},{6,102},{7,1},{8,104},{9,1... | collective-permute-start | bytes 1572872 | tf_op jit(solution)/shard_map/ppermute | solution.py:169
  26.6 0.9 pad_maximum_fusion.rest_0_
  27.5 5.4 %collective-permute-start.15 = (bf16[16,64,256]{2,1,0:T(8,128)(2,1)}, bf16[16,64,256]{2,1,0:T(8,128)(2,1)}, u32[]{:S(2)}, u32[]{:S(2)}) collective-permute-start(bf16[16,64,256]{2,1,0:T(8,128)(2,1)} %pad_maximum_fusion.rest_0_), channel_id=1, source_target_pairs={{0,0},{1,8},{2,2},{3,10},{4,4},{5,12},{6,6},{7,14},{8,1},{9,64},{1... | collective-permute-start | bytes 1572872 | tf_op jit(solution)/shard_map/ppermute | solution.py:192
  32.9 0.1 pad_add_fusion.nodes
  33.0 0.1 and_add_fusion
  33.1 0.1 reshape.16.halves
  33.1 0.1 reshape.17.tiles
  33.2 0.1 reshape.18.slots
  33.3 4.2 %copy.15.upper_transfer = bf16[126,64,64]{2,1,0:T(8,128)(2,1)S(1)} copy(bf16[126,64,64]{0,2,1:T(8,128)(2,1)} %param.23) | data formatting | bytes 2064384 | tf_op jit(solution)/shard_map/optimization_barrier | solution.py:494
  37.5 0.1 collective-permute-start.16
  37.6 0.8 select_transfers.1.transfers.rest_3_
  38.5 0.0 copy-start.5
  38.5 1.1 %part.2 = bf16[16,64,128]{2,1,0:T(8,128)(2,1)S(1)} custom-call(bf16[32,64,128]{2,1,0:T(8,128)(2,1)} %collective-permute-done.7.whole.rest_2_), custom_call_target="tpu_custom_call" | custom-call | tf_op jit(solution)/shard_map/part/pallas_call | solution.py:157
  39.6 4.6 %collective-permute-start.8 = (bf16[16,64,128]{2,1,0:T(8,128)(2,1)S(1)}, bf16[16,64,128]{2,1,0:T(8,128)(2,1)S(1)}, u32[]{:S(2)}, u32[]{:S(2)}) collective-permute-start(bf16[16,64,128]{2,1,0:T(8,128)(2,1)S(1)} %part.2), channel_id=1, source_target_pairs={{0,32},{1,3},{2,34},{3,1},{4,36},{5,7},{6,38},{7,5},{8,40},{9,11},... | collective-permute-start | bytes 786440 | tf_op jit(solution)/shard_map/ppermute | solution.py:169
  44.3 0.1 collective-permute-start.9
  44.4 1.8 %collective-permute-start.17 = (bf16[32,64,128]{2,1,0:T(8,128)(2,1)S(1)}, bf16[32,64,128]{2,1,0:T(8,128)(2,1)S(1)}, u32[]{:S(2)}, u32[]{:S(2)}) collective-permute-start(bf16[32,64,128]{2,1,0:T(8,128)(2,1)S(1)} %collective-permute-done.6.whole.rest_1_), channel_id=1, source_target_pairs={{0,1},{1,0},{2,3},{3,2},{4,5},{5,4},{6,7},{7,6},{8,9},{9,8},{10,11... | collective-permute-start | bytes 1572872 | tf_op jit(solution)/shard_map/ppermute | solution.py:202
  46.2 0.1 collective-permute-start.18
  46.3 2.2 %copy-done = bf16[4,8,256,256]{3,2,1,0:T(8,128)(2,1)S(1)} copy-done((bf16[4,8,256,256]{3,2,1,0:T(8,128)(2,1)S(1)}, bf16[4,8,256,256]{3,2,1,0:T(8,128)(2,1)}, u32[]{:S(2)}) %copy-start) | copy-done | bytes 4194328
  48.5 4.9 %near_grams.1.near_gram = f32[4,64,64]{2,1,0:T(8,128)S(1)} custom-call(s32[32]{0:T(128)S(1)} %reshape.18.slots, bf16[4,8,256,256]{3,2,1,0:T(8,128)(2,1)S(1)} %copy-done, bf16[4,64,256]{2,1,0:T(8,128)(2,1)S(1)} %copy-done.2, bf16[4,64,256]{2,1,0:T(8,128)(2,1)S(1)} %copy-done.3, bf16[16,64,256]{2,1,0:T(8,128)(2,1)} %pad_maximum_fusion.rest_0_, ...), custom_call_target="tpu_custom_call" | custom-call | tf_op jit(solution)/shard_map/near_grams/pallas_call | solution.py:281
  53.3 0.0 collective-permute-done.8.rest_3_
  53.4 0.5 collective-permute-start.19
  53.9 0.1 collective-permute-start.20
  54.0 1.1 %collective-permute-done.19.rest_8_ = bf16[16,64,128]{2,1,0:T(8,128)(2,1)S(1)} collective-permute-done((bf16[16,64,128]{2,1,0:T(8,128)(2,1)S(1)}, bf16[16,64,128]{2,1,0:T(8,128)(2,1)S(1)}, u32[]{:S(2)}, u32[]{:S(2)}) %collective-permute-start.19) | collective-permute-done | bytes 262176 | tf_op jit(solution)/shard_map/ppermute | solution.py:202
  55.0 0.4 collective-permute-done.20.rest_9_
  55.4 5.2 %leaf_levels.1 = (f32[4,64,64]{2,1,0:T(8,128)S(1)}, f32[3,64,64]{2,1,0:T(8,128)S(1)}, f32[64,64]{1,0:T(8,128)S(1)}) custom-call(s32[128]{0:T(128)S(1)} %reshape.17.tiles, s32[128]{0:T(128)S(1)} %reshape.16.halves, bf16[4,64,2048]{2,1,0:T(8,128)(2,1)S(1)} %copy-done.1, f32[4,64,64]{2,1,0:T(8,128)S(1)} %near_grams.1.near_gram, ...), custom_call_target="tpu_custom_call" | custom-call | tf_op jit(solution)/shard_map/leaf_levels/pallas_call | solution.py:373
  60.6 0.4 collective-permute-start.21
  61.0 0.9 collective-permute-done.21.other
  61.8 0.3 merge_pair.1
  62.1 1.6 %collective-permute-start.22 = (f32[64,64]{1,0:T(8,128)S(1)}, f32[64,64]{1,0:T(8,128)S(1)}, u32[]{:S(2)}, u32[]{:S(2)}) collective-permute-start(f32[64,64]{1,0:T(8,128)S(1)} %get-tuple-element.51.own), channel_id=1, source_target_pairs={{0,4},{1,5},{2,6},{3,7},{4,0},{5,1},{6,2},{7,3},{8,12},{9,13},{10,... | collective-permute-start | bytes 49160 | tf_op jit(solution)/shard_map/ppermute | solution.py:520
  63.7 1.4 %collective-permute-start.23 = (f32[64,64]{1,0:T(8,128)S(1)}, f32[64,64]{1,0:T(8,128)S(1)}, u32[]{:S(2)}, u32[]{:S(2)}) collective-permute-start(f32[64,64]{1,0:T(8,128)S(1)} %get-tuple-element.51.own), channel_id=1, source_target_pairs={{0,2},{1,3},{2,0},{3,1},{4,6},{5,7},{6,4},{7,5},{8,10},{9,11},{10,... | collective-permute-start | bytes 49160 | tf_op jit(solution)/shard_map/ppermute | solution.py:520
  65.1 1.2 %collective-permute-start.24 = (f32[64,64]{1,0:T(8,128)S(1)}, f32[64,64]{1,0:T(8,128)S(1)}, u32[]{:S(2)}, u32[]{:S(2)}) collective-permute-start(f32[64,64]{1,0:T(8,128)S(1)} %get-tuple-element.51.own), channel_id=1, source_target_pairs={{0,6},{1,7},{2,4},{3,5},{4,2},{5,3},{6,0},{7,1},{8,14},{9,15},{10,... | collective-permute-start | bytes 49160 | tf_op jit(solution)/shard_map/ppermute | solution.py:520
  66.2 3.7 %factor.3 = f32[4,64,64]{2,1,0:T(8,128)} custom-call(f32[4,64,64]{2,1,0:T(8,128)S(1)} %get-tuple-element.52.refs_0_), custom_call_target="tpu_custom_call" | custom-call | tf_op jit(solution)/shard_map/factor/pallas_call | solution.py:110
  69.9 0.2 collective-permute-done.24.rest_2_
  70.2 0.6 merge_quad.2
  70.8 2.3 %collective-permute-start.25 = (f32[64,64]{1,0:T(8,128)S(1)}, f32[64,64]{1,0:T(8,128)S(1)}, u32[]{:S(2)}, u32[]{:S(2)}) collective-permute-start(f32[64,64]{1,0:T(8,128)S(1)} %get-tuple-element.55.own), channel_id=1, source_target_pairs={{0,16},{1,17},{2,18},{3,19},{4,20},{5,21},{6,22},{7,23},{8,24},{9,... | collective-permute-start | bytes 49160 | tf_op jit(solution)/shard_map/ppermute | solution.py:520
  73.1 2.4 %collective-permute-start.26 = (f32[64,64]{1,0:T(8,128)S(1)}, f32[64,64]{1,0:T(8,128)S(1)}, u32[]{:S(2)}, u32[]{:S(2)}) collective-permute-start(f32[64,64]{1,0:T(8,128)S(1)} %get-tuple-element.55.own), channel_id=1, source_target_pairs={{0,8},{1,9},{2,10},{3,11},{4,12},{5,13},{6,14},{7,15},{8,0},{9,1},... | collective-permute-start | bytes 49160 | tf_op jit(solution)/shard_map/ppermute | solution.py:520
  75.5 0.6 collective-permute-start.27
  76.1 3.2 %factor.4 = f32[3,64,64]{2,1,0:T(8,128)} custom-call(f32[3,64,64]{2,1,0:T(8,128)S(1)} %get-tuple-element.56.refs_0_), custom_call_target="tpu_custom_call" | custom-call | tf_op jit(solution)/shard_map/factor/pallas_call | solution.py:110
  79.3 1.3 %collective-permute-done.27.rest_2_ = f32[64,64]{1,0:T(8,128)S(1)} collective-permute-done((f32[64,64]{1,0:T(8,128)S(1)}, f32[64,64]{1,0:T(8,128)S(1)}, u32[]{:S(2)}, u32[]{:S(2)}) %collective-permute-start.27) | collective-permute-done | bytes 16416 | tf_op jit(solution)/shard_map/ppermute | solution.py:520
  80.6 0.6 merge_quad.3
  81.2 2.7 %collective-permute-start.29 = (f32[64,64]{1,0:T(8,128)S(1)}, f32[64,64]{1,0:T(8,128)S(1)}, u32[]{:S(2)}, u32[]{:S(2)}) collective-permute-start(f32[64,64]{1,0:T(8,128)S(1)} %get-tuple-element.59.own), channel_id=1, source_target_pairs={{0,64},{1,65},{2,66},{3,67},{4,68},{5,69},{6,70},{7,71},{8,72},{9,... | collective-permute-start | bytes 49160 | tf_op jit(solution)/shard_map/ppermute | solution.py:520
  84.0 1.3 %collective-permute-start.28 = (f32[64,64]{1,0:T(8,128)S(1)}, f32[64,64]{1,0:T(8,128)S(1)}, u32[]{:S(2)}, u32[]{:S(2)}) collective-permute-start(f32[64,64]{1,0:T(8,128)S(1)} %get-tuple-element.59.own), channel_id=1, source_target_pairs={{0,32},{1,33},{2,34},{3,35},{4,36},{5,37},{6,38},{7,39},{8,40},{9,... | collective-permute-start | bytes 49160 | tf_op jit(solution)/shard_map/ppermute | solution.py:520
  85.2 0.7 collective-permute-start.30
  85.9 3.6 %factor.5.rest_4_ = f32[5,64,64]{2,1,0:T(8,128)S(1)} custom-call(f32[64,64]{1,0:T(8,128)S(1)} %get-tuple-element.60.refs_0_, f32[64,64]{1,0:T(8,128)S(1)} %get-tuple-element.61.refs_1_, f32[64,64]{1,0:T(8,128)S(1)} %get-tuple-element.62.refs_2_, f32[64,64]{1,0:T(8,128)S(1)} %get-tuple-element.63.refs_3_, f32[64,64]{1,0:T(8,128)S(1)} %get-tuple-element.64.refs_4_), custom_call_target="tpu_custom_call" | custom-call | tf_op jit(solution)/shard_map/factor/pallas_call | solution.py:110
  89.5 0.8 collective-permute-done.30.rest_2_
  90.4 3.2 %factor_root.1 = f32[7,64,64]{2,1,0:T(8,128)} custom-call(f32[64,64]{1,0:T(8,128)S(1)} %get-tuple-element.59.own, f32[64,64]{1,0:T(8,128)S(1)} %collective-permute-done.28.rest_0_, f32[64,64]{1,0:T(8,128)S(1)} %collective-permute-done.29.rest_1_, f32[64,64]{1,0:T(8,128)S(1)} %collective-permute-done.30.rest_2_, ...), custom_call_target="tpu_custom_call" | custom-call | tf_op jit(solution)/shard_map/factor_root/pallas_call | solution.py:453
  (52 shorter events, 0.3 us)
Async XLA Ops:
  0.6 32.6 %copy-start.6 = (s32[4,8]{1,0:T(4,128)S(1)}, s32[4,8]{1,0:T(4,128)}, u32[]{:S(2)}) copy-start(s32[4,8]{1,0:T(4,128)} %param.13) | copy-start | bytes 388
  0.6 32.3 %copy-start.7 = (s32[4,32]{1,0:T(4,128)S(1)}, s32[4,32]{1,0:T(4,128)}, u32[]{:S(2)}) copy-start(s32[4,32]{1,0:T(4,128)} %param.19) | copy-start | bytes 1540
  0.7 32.3 %copy-start.8 = (s32[4]{0:T(128)S(1)}, s32[4]{0:T(128)}, u32[]{:S(2)}) copy-start(s32[4]{0:T(128)} %param.20) | copy-start | bytes 52
  1.5 8.1 %collective-permute-start = (bf16[2,64,128]{2,1,0:T(8,128)(2,1)S(1)}, bf16[2,64,128]{2,1,0:T(8,128)(2,1)S(1)}, u32[]{:S(2)}, u32[]{:S(2)}) collective-permute-start(bf16[2,64,128]{2,1,0:T(8,128)(2,1)S(1)} %pad_maximum_fusion.2.refs_0_), channel_id=1, source_target_pairs={{0,2},{1,9},{2,0},{3,11},{4,6},{5,13},{6,4},{7,15},{8,10},{9,1},{1... | collective-permute-start | bytes 98312 | tf_op jit(solution)/shard_map/ppermute | solution.py:169
  3.7 6.0 %collective-permute-start.1 = (bf16[2,64,128]{2,1,0:T(8,128)(2,1)S(1)}, bf16[2,64,128]{2,1,0:T(8,128)(2,1)S(1)}, u32[]{:S(2)}, u32[]{:S(2)}) collective-permute-start(bf16[2,64,128]{2,1,0:T(8,128)(2,1)S(1)} %pad_maximum_fusion.2.refs_0_), channel_id=1, source_target_pairs={{0,6},{1,25},{2,4},{3,27},{4,2},{5,29},{6,0},{7,31},{8,14},{9,17},... | collective-permute-start | bytes 98312 | tf_op jit(solution)/shard_map/ppermute | solution.py:169
  6.2 5.4 %collective-permute-start.2 = (bf16[2,64,128]{2,1,0:T(8,128)(2,1)S(1)}, bf16[2,64,128]{2,1,0:T(8,128)(2,1)S(1)}, u32[]{:S(2)}, u32[]{:S(2)}) collective-permute-start(bf16[2,64,128]{2,1,0:T(8,128)(2,1)S(1)} %pad_maximum_fusion.2.refs_0_), channel_id=1, source_target_pairs={{0,4},{1,17},{2,6},{3,19},{4,0},{5,21},{6,2},{7,23},{8,12},{9,25},... | collective-permute-start | bytes 98312 | tf_op jit(solution)/shard_map/ppermute | solution.py:169
  8.1 9.5 %collective-permute-start.10 = (bf16[2,64,256]{2,1,0:T(8,128)(2,1)S(1)}, bf16[2,64,256]{2,1,0:T(8,128)(2,1)S(1)}, u32[]{:S(2)}, u32[]{:S(2)}) collective-permute-start(bf16[2,64,256]{2,1,0:T(8,128)(2,1)S(1)} %get-tuple-element.78), channel_id=1, source_target_pairs={{0,2},{1,3},{2,0},{3,1},{4,6},{5,7},{6,4},{7,5},{8,10},{9,11},{10,... | collective-permute-start | bytes 196616 | tf_op jit(solution)/shard_map/ppermute | solution.py:192
  8.7 9.0 %collective-permute-start.11 = (bf16[2,64,256]{2,1,0:T(8,128)(2,1)S(1)}, bf16[2,64,256]{2,1,0:T(8,128)(2,1)S(1)}, u32[]{:S(2)}, u32[]{:S(2)}) collective-permute-start(bf16[2,64,256]{2,1,0:T(8,128)(2,1)S(1)} %get-tuple-element.76), channel_id=1, source_target_pairs={{0,0},{1,1},{2,16},{3,17},{4,4},{5,5},{6,20},{7,21},{8,8},{9,9},{1... | collective-permute-start | bytes 196616 | tf_op jit(solution)/shard_map/ppermute | solution.py:192
  11.6 9.4 %collective-permute-start.3 = (bf16[8,64,128]{2,1,0:T(8,128)(2,1)S(1)}, bf16[8,64,128]{2,1,0:T(8,128)(2,1)S(1)}, u32[]{:S(2)}, u32[]{:S(2)}) collective-permute-start(bf16[8,64,128]{2,1,0:T(8,128)(2,1)S(1)} %join.2.refs_0_), channel_id=1, source_target_pairs={{0,8},{1,33},{2,10},{3,35},{4,12},{5,37},{6,14},{7,39},{8,0},{9,41... | collective-permute-start | bytes 393224 | tf_op jit(solution)/shard_map/ppermute | solution.py:169
  13.3 7.8 %collective-permute-start.4 = (bf16[8,64,128]{2,1,0:T(8,128)(2,1)S(1)}, bf16[8,64,128]{2,1,0:T(8,128)(2,1)S(1)}, u32[]{:S(2)}, u32[]{:S(2)}) collective-permute-start(bf16[8,64,128]{2,1,0:T(8,128)(2,1)S(1)} %join.2.refs_0_), channel_id=1, source_target_pairs={{0,24},{1,97},{2,26},{3,99},{4,28},{5,101},{6,30},{7,103},{8,16},{... | collective-permute-start | bytes 393224 | tf_op jit(solution)/shard_map/ppermute | solution.py:169
  16.3 6.5 %collective-permute-start.5 = (bf16[8,64,128]{2,1,0:T(8,128)(2,1)S(1)}, bf16[8,64,128]{2,1,0:T(8,128)(2,1)S(1)}, u32[]{:S(2)}, u32[]{:S(2)}) collective-permute-start(bf16[8,64,128]{2,1,0:T(8,128)(2,1)S(1)} %join.2.refs_0_), channel_id=1, source_target_pairs={{0,16},{1,65},{2,18},{3,67},{4,20},{5,69},{6,22},{7,71},{8,24},{9,... | collective-permute-start | bytes 393224 | tf_op jit(solution)/shard_map/ppermute | solution.py:169
  17.8 8.8 %collective-permute-start.12 = (bf16[4,64,256]{2,1,0:T(8,128)(2,1)S(1)}, bf16[4,64,256]{2,1,0:T(8,128)(2,1)S(1)}, u32[]{:S(2)}, u32[]{:S(2)}) collective-permute-start(bf16[4,64,256]{2,1,0:T(8,128)(2,1)S(1)} %get-tuple-element.71), channel_id=1, source_target_pairs={{0,4},{1,5},{2,6},{3,7},{4,0},{5,1},{6,2},{7,3},{8,12},{9,13},{10,... | collective-permute-start | bytes 393224 | tf_op jit(solution)/shard_map/ppermute | solution.py:192
  20.3 6.3 %collective-permute-start.13 = (bf16[4,64,256]{2,1,0:T(8,128)(2,1)S(1)}, bf16[4,64,256]{2,1,0:T(8,128)(2,1)S(1)}, u32[]{:S(2)}, u32[]{:S(2)}) collective-permute-start(bf16[4,64,256]{2,1,0:T(8,128)(2,1)S(1)} %get-tuple-element.72), channel_id=1, source_target_pairs={{0,0},{1,1},{2,2},{3,3},{4,32},{5,33},{6,34},{7,35},{8,8},{9,9},{1... | collective-permute-start | bytes 393224 | tf_op jit(solution)/shard_map/ppermute | solution.py:192
  22.8 23.5 %copy-start.2 = (bf16[4,64,256]{2,1,0:T(8,128)(2,1)S(1)}, bf16[4,64,256]{2,1,0:T(8,128)(2,1)}, u32[]{:S(2)}) copy-start(bf16[4,64,256]{2,1,0:T(8,128)(2,1)} %samples.1) | copy-start | bytes 393220
  22.8 23.4 %copy-start.3 = (bf16[4,64,256]{2,1,0:T(8,128)(2,1)S(1)}, bf16[4,64,256]{2,1,0:T(8,128)(2,1)}, u32[]{:S(2)}) copy-start(bf16[4,64,256]{2,1,0:T(8,128)(2,1)} %basis.1) | copy-start | bytes 393220
  22.8 15.6 %collective-permute-start.6 = (bf16[32,64,128]{2,1,0:T(8,128)(2,1)S(1)}, bf16[32,64,128]{2,1,0:T(8,128)(2,1)S(1)}, u32[]{:S(2)}, u32[]{:S(2)}) collective-permute-start(bf16[32,64,128]{2,1,0:T(8,128)(2,1)S(1)} %join.3.rest_0_), channel_id=1, source_target_pairs={{0,32},{1,3},{2,34},{3,1},{4,36},{5,7},{6,38},{7,5},{8,40},{9,11},... | collective-permute-start | bytes 1572872 | tf_op jit(solution)/shard_map/ppermute | solution.py:169
  25.0 13.5 %collective-permute-start.7 = (bf16[32,64,128]{2,1,0:T(8,128)(2,1)S(1)}, bf16[32,64,128]{2,1,0:T(8,128)(2,1)}, u32[]{:S(2)}, u32[]{:S(2)}) collective-permute-start(bf16[32,64,128]{2,1,0:T(8,128)(2,1)S(1)} %join.3.rest_0_), channel_id=1, source_target_pairs={{0,96},{1,7},{2,98},{3,5},{4,100},{5,3},{6,102},{7,1},{8,104},{9,1... | collective-permute-start | bytes 1572872 | tf_op jit(solution)/shard_map/ppermute | solution.py:169
  27.5 16.8 %collective-permute-start.14 = (bf16[16,64,256]{2,1,0:T(8,128)(2,1)}, bf16[16,64,256]{2,1,0:T(8,128)(2,1)}, u32[]{:S(2)}, u32[]{:S(2)}) collective-permute-start(bf16[16,64,256]{2,1,0:T(8,128)(2,1)} %pad_maximum_fusion.rest_0_), channel_id=1, source_target_pairs={{0,1},{1,0},{2,3},{3,2},{4,5},{5,4},{6,7},{7,6},{8,9},{9,8},{10,11... | collective-permute-start | bytes 1572872 | tf_op jit(solution)/shard_map/ppermute | solution.py:202
  27.5 18.6 %collective-permute-start.15 = (bf16[16,64,256]{2,1,0:T(8,128)(2,1)}, bf16[16,64,256]{2,1,0:T(8,128)(2,1)}, u32[]{:S(2)}, u32[]{:S(2)}) collective-permute-start(bf16[16,64,256]{2,1,0:T(8,128)(2,1)} %pad_maximum_fusion.rest_0_), channel_id=1, source_target_pairs={{0,0},{1,8},{2,2},{3,10},{4,4},{5,12},{6,6},{7,14},{8,1},{9,64},{1... | collective-permute-start | bytes 1572872 | tf_op jit(solution)/shard_map/ppermute | solution.py:192
  37.5 16.5 %collective-permute-start.16 = (bf16[32,64,128]{2,1,0:T(8,128)(2,1)S(1)}, bf16[32,64,128]{2,1,0:T(8,128)(2,1)S(1)}, u32[]{:S(2)}, u32[]{:S(2)}) collective-permute-start(bf16[32,64,128]{2,1,0:T(8,128)(2,1)S(1)} %join.3.rest_0_), channel_id=1, source_target_pairs={{0,1},{1,0},{2,3},{3,2},{4,5},{5,4},{6,7},{7,6},{8,9},{9,8},{10,11... | collective-permute-start | bytes 1572872 | tf_op jit(solution)/shard_map/ppermute | solution.py:202
  38.4 17.0 %copy-start.1 = (bf16[4,64,2048]{2,1,0:T(8,128)(2,1)S(1)}, bf16[4,64,2048]{2,1,0:T(8,128)(2,1)}, u32[]{:S(2)}) copy-start(bf16[4,64,2048]{2,1,0:T(8,128)(2,1)} %coupling.1) | copy-start | bytes 3145732
  38.4 17.0 %copy-start.4 = (bf16[4,64,64]{2,1,0:T(8,128)(2,1)S(1)}, bf16[4,64,64]{2,1,0:T(8,128)(2,1)}, u32[]{:S(2)}) copy-start(bf16[4,64,64]{2,1,0:T(8,128)(2,1)} %leaf_transfer.1) | copy-start | bytes 98308
  38.5 17.0 %copy-start.5 = (bf16[1,3,64,64]{3,2,1,0:T(8,128)(2,1)S(1)}, bf16[1,3,64,64]{3,2,1,0:T(8,128)(2,1)}, u32[]{:S(2)}) copy-start(bf16[1,3,64,64]{3,2,1,0:T(8,128)(2,1)} %inner_transfer.1) | copy-start | bytes 73732
  39.6 13.7 %collective-permute-start.8 = (bf16[16,64,128]{2,1,0:T(8,128)(2,1)S(1)}, bf16[16,64,128]{2,1,0:T(8,128)(2,1)S(1)}, u32[]{:S(2)}, u32[]{:S(2)}) collective-permute-start(bf16[16,64,128]{2,1,0:T(8,128)(2,1)S(1)} %part.2), channel_id=1, source_target_pairs={{0,32},{1,3},{2,34},{3,1},{4,36},{5,7},{6,38},{7,5},{8,40},{9,11},... | collective-permute-start | bytes 786440 | tf_op jit(solution)/shard_map/ppermute | solution.py:169
  44.3 9.1 %collective-permute-start.9 = (bf16[16,64,128]{2,1,0:T(8,128)(2,1)S(1)}, bf16[16,64,128]{2,1,0:T(8,128)(2,1)S(1)}, u32[]{:S(2)}, u32[]{:S(2)}) collective-permute-start(bf16[16,64,128]{2,1,0:T(8,128)(2,1)S(1)} %part.3), channel_id=1, source_target_pairs={{0,96},{1,7},{2,98},{3,5},{4,100},{5,3},{6,102},{7,1},{8,104},{9,1... | collective-permute-start | bytes 786440 | tf_op jit(solution)/shard_map/ppermute | solution.py:169
  44.4 9.6 %collective-permute-start.17 = (bf16[32,64,128]{2,1,0:T(8,128)(2,1)S(1)}, bf16[32,64,128]{2,1,0:T(8,128)(2,1)S(1)}, u32[]{:S(2)}, u32[]{:S(2)}) collective-permute-start(bf16[32,64,128]{2,1,0:T(8,128)(2,1)S(1)} %collective-permute-done.6.whole.rest_1_), channel_id=1, source_target_pairs={{0,1},{1,0},{2,3},{3,2},{4,5},{5,4},{6,7},{7,6},{8,9},{9,8},{10,11... | collective-permute-start | bytes 1572872 | tf_op jit(solution)/shard_map/ppermute | solution.py:202
  46.2 7.8 %collective-permute-start.18 = (bf16[32,64,128]{2,1,0:T(8,128)(2,1)}, bf16[32,64,128]{2,1,0:T(8,128)(2,1)S(1)}, u32[]{:S(2)}, u32[]{:S(2)}) collective-permute-start(bf16[32,64,128]{2,1,0:T(8,128)(2,1)} %collective-permute-done.7.whole.rest_2_), channel_id=1, source_target_pairs={{0,1},{1,0},{2,3},{3,2},{4,5},{5,4},{6,7},{7,6},{8,9},{9,8},{10,11... | collective-permute-start | bytes 1572872 | tf_op jit(solution)/shard_map/ppermute | solution.py:202
  46.3 2.2 %copy-start = (bf16[4,8,256,256]{3,2,1,0:T(8,128)(2,1)S(1)}, bf16[4,8,256,256]{3,2,1,0:T(8,128)(2,1)}, u32[]{:S(2)}) copy-start(bf16[4,8,256,256]{3,2,1,0:T(8,128)(2,1)} %blocks.1) | copy-start | bytes 12582916
  53.4 1.7 %collective-permute-start.19 = (bf16[16,64,128]{2,1,0:T(8,128)(2,1)S(1)}, bf16[16,64,128]{2,1,0:T(8,128)(2,1)S(1)}, u32[]{:S(2)}, u32[]{:S(2)}) collective-permute-start(bf16[16,64,128]{2,1,0:T(8,128)(2,1)S(1)} %collective-permute-done.8.rest_3_), channel_id=1, source_target_pairs={{0,1},{1,0},{2,3},{3,2},{4,5},{5,4},{6,7},{7,6},{8,9},{9,8},{10,11... | collective-permute-start | bytes 786440 | tf_op jit(solution)/shard_map/ppermute | solution.py:202
  53.9 1.5 %collective-permute-start.20 = (bf16[16,64,128]{2,1,0:T(8,128)(2,1)S(1)}, bf16[16,64,128]{2,1,0:T(8,128)(2,1)S(1)}, u32[]{:S(2)}, u32[]{:S(2)}) collective-permute-start(bf16[16,64,128]{2,1,0:T(8,128)(2,1)S(1)} %collective-permute-done.9.rest_4_), channel_id=1, source_target_pairs={{0,1},{1,0},{2,3},{3,2},{4,5},{5,4},{6,7},{7,6},{8,9},{9,8},{10,11... | collective-permute-start | bytes 786440 | tf_op jit(solution)/shard_map/ppermute | solution.py:202
  60.6 1.2 %collective-permute-start.21 = (f32[64,64]{1,0:T(8,128)S(1)}, f32[64,64]{1,0:T(8,128)S(1)}, u32[]{:S(2)}, u32[]{:S(2)}) collective-permute-start(f32[64,64]{1,0:T(8,128)S(1)} %get-tuple-element.49.own), channel_id=1, source_target_pairs={{0,1},{1,0},{2,3},{3,2},{4,5},{5,4},{6,7},{7,6},{8,9},{9,8},{10,11... | collective-permute-start | bytes 49160 | tf_op jit(solution)/shard_map/ppermute | solution.py:520
  62.1 7.8 %collective-permute-start.22 = (f32[64,64]{1,0:T(8,128)S(1)}, f32[64,64]{1,0:T(8,128)S(1)}, u32[]{:S(2)}, u32[]{:S(2)}) collective-permute-start(f32[64,64]{1,0:T(8,128)S(1)} %get-tuple-element.51.own), channel_id=1, source_target_pairs={{0,4},{1,5},{2,6},{3,7},{4,0},{5,1},{6,2},{7,3},{8,12},{9,13},{10,... | collective-permute-start | bytes 49160 | tf_op jit(solution)/shard_map/ppermute | solution.py:520
  63.7 6.3 %collective-permute-start.23 = (f32[64,64]{1,0:T(8,128)S(1)}, f32[64,64]{1,0:T(8,128)S(1)}, u32[]{:S(2)}, u32[]{:S(2)}) collective-permute-start(f32[64,64]{1,0:T(8,128)S(1)} %get-tuple-element.51.own), channel_id=1, source_target_pairs={{0,2},{1,3},{2,0},{3,1},{4,6},{5,7},{6,4},{7,5},{8,10},{9,11},{10,... | collective-permute-start | bytes 49160 | tf_op jit(solution)/shard_map/ppermute | solution.py:520
  65.1 5.1 %collective-permute-start.24 = (f32[64,64]{1,0:T(8,128)S(1)}, f32[64,64]{1,0:T(8,128)S(1)}, u32[]{:S(2)}, u32[]{:S(2)}) collective-permute-start(f32[64,64]{1,0:T(8,128)S(1)} %get-tuple-element.51.own), channel_id=1, source_target_pairs={{0,6},{1,7},{2,4},{3,5},{4,2},{5,3},{6,0},{7,1},{8,14},{9,15},{10,... | collective-permute-start | bytes 49160 | tf_op jit(solution)/shard_map/ppermute | solution.py:520
  70.8 8.5 %collective-permute-start.25 = (f32[64,64]{1,0:T(8,128)S(1)}, f32[64,64]{1,0:T(8,128)S(1)}, u32[]{:S(2)}, u32[]{:S(2)}) collective-permute-start(f32[64,64]{1,0:T(8,128)S(1)} %get-tuple-element.55.own), channel_id=1, source_target_pairs={{0,16},{1,17},{2,18},{3,19},{4,20},{5,21},{6,22},{7,23},{8,24},{9,... | collective-permute-start | bytes 49160 | tf_op jit(solution)/shard_map/ppermute | solution.py:520
  73.1 6.2 %collective-permute-start.26 = (f32[64,64]{1,0:T(8,128)S(1)}, f32[64,64]{1,0:T(8,128)S(1)}, u32[]{:S(2)}, u32[]{:S(2)}) collective-permute-start(f32[64,64]{1,0:T(8,128)S(1)} %get-tuple-element.55.own), channel_id=1, source_target_pairs={{0,8},{1,9},{2,10},{3,11},{4,12},{5,13},{6,14},{7,15},{8,0},{9,1},... | collective-permute-start | bytes 49160 | tf_op jit(solution)/shard_map/ppermute | solution.py:520
  75.5 5.1 %collective-permute-start.27 = (f32[64,64]{1,0:T(8,128)S(1)}, f32[64,64]{1,0:T(8,128)S(1)}, u32[]{:S(2)}, u32[]{:S(2)}) collective-permute-start(f32[64,64]{1,0:T(8,128)S(1)} %get-tuple-element.55.own), channel_id=1, source_target_pairs={{0,24},{1,25},{2,26},{3,27},{4,28},{5,29},{6,30},{7,31},{8,16},{9,... | collective-permute-start | bytes 49160 | tf_op jit(solution)/shard_map/ppermute | solution.py:520
  81.2 8.3 %collective-permute-start.29 = (f32[64,64]{1,0:T(8,128)S(1)}, f32[64,64]{1,0:T(8,128)S(1)}, u32[]{:S(2)}, u32[]{:S(2)}) collective-permute-start(f32[64,64]{1,0:T(8,128)S(1)} %get-tuple-element.59.own), channel_id=1, source_target_pairs={{0,64},{1,65},{2,66},{3,67},{4,68},{5,69},{6,70},{7,71},{8,72},{9,... | collective-permute-start | bytes 49160 | tf_op jit(solution)/shard_map/ppermute | solution.py:520
  84.0 5.6 %collective-permute-start.28 = (f32[64,64]{1,0:T(8,128)S(1)}, f32[64,64]{1,0:T(8,128)S(1)}, u32[]{:S(2)}, u32[]{:S(2)}) collective-permute-start(f32[64,64]{1,0:T(8,128)S(1)} %get-tuple-element.59.own), channel_id=1, source_target_pairs={{0,32},{1,33},{2,34},{3,35},{4,36},{5,37},{6,38},{7,39},{8,40},{9,... | collective-permute-start | bytes 49160 | tf_op jit(solution)/shard_map/ppermute | solution.py:520
  85.2 5.1 %collective-permute-start.30 = (f32[64,64]{1,0:T(8,128)S(1)}, f32[64,64]{1,0:T(8,128)S(1)}, u32[]{:S(2)}, u32[]{:S(2)}) collective-permute-start(f32[64,64]{1,0:T(8,128)S(1)} %get-tuple-element.59.own), channel_id=1, source_target_pairs={{0,96},{1,97},{2,98},{3,99},{4,100},{5,101},{6,102},{7,103},{8,104... | collective-permute-start | bytes 49160 | tf_op jit(solution)/shard_map/ppermute | solution.py:520

commit v7 on v6

--- a/solution.py
+++ b/solution.py
@@ -253,10 +253,17 @@
 
 
 def near_kernel(slots, blocks, samples, basis, *rest):
-    pieces, (gram, vectors) = rest[:3], rest[3:]
+    pieces, (gram, vectors, held, semaphores) = rest[:3], rest[3:]
+    copies = [
+        pltpu.make_async_copy(blocks.at[leaf], held.at[leaf], semaphores.at[leaf])
+        for leaf in range(blocks.shape[0])
+    ]
+    for copy in copies:
+        copy.start()
     join_pieces(pieces, vectors)
-    for leaf in range(blocks.shape[0]):
-        near_leaf(leaf, slots, blocks, samples, basis, vectors, gram)
+    for leaf, copy in enumerate(copies):
+        copy.wait()
+        near_leaf(leaf, slots, held, samples, basis, vectors, gram)
 
 
 def near_leaf(leaf, slots, blocks, samples, basis, vectors, gram):
@@ -280,15 +287,20 @@
     vmem = pl.BlockSpec(memory_space=pltpu.VMEM)
     return pl.pallas_call(
         near_kernel,
-        in_specs=[pl.BlockSpec(memory_space=pltpu.SMEM)] + [vmem] * (3 + len(pieces)),
+        in_specs=[pl.BlockSpec(memory_space=pltpu.SMEM), pl.BlockSpec(memory_space=pltpu.HBM)]
+        + [vmem] * (2 + len(pieces)),
         out_specs=vmem,
         out_shape=pltpu.VMEM((count, rank, rank), jnp.float32),
-        scratch_shapes=[pltpu.VMEM((48, rank, size), jnp.bfloat16)],
-        compiler_params=limit(8),
+        scratch_shapes=[
+            pltpu.VMEM((48, rank, size), jnp.bfloat16),
+            pltpu.VMEM(near_blocks.shape, near_blocks.dtype),
+            pltpu.SemaphoreType.DMA((count,)),
+        ],
+        compiler_params=limit(12),
         name="near_grams",
     )(
         slots,
-        in_vmem(near_blocks),
+        pltpu.with_memory_space_constraint(near_blocks, pltpu.HBM),
         in_vmem(samples),
         in_vmem(leaf_basis),
         *[in_vmem(piece) for piece in pieces],

time: 94.3 us -> 93.6 us (level)
  local copies, waits for them, and re-layouts: 7.64 us -> 5.46 us
  Pallas kernels: 27.3 us -> 28.9 us
    unnamed x18 -> x16, local copies, waits for them, and re-layouts: 2.23 us -> 0.04 us
    pallas_call x1, Pallas kernels: 4.87 us -> 6.47 us  [near_grams(): pl.pallas_call(near_kernel, in_specs=[pl.BlockSpec(memory_space=pltpu.SME...]
  transfers between devices with their start and end apart: 31 -> 31, of which waited for: 8 -> 8; matrix products, arithmetic and copies ran while one was open for 7% -> 7% of each run, Pallas kernels for 19% -> 20%
where the time goes in v7:
time: 93.6 us; the launch traced here: 93 us
  starting transfers between devices  47.3 us (51%)
  Pallas kernels  28.9 us (31%)
  waiting for transfers between devices  8.24 us (9%)
  local copies, waits for them, and re-layouts  5.46 us (6%)
  other arithmetic  2.14 us (2%)
  between operations  0.98 us (1%)
    ppermute x10, starting transfers between devices, ring_swap(): return lax.ppermute(x, AXES, pairs)  20.2 us
    ppermute x10, starting transfers between devices, swapped_with(): return lax.ppermute(x, AXES, [(d, d ^ flip) for d in range(devices)])  14.7 us
    pallas_call x3, Pallas kernels, factor(): pl.pallas_call(factor_kernel, in_specs=[vmem] * len(grams), out_specs=vme...  10.5 us
    ppermute x5, starting transfers between devices, grid_swap(): return lax.ppermute(x, AXES, pairs)  9.8 us
    pallas_call x1, Pallas kernels, near_grams(): pl.pallas_call(near_kernel, in_specs=[pl.BlockSpec(memory_space=pltpu.SME...  6.47 us
    pallas_call x1, Pallas kernels, leaf_levels(): pl.pallas_call(leaf_kernel, in_specs=[pl.BlockSpec(memory_space=pltpu.SME...  5.16 us
    optimization_barrier x1, local copies, waits for them, and re-layouts, body(): lax.optimization_barrier((weights[0], upper_transfer))  4.16 us
    ppermute x10, waiting for transfers between devices, ring_swap(): return lax.ppermute(x, AXES, pairs)  3.71 us
  transfers between devices with their start and end apart: 31, of which 8 were waited for; matrix products, arithmetic and copies ran while one was open for 7% of the time, Pallas kernels for 20%

profile of v7, /device:TPU:0, one launch (start us, length us, event | category | flops | bytes accessed | tf_op | source)
XLA Modules:
  0.0 93.0 jit_solution(17298175450527336992)
XLA Ops:
  0.7 0.8 fusion
  1.5 0.1 pad_maximum_fusion.2.refs_0_
  1.5 2.1 %collective-permute-start = (bf16[2,64,128]{2,1,0:T(8,128)(2,1)S(1)}, bf16[2,64,128]{2,1,0:T(8,128)(2,1)S(1)}, u32[]{:S(2)}, u32[]{:S(2)}) collective-permute-start(bf16[2,64,128]{2,1,0:T(8,128)(2,1)S(1)} %pad_maximum_fusion.2.refs_0_), channel_id=1, source_target_pairs={{0,2},{1,9},{2,0},{3,11},{4,6},{5,13},{6,4},{7,15},{8,10},{9,1},{1... | collective-permute-start | bytes 98312 | tf_op jit(solution)/shard_map/ppermute | solution.py:169
  3.7 2.5 %collective-permute-start.1 = (bf16[2,64,128]{2,1,0:T(8,128)(2,1)S(1)}, bf16[2,64,128]{2,1,0:T(8,128)(2,1)S(1)}, u32[]{:S(2)}, u32[]{:S(2)}) collective-permute-start(bf16[2,64,128]{2,1,0:T(8,128)(2,1)S(1)} %pad_maximum_fusion.2.refs_0_), channel_id=1, source_target_pairs={{0,6},{1,25},{2,4},{3,27},{4,2},{5,29},{6,0},{7,31},{8,14},{9,17},... | collective-permute-start | bytes 98312 | tf_op jit(solution)/shard_map/ppermute | solution.py:169
  6.2 1.1 %collective-permute-start.2 = (bf16[2,64,128]{2,1,0:T(8,128)(2,1)S(1)}, bf16[2,64,128]{2,1,0:T(8,128)(2,1)S(1)}, u32[]{:S(2)}, u32[]{:S(2)}) collective-permute-start(bf16[2,64,128]{2,1,0:T(8,128)(2,1)S(1)} %pad_maximum_fusion.2.refs_0_), channel_id=1, source_target_pairs={{0,4},{1,17},{2,6},{3,19},{4,0},{5,21},{6,2},{7,23},{8,12},{9,25},... | collective-permute-start | bytes 98312 | tf_op jit(solution)/shard_map/ppermute | solution.py:169
  7.2 0.9 slice_bitcast_fusion.3
  8.1 0.6 collective-permute-start.10
  8.7 0.7 collective-permute-start.11
  9.4 0.1 slice.30
  9.5 0.1 slice.31
  9.7 1.9 %collective-permute-done.2.refs_3_ = bf16[2,64,128]{2,1,0:T(8,128)(2,1)S(1)} collective-permute-done((bf16[2,64,128]{2,1,0:T(8,128)(2,1)S(1)}, bf16[2,64,128]{2,1,0:T(8,128)(2,1)S(1)}, u32[]{:S(2)}, u32[]{:S(2)}) %collective-permute-start.2) | collective-permute-done | bytes 32800 | tf_op jit(solution)/shard_map/ppermute | solution.py:169
  11.6 1.7 %collective-permute-start.3 = (bf16[8,64,128]{2,1,0:T(8,128)(2,1)S(1)}, bf16[8,64,128]{2,1,0:T(8,128)(2,1)S(1)}, u32[]{:S(2)}, u32[]{:S(2)}) collective-permute-start(bf16[8,64,128]{2,1,0:T(8,128)(2,1)S(1)} %join.2.refs_0_), channel_id=1, source_target_pairs={{0,8},{1,33},{2,10},{3,35},{4,12},{5,37},{6,14},{7,39},{8,0},{9,41... | collective-permute-start | bytes 393224 | tf_op jit(solution)/shard_map/ppermute | solution.py:169
  13.3 3.0 %collective-permute-start.4 = (bf16[8,64,128]{2,1,0:T(8,128)(2,1)S(1)}, bf16[8,64,128]{2,1,0:T(8,128)(2,1)S(1)}, u32[]{:S(2)}, u32[]{:S(2)}) collective-permute-start(bf16[8,64,128]{2,1,0:T(8,128)(2,1)S(1)} %join.2.refs_0_), channel_id=1, source_target_pairs={{0,24},{1,97},{2,26},{3,99},{4,28},{5,101},{6,30},{7,103},{8,16},{... | collective-permute-start | bytes 393224 | tf_op jit(solution)/shard_map/ppermute | solution.py:169
  16.3 1.4 %collective-permute-start.5 = (bf16[8,64,128]{2,1,0:T(8,128)(2,1)S(1)}, bf16[8,64,128]{2,1,0:T(8,128)(2,1)S(1)}, u32[]{:S(2)}, u32[]{:S(2)}) collective-permute-start(bf16[8,64,128]{2,1,0:T(8,128)(2,1)S(1)} %join.2.refs_0_), channel_id=1, source_target_pairs={{0,16},{1,65},{2,18},{3,67},{4,20},{5,69},{6,22},{7,71},{8,24},{9,... | collective-permute-start | bytes 393224 | tf_op jit(solution)/shard_map/ppermute | solution.py:169
  17.8 2.5 %collective-permute-start.12 = (bf16[4,64,256]{2,1,0:T(8,128)(2,1)S(1)}, bf16[4,64,256]{2,1,0:T(8,128)(2,1)S(1)}, u32[]{:S(2)}, u32[]{:S(2)}) collective-permute-start(bf16[4,64,256]{2,1,0:T(8,128)(2,1)S(1)} %get-tuple-element.71), channel_id=1, source_target_pairs={{0,4},{1,5},{2,6},{3,7},{4,0},{5,1},{6,2},{7,3},{8,12},{9,13},{10,... | collective-permute-start | bytes 393224 | tf_op jit(solution)/shard_map/ppermute | solution.py:192
  20.3 0.7 collective-permute-start.13
  21.0 1.7 %collective-permute-done.5.refs_3_ = bf16[8,64,128]{2,1,0:T(8,128)(2,1)S(1)} collective-permute-done((bf16[8,64,128]{2,1,0:T(8,128)(2,1)S(1)}, bf16[8,64,128]{2,1,0:T(8,128)(2,1)S(1)}, u32[]{:S(2)}, u32[]{:S(2)}) %collective-permute-start.5) | collective-permute-done | bytes 131104 | tf_op jit(solution)/shard_map/ppermute | solution.py:169
  22.8 0.0 copy-start.1
  22.8 0.0 copy-start.2
  22.8 2.1 %collective-permute-start.6 = (bf16[32,64,128]{2,1,0:T(8,128)(2,1)S(1)}, bf16[32,64,128]{2,1,0:T(8,128)(2,1)S(1)}, u32[]{:S(2)}, u32[]{:S(2)}) collective-permute-start(bf16[32,64,128]{2,1,0:T(8,128)(2,1)S(1)} %join.3.rest_0_), channel_id=1, source_target_pairs={{0,32},{1,3},{2,34},{3,1},{4,36},{5,7},{6,38},{7,5},{8,40},{9,11},... | collective-permute-start | bytes 1572872 | tf_op jit(solution)/shard_map/ppermute | solution.py:169
  25.0 1.7 %collective-permute-start.7 = (bf16[32,64,128]{2,1,0:T(8,128)(2,1)S(1)}, bf16[32,64,128]{2,1,0:T(8,128)(2,1)}, u32[]{:S(2)}, u32[]{:S(2)}) collective-permute-start(bf16[32,64,128]{2,1,0:T(8,128)(2,1)S(1)} %join.3.rest_0_), channel_id=1, source_target_pairs={{0,96},{1,7},{2,98},{3,5},{4,100},{5,3},{6,102},{7,1},{8,104},{9,1... | collective-permute-start | bytes 1572872 | tf_op jit(solution)/shard_map/ppermute | solution.py:169
  26.6 0.9 pad_maximum_fusion.rest_0_
  27.5 5.4 %collective-permute-start.15 = (bf16[16,64,256]{2,1,0:T(8,128)(2,1)}, bf16[16,64,256]{2,1,0:T(8,128)(2,1)}, u32[]{:S(2)}, u32[]{:S(2)}) collective-permute-start(bf16[16,64,256]{2,1,0:T(8,128)(2,1)} %pad_maximum_fusion.rest_0_), channel_id=1, source_target_pairs={{0,0},{1,8},{2,2},{3,10},{4,4},{5,12},{6,6},{7,14},{8,1},{9,64},{1... | collective-permute-start | bytes 1572872 | tf_op jit(solution)/shard_map/ppermute | solution.py:192
  32.9 0.1 pad_add_fusion.nodes
  33.0 0.1 and_add_fusion
  33.0 0.1 reshape.16.halves
  33.1 0.1 reshape.17.tiles
  33.2 0.1 reshape.18.slots
  33.3 4.2 %copy.15.upper_transfer = bf16[126,64,64]{2,1,0:T(8,128)(2,1)S(1)} copy(bf16[126,64,64]{0,2,1:T(8,128)(2,1)} %param.23) | data formatting | bytes 2064384 | tf_op jit(solution)/shard_map/optimization_barrier | solution.py:506
  37.5 0.1 collective-permute-start.16
  37.6 0.8 select_transfers.1.transfers.rest_3_
  38.4 0.0 copy-start.4
  38.5 1.1 %part.2 = bf16[16,64,128]{2,1,0:T(8,128)(2,1)S(1)} custom-call(bf16[32,64,128]{2,1,0:T(8,128)(2,1)} %collective-permute-done.7.whole.rest_2_), custom_call_target="tpu_custom_call" | custom-call | tf_op jit(solution)/shard_map/part/pallas_call | solution.py:157
  39.6 4.6 %collective-permute-start.8 = (bf16[16,64,128]{2,1,0:T(8,128)(2,1)S(1)}, bf16[16,64,128]{2,1,0:T(8,128)(2,1)S(1)}, u32[]{:S(2)}, u32[]{:S(2)}) collective-permute-start(bf16[16,64,128]{2,1,0:T(8,128)(2,1)S(1)} %part.2), channel_id=1, source_target_pairs={{0,32},{1,3},{2,34},{3,1},{4,36},{5,7},{6,38},{7,5},{8,40},{9,11},... | collective-permute-start | bytes 786440 | tf_op jit(solution)/shard_map/ppermute | solution.py:169
  44.3 0.1 collective-permute-start.9
  44.4 1.8 %collective-permute-start.17 = (bf16[32,64,128]{2,1,0:T(8,128)(2,1)S(1)}, bf16[32,64,128]{2,1,0:T(8,128)(2,1)S(1)}, u32[]{:S(2)}, u32[]{:S(2)}) collective-permute-start(bf16[32,64,128]{2,1,0:T(8,128)(2,1)S(1)} %collective-permute-done.6.whole.rest_1_), channel_id=1, source_target_pairs={{0,1},{1,0},{2,3},{3,2},{4,5},{5,4},{6,7},{7,6},{8,9},{9,8},{10,11... | collective-permute-start | bytes 1572872 | tf_op jit(solution)/shard_map/ppermute | solution.py:202
  46.2 0.1 collective-permute-start.18
  46.3 6.5 %near_grams.1.near_gram = f32[4,64,64]{2,1,0:T(8,128)S(1)} custom-call(s32[32]{0:T(128)S(1)} %reshape.18.slots, bf16[4,8,256,256]{3,2,1,0:T(8,128)(2,1)} %blocks.1, bf16[4,64,256]{2,1,0:T(8,128)(2,1)S(1)} %copy-done.1, bf16[4,64,256]{2,1,0:T(8,128)(2,1)S(1)} %copy-done.2, bf16[16,64,256]{2,1,0:T(8,128)(2,1)} %pad_maximum_fusion.rest_0_, ...), custom_call_target="tpu_custom_call" | custom-call | tf_op jit(solution)/shard_map/near_grams/pallas_call | solution.py:288
  52.8 0.5 collective-permute-start.19
  53.3 0.1 collective-permute-start.20
  53.4 1.1 %collective-permute-done.19.rest_8_ = bf16[16,64,128]{2,1,0:T(8,128)(2,1)S(1)} collective-permute-done((bf16[16,64,128]{2,1,0:T(8,128)(2,1)S(1)}, bf16[16,64,128]{2,1,0:T(8,128)(2,1)S(1)}, u32[]{:S(2)}, u32[]{:S(2)}) %collective-permute-start.19) | collective-permute-done | bytes 262176 | tf_op jit(solution)/shard_map/ppermute | solution.py:202
  54.4 0.4 collective-permute-done.20.rest_9_
  54.8 5.2 %leaf_levels.1 = (f32[4,64,64]{2,1,0:T(8,128)S(1)}, f32[3,64,64]{2,1,0:T(8,128)S(1)}, f32[64,64]{1,0:T(8,128)S(1)}) custom-call(s32[128]{0:T(128)S(1)} %reshape.17.tiles, s32[128]{0:T(128)S(1)} %reshape.16.halves, bf16[4,64,2048]{2,1,0:T(8,128)(2,1)S(1)} %copy-done, f32[4,64,64]{2,1,0:T(8,128)S(1)} %near_grams.1.near_gram, bf16[4,64,64]{2,1,0:T(8,128)(2,1)S(1)} %copy-done.3, ...), custom_call_target="tpu_custom_call" | custom-call | tf_op jit(solution)/shard_map/leaf_levels/pallas_call | solution.py:385
  60.0 0.4 collective-permute-start.21
  60.4 0.9 collective-permute-done.21.other
  61.2 0.3 merge_pair.1
  61.5 1.6 %collective-permute-start.22 = (f32[64,64]{1,0:T(8,128)S(1)}, f32[64,64]{1,0:T(8,128)S(1)}, u32[]{:S(2)}, u32[]{:S(2)}) collective-permute-start(f32[64,64]{1,0:T(8,128)S(1)} %get-tuple-element.51.own), channel_id=1, source_target_pairs={{0,4},{1,5},{2,6},{3,7},{4,0},{5,1},{6,2},{7,3},{8,12},{9,13},{10,... | collective-permute-start | bytes 49160 | tf_op jit(solution)/shard_map/ppermute | solution.py:532
  63.1 1.4 %collective-permute-start.23 = (f32[64,64]{1,0:T(8,128)S(1)}, f32[64,64]{1,0:T(8,128)S(1)}, u32[]{:S(2)}, u32[]{:S(2)}) collective-permute-start(f32[64,64]{1,0:T(8,128)S(1)} %get-tuple-element.51.own), channel_id=1, source_target_pairs={{0,2},{1,3},{2,0},{3,1},{4,6},{5,7},{6,4},{7,5},{8,10},{9,11},{10,... | collective-permute-start | bytes 49160 | tf_op jit(solution)/shard_map/ppermute | solution.py:532
  64.5 1.4 %collective-permute-start.24 = (f32[64,64]{1,0:T(8,128)S(1)}, f32[64,64]{1,0:T(8,128)S(1)}, u32[]{:S(2)}, u32[]{:S(2)}) collective-permute-start(f32[64,64]{1,0:T(8,128)S(1)} %get-tuple-element.51.own), channel_id=1, source_target_pairs={{0,6},{1,7},{2,4},{3,5},{4,2},{5,3},{6,0},{7,1},{8,14},{9,15},{10,... | collective-permute-start | bytes 49160 | tf_op jit(solution)/shard_map/ppermute | solution.py:532
  65.8 3.7 %factor.3 = f32[4,64,64]{2,1,0:T(8,128)} custom-call(f32[4,64,64]{2,1,0:T(8,128)S(1)} %get-tuple-element.52.refs_0_), custom_call_target="tpu_custom_call" | custom-call | tf_op jit(solution)/shard_map/factor/pallas_call | solution.py:110
  69.5 0.1 collective-permute-done.24.rest_2_
  69.6 0.6 merge_quad.2
  70.2 2.7 %collective-permute-start.25 = (f32[64,64]{1,0:T(8,128)S(1)}, f32[64,64]{1,0:T(8,128)S(1)}, u32[]{:S(2)}, u32[]{:S(2)}) collective-permute-start(f32[64,64]{1,0:T(8,128)S(1)} %get-tuple-element.55.own), channel_id=1, source_target_pairs={{0,16},{1,17},{2,18},{3,19},{4,20},{5,21},{6,22},{7,23},{8,24},{9,... | collective-permute-start | bytes 49160 | tf_op jit(solution)/shard_map/ppermute | solution.py:532
  72.9 2.0 %collective-permute-start.26 = (f32[64,64]{1,0:T(8,128)S(1)}, f32[64,64]{1,0:T(8,128)S(1)}, u32[]{:S(2)}, u32[]{:S(2)}) collective-permute-start(f32[64,64]{1,0:T(8,128)S(1)} %get-tuple-element.55.own), channel_id=1, source_target_pairs={{0,8},{1,9},{2,10},{3,11},{4,12},{5,13},{6,14},{7,15},{8,0},{9,1},... | collective-permute-start | bytes 49160 | tf_op jit(solution)/shard_map/ppermute | solution.py:532
  74.9 0.6 collective-permute-start.27
  75.5 3.2 %factor.4 = f32[3,64,64]{2,1,0:T(8,128)} custom-call(f32[3,64,64]{2,1,0:T(8,128)S(1)} %get-tuple-element.56.refs_0_), custom_call_target="tpu_custom_call" | custom-call | tf_op jit(solution)/shard_map/factor/pallas_call | solution.py:110
  78.7 1.3 %collective-permute-done.27.rest_2_ = f32[64,64]{1,0:T(8,128)S(1)} collective-permute-done((f32[64,64]{1,0:T(8,128)S(1)}, f32[64,64]{1,0:T(8,128)S(1)}, u32[]{:S(2)}, u32[]{:S(2)}) %collective-permute-start.27) | collective-permute-done | bytes 16416 | tf_op jit(solution)/shard_map/ppermute | solution.py:532
  80.0 0.6 merge_quad.3
  80.6 2.7 %collective-permute-start.29 = (f32[64,64]{1,0:T(8,128)S(1)}, f32[64,64]{1,0:T(8,128)S(1)}, u32[]{:S(2)}, u32[]{:S(2)}) collective-permute-start(f32[64,64]{1,0:T(8,128)S(1)} %get-tuple-element.59.own), channel_id=1, source_target_pairs={{0,64},{1,65},{2,66},{3,67},{4,68},{5,69},{6,70},{7,71},{8,72},{9,... | collective-permute-start | bytes 49160 | tf_op jit(solution)/shard_map/ppermute | solution.py:532
  83.3 1.3 %collective-permute-start.28 = (f32[64,64]{1,0:T(8,128)S(1)}, f32[64,64]{1,0:T(8,128)S(1)}, u32[]{:S(2)}, u32[]{:S(2)}) collective-permute-start(f32[64,64]{1,0:T(8,128)S(1)} %get-tuple-element.59.own), channel_id=1, source_target_pairs={{0,32},{1,33},{2,34},{3,35},{4,36},{5,37},{6,38},{7,39},{8,40},{9,... | collective-permute-start | bytes 49160 | tf_op jit(solution)/shard_map/ppermute | solution.py:532
  84.6 0.7 collective-permute-start.30
  85.3 3.6 %factor.5.rest_4_ = f32[5,64,64]{2,1,0:T(8,128)S(1)} custom-call(f32[64,64]{1,0:T(8,128)S(1)} %get-tuple-element.60.refs_0_, f32[64,64]{1,0:T(8,128)S(1)} %get-tuple-element.61.refs_1_, f32[64,64]{1,0:T(8,128)S(1)} %get-tuple-element.62.refs_2_, f32[64,64]{1,0:T(8,128)S(1)} %get-tuple-element.63.refs_3_, f32[64,64]{1,0:T(8,128)S(1)} %get-tuple-element.64.refs_4_), custom_call_target="tpu_custom_call" | custom-call | tf_op jit(solution)/shard_map/factor/pallas_call | solution.py:110
  88.9 0.8 collective-permute-done.30.rest_2_
  89.8 3.2 %factor_root.1 = f32[7,64,64]{2,1,0:T(8,128)} custom-call(f32[64,64]{1,0:T(8,128)S(1)} %get-tuple-element.59.own, f32[64,64]{1,0:T(8,128)S(1)} %collective-permute-done.28.rest_0_, f32[64,64]{1,0:T(8,128)S(1)} %collective-permute-done.29.rest_1_, f32[64,64]{1,0:T(8,128)S(1)} %collective-permute-done.30.rest_2_, ...), custom_call_target="tpu_custom_call" | custom-call | tf_op jit(solution)/shard_map/factor_root/pallas_call | solution.py:465
  (50 shorter events, 0.3 us)
Async XLA Ops:
  0.6 32.6 %copy-start.5 = (s32[4,8]{1,0:T(4,128)S(1)}, s32[4,8]{1,0:T(4,128)}, u32[]{:S(2)}) copy-start(s32[4,8]{1,0:T(4,128)} %param.13) | copy-start | bytes 388
  0.6 32.3 %copy-start.6 = (s32[4,32]{1,0:T(4,128)S(1)}, s32[4,32]{1,0:T(4,128)}, u32[]{:S(2)}) copy-start(s32[4,32]{1,0:T(4,128)} %param.19) | copy-start | bytes 1540
  0.7 32.3 %copy-start.7 = (s32[4]{0:T(128)S(1)}, s32[4]{0:T(128)}, u32[]{:S(2)}) copy-start(s32[4]{0:T(128)} %param.20) | copy-start | bytes 52
  1.5 8.1 %collective-permute-start = (bf16[2,64,128]{2,1,0:T(8,128)(2,1)S(1)}, bf16[2,64,128]{2,1,0:T(8,128)(2,1)S(1)}, u32[]{:S(2)}, u32[]{:S(2)}) collective-permute-start(bf16[2,64,128]{2,1,0:T(8,128)(2,1)S(1)} %pad_maximum_fusion.2.refs_0_), channel_id=1, source_target_pairs={{0,2},{1,9},{2,0},{3,11},{4,6},{5,13},{6,4},{7,15},{8,10},{9,1},{1... | collective-permute-start | bytes 98312 | tf_op jit(solution)/shard_map/ppermute | solution.py:169
  3.7 6.0 %collective-permute-start.1 = (bf16[2,64,128]{2,1,0:T(8,128)(2,1)S(1)}, bf16[2,64,128]{2,1,0:T(8,128)(2,1)S(1)}, u32[]{:S(2)}, u32[]{:S(2)}) collective-permute-start(bf16[2,64,128]{2,1,0:T(8,128)(2,1)S(1)} %pad_maximum_fusion.2.refs_0_), channel_id=1, source_target_pairs={{0,6},{1,25},{2,4},{3,27},{4,2},{5,29},{6,0},{7,31},{8,14},{9,17},... | collective-permute-start | bytes 98312 | tf_op jit(solution)/shard_map/ppermute | solution.py:169
  6.2 5.4 %collective-permute-start.2 = (bf16[2,64,128]{2,1,0:T(8,128)(2,1)S(1)}, bf16[2,64,128]{2,1,0:T(8,128)(2,1)S(1)}, u32[]{:S(2)}, u32[]{:S(2)}) collective-permute-start(bf16[2,64,128]{2,1,0:T(8,128)(2,1)S(1)} %pad_maximum_fusion.2.refs_0_), channel_id=1, source_target_pairs={{0,4},{1,17},{2,6},{3,19},{4,0},{5,21},{6,2},{7,23},{8,12},{9,25},... | collective-permute-start | bytes 98312 | tf_op jit(solution)/shard_map/ppermute | solution.py:169
  8.1 9.5 %collective-permute-start.10 = (bf16[2,64,256]{2,1,0:T(8,128)(2,1)S(1)}, bf16[2,64,256]{2,1,0:T(8,128)(2,1)S(1)}, u32[]{:S(2)}, u32[]{:S(2)}) collective-permute-start(bf16[2,64,256]{2,1,0:T(8,128)(2,1)S(1)} %get-tuple-element.78), channel_id=1, source_target_pairs={{0,2},{1,3},{2,0},{3,1},{4,6},{5,7},{6,4},{7,5},{8,10},{9,11},{10,... | collective-permute-start | bytes 196616 | tf_op jit(solution)/shard_map/ppermute | solution.py:192
  8.7 9.0 %collective-permute-start.11 = (bf16[2,64,256]{2,1,0:T(8,128)(2,1)S(1)}, bf16[2,64,256]{2,1,0:T(8,128)(2,1)S(1)}, u32[]{:S(2)}, u32[]{:S(2)}) collective-permute-start(bf16[2,64,256]{2,1,0:T(8,128)(2,1)S(1)} %get-tuple-element.76), channel_id=1, source_target_pairs={{0,0},{1,1},{2,16},{3,17},{4,4},{5,5},{6,20},{7,21},{8,8},{9,9},{1... | collective-permute-start | bytes 196616 | tf_op jit(solution)/shard_map/ppermute | solution.py:192
  11.6 9.4 %collective-permute-start.3 = (bf16[8,64,128]{2,1,0:T(8,128)(2,1)S(1)}, bf16[8,64,128]{2,1,0:T(8,128)(2,1)S(1)}, u32[]{:S(2)}, u32[]{:S(2)}) collective-permute-start(bf16[8,64,128]{2,1,0:T(8,128)(2,1)S(1)} %join.2.refs_0_), channel_id=1, source_target_pairs={{0,8},{1,33},{2,10},{3,35},{4,12},{5,37},{6,14},{7,39},{8,0},{9,41... | collective-permute-start | bytes 393224 | tf_op jit(solution)/shard_map/ppermute | solution.py:169
  13.3 7.8 %collective-permute-start.4 = (bf16[8,64,128]{2,1,0:T(8,128)(2,1)S(1)}, bf16[8,64,128]{2,1,0:T(8,128)(2,1)S(1)}, u32[]{:S(2)}, u32[]{:S(2)}) collective-permute-start(bf16[8,64,128]{2,1,0:T(8,128)(2,1)S(1)} %join.2.refs_0_), channel_id=1, source_target_pairs={{0,24},{1,97},{2,26},{3,99},{4,28},{5,101},{6,30},{7,103},{8,16},{... | collective-permute-start | bytes 393224 | tf_op jit(solution)/shard_map/ppermute | solution.py:169
  16.3 6.5 %collective-permute-start.5 = (bf16[8,64,128]{2,1,0:T(8,128)(2,1)S(1)}, bf16[8,64,128]{2,1,0:T(8,128)(2,1)S(1)}, u32[]{:S(2)}, u32[]{:S(2)}) collective-permute-start(bf16[8,64,128]{2,1,0:T(8,128)(2,1)S(1)} %join.2.refs_0_), channel_id=1, source_target_pairs={{0,16},{1,65},{2,18},{3,67},{4,20},{5,69},{6,22},{7,71},{8,24},{9,... | collective-permute-start | bytes 393224 | tf_op jit(solution)/shard_map/ppermute | solution.py:169
  17.8 8.8 %collective-permute-start.12 = (bf16[4,64,256]{2,1,0:T(8,128)(2,1)S(1)}, bf16[4,64,256]{2,1,0:T(8,128)(2,1)S(1)}, u32[]{:S(2)}, u32[]{:S(2)}) collective-permute-start(bf16[4,64,256]{2,1,0:T(8,128)(2,1)S(1)} %get-tuple-element.71), channel_id=1, source_target_pairs={{0,4},{1,5},{2,6},{3,7},{4,0},{5,1},{6,2},{7,3},{8,12},{9,13},{10,... | collective-permute-start | bytes 393224 | tf_op jit(solution)/shard_map/ppermute | solution.py:192
  20.3 6.3 %collective-permute-start.13 = (bf16[4,64,256]{2,1,0:T(8,128)(2,1)S(1)}, bf16[4,64,256]{2,1,0:T(8,128)(2,1)S(1)}, u32[]{:S(2)}, u32[]{:S(2)}) collective-permute-start(bf16[4,64,256]{2,1,0:T(8,128)(2,1)S(1)} %get-tuple-element.72), channel_id=1, source_target_pairs={{0,0},{1,1},{2,2},{3,3},{4,32},{5,33},{6,34},{7,35},{8,8},{9,9},{1... | collective-permute-start | bytes 393224 | tf_op jit(solution)/shard_map/ppermute | solution.py:192
  22.8 23.4 %copy-start.1 = (bf16[4,64,256]{2,1,0:T(8,128)(2,1)S(1)}, bf16[4,64,256]{2,1,0:T(8,128)(2,1)}, u32[]{:S(2)}) copy-start(bf16[4,64,256]{2,1,0:T(8,128)(2,1)} %samples.1) | copy-start | bytes 393220
  22.8 23.4 %copy-start.2 = (bf16[4,64,256]{2,1,0:T(8,128)(2,1)S(1)}, bf16[4,64,256]{2,1,0:T(8,128)(2,1)}, u32[]{:S(2)}) copy-start(bf16[4,64,256]{2,1,0:T(8,128)(2,1)} %basis.1) | copy-start | bytes 393220
  22.8 15.6 %collective-permute-start.6 = (bf16[32,64,128]{2,1,0:T(8,128)(2,1)S(1)}, bf16[32,64,128]{2,1,0:T(8,128)(2,1)S(1)}, u32[]{:S(2)}, u32[]{:S(2)}) collective-permute-start(bf16[32,64,128]{2,1,0:T(8,128)(2,1)S(1)} %join.3.rest_0_), channel_id=1, source_target_pairs={{0,32},{1,3},{2,34},{3,1},{4,36},{5,7},{6,38},{7,5},{8,40},{9,11},... | collective-permute-start | bytes 1572872 | tf_op jit(solution)/shard_map/ppermute | solution.py:169
  25.0 13.5 %collective-permute-start.7 = (bf16[32,64,128]{2,1,0:T(8,128)(2,1)S(1)}, bf16[32,64,128]{2,1,0:T(8,128)(2,1)}, u32[]{:S(2)}, u32[]{:S(2)}) collective-permute-start(bf16[32,64,128]{2,1,0:T(8,128)(2,1)S(1)} %join.3.rest_0_), channel_id=1, source_target_pairs={{0,96},{1,7},{2,98},{3,5},{4,100},{5,3},{6,102},{7,1},{8,104},{9,1... | collective-permute-start | bytes 1572872 | tf_op jit(solution)/shard_map/ppermute | solution.py:169
  27.5 16.8 %collective-permute-start.14 = (bf16[16,64,256]{2,1,0:T(8,128)(2,1)}, bf16[16,64,256]{2,1,0:T(8,128)(2,1)}, u32[]{:S(2)}, u32[]{:S(2)}) collective-permute-start(bf16[16,64,256]{2,1,0:T(8,128)(2,1)} %pad_maximum_fusion.rest_0_), channel_id=1, source_target_pairs={{0,1},{1,0},{2,3},{3,2},{4,5},{5,4},{6,7},{7,6},{8,9},{9,8},{10,11... | collective-permute-start | bytes 1572872 | tf_op jit(solution)/shard_map/ppermute | solution.py:202
  27.5 18.6 %collective-permute-start.15 = (bf16[16,64,256]{2,1,0:T(8,128)(2,1)}, bf16[16,64,256]{2,1,0:T(8,128)(2,1)}, u32[]{:S(2)}, u32[]{:S(2)}) collective-permute-start(bf16[16,64,256]{2,1,0:T(8,128)(2,1)} %pad_maximum_fusion.rest_0_), channel_id=1, source_target_pairs={{0,0},{1,8},{2,2},{3,10},{4,4},{5,12},{6,6},{7,14},{8,1},{9,64},{1... | collective-permute-start | bytes 1572872 | tf_op jit(solution)/shard_map/ppermute | solution.py:192
  37.5 15.9 %collective-permute-start.16 = (bf16[32,64,128]{2,1,0:T(8,128)(2,1)S(1)}, bf16[32,64,128]{2,1,0:T(8,128)(2,1)S(1)}, u32[]{:S(2)}, u32[]{:S(2)}) collective-permute-start(bf16[32,64,128]{2,1,0:T(8,128)(2,1)S(1)} %join.3.rest_0_), channel_id=1, source_target_pairs={{0,1},{1,0},{2,3},{3,2},{4,5},{5,4},{6,7},{7,6},{8,9},{9,8},{10,11... | collective-permute-start | bytes 1572872 | tf_op jit(solution)/shard_map/ppermute | solution.py:202
  38.4 16.4 %copy-start = (bf16[4,64,2048]{2,1,0:T(8,128)(2,1)S(1)}, bf16[4,64,2048]{2,1,0:T(8,128)(2,1)}, u32[]{:S(2)}) copy-start(bf16[4,64,2048]{2,1,0:T(8,128)(2,1)} %coupling.1) | copy-start | bytes 3145732
  38.4 16.4 %copy-start.3 = (bf16[4,64,64]{2,1,0:T(8,128)(2,1)S(1)}, bf16[4,64,64]{2,1,0:T(8,128)(2,1)}, u32[]{:S(2)}) copy-start(bf16[4,64,64]{2,1,0:T(8,128)(2,1)} %leaf_transfer.1) | copy-start | bytes 98308
  38.4 16.4 %copy-start.4 = (bf16[1,3,64,64]{3,2,1,0:T(8,128)(2,1)S(1)}, bf16[1,3,64,64]{3,2,1,0:T(8,128)(2,1)}, u32[]{:S(2)}) copy-start(bf16[1,3,64,64]{3,2,1,0:T(8,128)(2,1)} %inner_transfer.1) | copy-start | bytes 73732
  39.6 13.1 %collective-permute-start.8 = (bf16[16,64,128]{2,1,0:T(8,128)(2,1)S(1)}, bf16[16,64,128]{2,1,0:T(8,128)(2,1)S(1)}, u32[]{:S(2)}, u32[]{:S(2)}) collective-permute-start(bf16[16,64,128]{2,1,0:T(8,128)(2,1)S(1)} %part.2), channel_id=1, source_target_pairs={{0,32},{1,3},{2,34},{3,1},{4,36},{5,7},{6,38},{7,5},{8,40},{9,11},... | collective-permute-start | bytes 786440 | tf_op jit(solution)/shard_map/ppermute | solution.py:169
  44.3 8.5 %collective-permute-start.9 = (bf16[16,64,128]{2,1,0:T(8,128)(2,1)S(1)}, bf16[16,64,128]{2,1,0:T(8,128)(2,1)S(1)}, u32[]{:S(2)}, u32[]{:S(2)}) collective-permute-start(bf16[16,64,128]{2,1,0:T(8,128)(2,1)S(1)} %part.3), channel_id=1, source_target_pairs={{0,96},{1,7},{2,98},{3,5},{4,100},{5,3},{6,102},{7,1},{8,104},{9,1... | collective-permute-start | bytes 786440 | tf_op jit(solution)/shard_map/ppermute | solution.py:169
  44.4 9.0 %collective-permute-start.17 = (bf16[32,64,128]{2,1,0:T(8,128)(2,1)S(1)}, bf16[32,64,128]{2,1,0:T(8,128)(2,1)S(1)}, u32[]{:S(2)}, u32[]{:S(2)}) collective-permute-start(bf16[32,64,128]{2,1,0:T(8,128)(2,1)S(1)} %collective-permute-done.6.whole.rest_1_), channel_id=1, source_target_pairs={{0,1},{1,0},{2,3},{3,2},{4,5},{5,4},{6,7},{7,6},{8,9},{9,8},{10,11... | collective-permute-start | bytes 1572872 | tf_op jit(solution)/shard_map/ppermute | solution.py:202
  46.2 7.2 %collective-permute-start.18 = (bf16[32,64,128]{2,1,0:T(8,128)(2,1)}, bf16[32,64,128]{2,1,0:T(8,128)(2,1)S(1)}, u32[]{:S(2)}, u32[]{:S(2)}) collective-permute-start(bf16[32,64,128]{2,1,0:T(8,128)(2,1)} %collective-permute-done.7.whole.rest_2_), channel_id=1, source_target_pairs={{0,1},{1,0},{2,3},{3,2},{4,5},{5,4},{6,7},{7,6},{8,9},{9,8},{10,11... | collective-permute-start | bytes 1572872 | tf_op jit(solution)/shard_map/ppermute | solution.py:202
  52.8 1.7 %collective-permute-start.19 = (bf16[16,64,128]{2,1,0:T(8,128)(2,1)S(1)}, bf16[16,64,128]{2,1,0:T(8,128)(2,1)S(1)}, u32[]{:S(2)}, u32[]{:S(2)}) collective-permute-start(bf16[16,64,128]{2,1,0:T(8,128)(2,1)S(1)} %collective-permute-done.8.rest_3_), channel_id=1, source_target_pairs={{0,1},{1,0},{2,3},{3,2},{4,5},{5,4},{6,7},{7,6},{8,9},{9,8},{10,11... | collective-permute-start | bytes 786440 | tf_op jit(solution)/shard_map/ppermute | solution.py:202
  53.3 1.5 %collective-permute-start.20 = (bf16[16,64,128]{2,1,0:T(8,128)(2,1)S(1)}, bf16[16,64,128]{2,1,0:T(8,128)(2,1)S(1)}, u32[]{:S(2)}, u32[]{:S(2)}) collective-permute-start(bf16[16,64,128]{2,1,0:T(8,128)(2,1)S(1)} %collective-permute-done.9.rest_4_), channel_id=1, source_target_pairs={{0,1},{1,0},{2,3},{3,2},{4,5},{5,4},{6,7},{7,6},{8,9},{9,8},{10,11... | collective-permute-start | bytes 786440 | tf_op jit(solution)/shard_map/ppermute | solution.py:202
  60.0 1.3 %collective-permute-start.21 = (f32[64,64]{1,0:T(8,128)S(1)}, f32[64,64]{1,0:T(8,128)S(1)}, u32[]{:S(2)}, u32[]{:S(2)}) collective-permute-start(f32[64,64]{1,0:T(8,128)S(1)} %get-tuple-element.49.own), channel_id=1, source_target_pairs={{0,1},{1,0},{2,3},{3,2},{4,5},{5,4},{6,7},{7,6},{8,9},{9,8},{10,11... | collective-permute-start | bytes 49160 | tf_op jit(solution)/shard_map/ppermute | solution.py:532
  61.5 8.0 %collective-permute-start.22 = (f32[64,64]{1,0:T(8,128)S(1)}, f32[64,64]{1,0:T(8,128)S(1)}, u32[]{:S(2)}, u32[]{:S(2)}) collective-permute-start(f32[64,64]{1,0:T(8,128)S(1)} %get-tuple-element.51.own), channel_id=1, source_target_pairs={{0,4},{1,5},{2,6},{3,7},{4,0},{5,1},{6,2},{7,3},{8,12},{9,13},{10,... | collective-permute-start | bytes 49160 | tf_op jit(solution)/shard_map/ppermute | solution.py:532
  63.1 6.5 %collective-permute-start.23 = (f32[64,64]{1,0:T(8,128)S(1)}, f32[64,64]{1,0:T(8,128)S(1)}, u32[]{:S(2)}, u32[]{:S(2)}) collective-permute-start(f32[64,64]{1,0:T(8,128)S(1)} %get-tuple-element.51.own), channel_id=1, source_target_pairs={{0,2},{1,3},{2,0},{3,1},{4,6},{5,7},{6,4},{7,5},{8,10},{9,11},{10,... | collective-permute-start | bytes 49160 | tf_op jit(solution)/shard_map/ppermute | solution.py:532
  64.5 5.1 %collective-permute-start.24 = (f32[64,64]{1,0:T(8,128)S(1)}, f32[64,64]{1,0:T(8,128)S(1)}, u32[]{:S(2)}, u32[]{:S(2)}) collective-permute-start(f32[64,64]{1,0:T(8,128)S(1)} %get-tuple-element.51.own), channel_id=1, source_target_pairs={{0,6},{1,7},{2,4},{3,5},{4,2},{5,3},{6,0},{7,1},{8,14},{9,15},{10,... | collective-permute-start | bytes 49160 | tf_op jit(solution)/shard_map/ppermute | solution.py:532
  70.2 8.5 %collective-permute-start.25 = (f32[64,64]{1,0:T(8,128)S(1)}, f32[64,64]{1,0:T(8,128)S(1)}, u32[]{:S(2)}, u32[]{:S(2)}) collective-permute-start(f32[64,64]{1,0:T(8,128)S(1)} %get-tuple-element.55.own), channel_id=1, source_target_pairs={{0,16},{1,17},{2,18},{3,19},{4,20},{5,21},{6,22},{7,23},{8,24},{9,... | collective-permute-start | bytes 49160 | tf_op jit(solution)/shard_map/ppermute | solution.py:532
  72.9 5.8 %collective-permute-start.26 = (f32[64,64]{1,0:T(8,128)S(1)}, f32[64,64]{1,0:T(8,128)S(1)}, u32[]{:S(2)}, u32[]{:S(2)}) collective-permute-start(f32[64,64]{1,0:T(8,128)S(1)} %get-tuple-element.55.own), channel_id=1, source_target_pairs={{0,8},{1,9},{2,10},{3,11},{4,12},{5,13},{6,14},{7,15},{8,0},{9,1},... | collective-permute-start | bytes 49160 | tf_op jit(solution)/shard_map/ppermute | solution.py:532
  74.9 5.1 %collective-permute-start.27 = (f32[64,64]{1,0:T(8,128)S(1)}, f32[64,64]{1,0:T(8,128)S(1)}, u32[]{:S(2)}, u32[]{:S(2)}) collective-permute-start(f32[64,64]{1,0:T(8,128)S(1)} %get-tuple-element.55.own), channel_id=1, source_target_pairs={{0,24},{1,25},{2,26},{3,27},{4,28},{5,29},{6,30},{7,31},{8,16},{9,... | collective-permute-start | bytes 49160 | tf_op jit(solution)/shard_map/ppermute | solution.py:532
  80.6 8.3 %collective-permute-start.29 = (f32[64,64]{1,0:T(8,128)S(1)}, f32[64,64]{1,0:T(8,128)S(1)}, u32[]{:S(2)}, u32[]{:S(2)}) collective-permute-start(f32[64,64]{1,0:T(8,128)S(1)} %get-tuple-element.59.own), channel_id=1, source_target_pairs={{0,64},{1,65},{2,66},{3,67},{4,68},{5,69},{6,70},{7,71},{8,72},{9,... | collective-permute-start | bytes 49160 | tf_op jit(solution)/shard_map/ppermute | solution.py:532
  83.3 5.6 %collective-permute-start.28 = (f32[64,64]{1,0:T(8,128)S(1)}, f32[64,64]{1,0:T(8,128)S(1)}, u32[]{:S(2)}, u32[]{:S(2)}) collective-permute-start(f32[64,64]{1,0:T(8,128)S(1)} %get-tuple-element.59.own), channel_id=1, source_target_pairs={{0,32},{1,33},{2,34},{3,35},{4,36},{5,37},{6,38},{7,39},{8,40},{9,... | collective-permute-start | bytes 49160 | tf_op jit(solution)/shard_map/ppermute | solution.py:532
  84.6 5.1 %collective-permute-start.30 = (f32[64,64]{1,0:T(8,128)S(1)}, f32[64,64]{1,0:T(8,128)S(1)}, u32[]{:S(2)}, u32[]{:S(2)}) collective-permute-start(f32[64,64]{1,0:T(8,128)S(1)} %get-tuple-element.59.own), channel_id=1, source_target_pairs={{0,96},{1,97},{2,98},{3,99},{4,100},{5,101},{6,102},{7,103},{8,104... | collective-permute-start | bytes 49160 | tf_op jit(solution)/shard_map/ppermute | solution.py:532
